TPU v7x, 32 devices: a whole 2x2x4 slice. The times are simulated.
32 devices in a mesh: group: 2 (over y), expert: 16 (over z, x, core), token: 1.
Axes of the slice: x: 2, y: 2, z: 4, core: 2. Of those that a mesh axis runs over, the one named last changes fastest.
Arguments:
- tokens: bfloat16 [4096, 2048], P(('group', 'expert', 'token')), parts along dimension 0, may hold values from -6 to 6
- expert_ids: int32 [4096, 8], P(('group', 'expert', 'token')), parts along dimension 0, may hold values from 0 to 15, all different within a row; in each aligned block of 128 rows (0 to 127, 128 to 255, ...) at most 96 rows name the same one
- route_weights: float32 [4096, 8], P(('group', 'expert', 'token')), parts along dimension 0, may hold values from 0.05 to 1
- gate_up: bfloat16 [16, 2048, 768], P('expert', 'token'), may hold values from -0.125 to 0.125
- down_t: bfloat16 [16, 2048, 384], P('expert', 'token'), may hold values from -0.3125 to 0.3125
Outputs:
- moe_out: bfloat16 [4096, 2048], P(('group', 'expert', 'token')), parts along dimension 0
There are 2 independent parts, one for each index of `group`. A program takes and returns all parts, laid end to end along the dimension named above; an argument that names none is the same for every part. Nothing has to cross between parts.
Inputs may be any that keep to these rules, and one draw needn't show every extreme that they name: `expert_ids`: each row names 8 different experts. Within the rows of one device (aligned blocks of 128 rows) no expert is named by more than 96 rows, a bound that some block reaches.
All inputs are finite; a program needn't handle non-finite values.
Results may differ from a plain program's by a relative error of at most 0.0058.
Values may be sent and summed in bfloat16 or wider, within the bound.
No kernel may reach another device: no remote copies, remote signals or barrier semaphores. Data moves between devices by JAX's collectives and lax.ppermute only.
A program may use at most 128 MiB of HBM per device.

v0:
```python
import functools

import jax
import jax.numpy as jnp
from jax import lax
from jax.experimental import pallas as pl
from jax.experimental.pallas import tpu as pltpu
from jax.sharding import PartitionSpec as P


def expert_apply(arrived, full_gate_up, full_down):
    shape = arrived.shape
    width = full_down.shape[2]
    rows = arrived.reshape(-1, shape[-1])
    pre = jnp.dot(rows, full_gate_up[0], preferred_element_type=jnp.float32)
    hidden = (jax.nn.silu(pre[:, :width]) * pre[:, width:]).astype(jnp.bfloat16)
    outputs = lax.dot_general(
        hidden, full_down[0], (((1,), (1,)), ((), ())), preferred_element_type=jnp.float32
    )
    return outputs.astype(jnp.bfloat16).reshape(shape)


def exchange_rows(tokens, expert_ids, route_weights, gate_up, down_t):
    tok_rows, choices_each = expert_ids.shape
    features = tokens.shape[1]
    num_experts = lax.axis_size("expert")
    slot_count = min(
        tok_rows, (3 * tok_rows * choices_each + 2 * num_experts - 1) // (2 * num_experts)
    )
    full_gate_up, full_down = (
        lax.all_gather(gate_up, "token", axis=1, tiled=True),
        lax.all_gather(down_t, "token", axis=1, tiled=True),
    )
    flat_ids = expert_ids.reshape(-1)
    onehot = (flat_ids[:, None] == jnp.arange(num_experts, dtype=jnp.int32)[None, :]).astype(
        jnp.int32
    )
    running = jnp.cumsum(onehot, axis=0)
    ranks = jnp.sum(running * onehot, axis=1) - 1
    slots = flat_ids * slot_count + ranks
    repeated = jnp.repeat(tokens, choices_each, axis=0)
    outgoing = jnp.zeros((num_experts * slot_count, features), jnp.bfloat16).at[slots].set(repeated)
    outgoing = outgoing.reshape(num_experts, slot_count, features)
    arrived = lax.all_to_all(outgoing, "expert", split_axis=0, concat_axis=0, tiled=True)
    served = expert_apply(arrived, full_gate_up, full_down)
    returned = lax.all_to_all(served, "expert", split_axis=0, concat_axis=0, tiled=True)
    picked = returned.reshape(num_experts * slot_count, features)[slots]
    picked = picked.reshape(tok_rows, choices_each, features)
    total = jnp.zeros((tok_rows, features), jnp.float32)
    for which in range(choices_each):
        total = total + route_weights[:, which : which + 1] * picked[:, which].astype(jnp.float32)
    return total.astype(jnp.bfloat16)


def chip_cycle(mesh):
    devices = mesh.devices[0, :, 0]
    chips = {}
    for index, device in enumerate(devices):
        chips.setdefault(tuple(getattr(device, "coords", (index // 2,))), []).append(index)
    coords = sorted(chips)
    wide = [d for d in range(len(coords[0])) if len({c[d] for c in coords}) > 1]
    if len(wide) == 2:
        wide.sort(key=lambda d: len({c[d] for c in coords}))
        short, long = wide
        turn = {v: i for i, v in enumerate(sorted({c[short] for c in coords}))}
        coords.sort(key=lambda c: (turn[c[short]], c[long] if turn[c[short]] % 2 == 0 else -c[long]))
    return [chips[c] for c in coords]


LANES = 128


def pack_rows(num_experts, tokens, ids_far, weights_far, out_a, out_b, ids, weights, done):
    outs = (out_a, out_b)
    tok_rows, features = tokens.shape
    half = features // 2
    pairs = [(ids_far, ids), (weights_far, weights)]
    for start in range(0, features, LANES):
        at = start % half // LANES * tok_rows
        pairs.append(
            (tokens.at[:, start : start + LANES], outs[start // half].at[at : at + tok_rows])
        )
    copies = [pltpu.make_async_copy(a, b, done.at[i]) for i, (a, b) in enumerate(pairs)]
    for copy in copies:
        copy.start()
    for copy in copies[:2]:
        copy.wait()
    place = lax.broadcasted_iota(jnp.int32, (num_experts, tok_rows), 0)
    share = jnp.zeros(place.shape, jnp.float32)
    for choice in range(ids.shape[0]):
        named = ids[choice : choice + 1] == place
        share += jnp.where(named, weights[choice : choice + 1], 0.0)
    high = share.astype(jnp.bfloat16).astype(jnp.float32)
    both = jnp.concatenate([high, share - high], axis=0)
    out_b[half // LANES * tok_rows :] = both.astype(jnp.bfloat16)
    for copy in copies[2:]:
        copy.wait()


def load(*refs):
    count = len(refs) // 2
    done = refs[-1]
    copies = [pltpu.make_async_copy(refs[i], refs[count + i], done.at[i]) for i in range(count)]
    for copy in copies:
        copy.start()
    for copy in copies:
        copy.wait()


def serve_rows(width, picks, partner, *refs):
    pieces, refs, out = refs[: -1 - 2 * len(picks)], refs[-1 - 2 * len(picks) : -1], refs[-1]
    tok_rows, _ = out.shape
    num_experts = len(partner)
    rows = [
        piece[at : at + tok_rows]
        for piece in pieces
        for at in range(0, piece.shape[0] - tok_rows + 1, tok_rows)
    ]
    rows = jnp.concatenate(rows, axis=1)
    shares = jnp.transpose(pieces[-1][-2 * num_experts :].astype(jnp.float32))
    lanes = lax.broadcasted_iota(jnp.int32, shares.shape, 1)
    me = lax.axis_index("expert")
    other = sum(jnp.where(me == e, partner[e], 0) for e in range(num_experts))
    total = None
    for place, which in enumerate(picks):
        gate, down = refs[2 * place], refs[2 * place + 1]
        expert = (me, other)[which]
        share = jnp.where((lanes == expert) | (lanes == expert + num_experts), shares, 0.0)
        share = jnp.sum(share, axis=1, keepdims=True)
        pre = jnp.dot(rows, gate[...], preferred_element_type=jnp.float32)
        gated, up = pre[:, :width], pre[:, width:]
        hidden = gated / (1.0 + jnp.exp(-gated)) * up
        part = lax.dot_general(
            hidden.astype(jnp.bfloat16),
            down[...],
            (((1,), (1,)), ((), ())),
            preferred_element_type=jnp.float32,
        )
        part = share * part.astype(jnp.bfloat16).astype(jnp.float32)
        total = part if total is None else total + part
    out[...] = total


def finish(at, home, got, *refs):
    out, rows, done = refs[-3:]
    count = got.shape[0]
    rows[...] = (home[at : at + count] + got[...].astype(jnp.float32)).astype(rows.dtype)
    copy = pltpu.make_async_copy(rows, out.at[at : at + count], done)
    copy.start()
    copy.wait()


def ring(stops, tokens, expert_ids, route_weights, gate_up, down_t):
    tok_rows, features = tokens.shape
    num_experts, width = lax.axis_size("expert"), down_t.shape[2]
    count = len(stops)
    partner = [0] * num_experts
    onward = [0] * num_experts
    for s in range(count):
        for place, turn in ((0, 1), (1, -1)):
            partner[stops[s][place]] = stops[s][1 - place]
            onward[stops[s][place]] = stops[(s + turn) % count][place]
    hop = functools.partial(lax.ppermute, axis_name="expert", perm=list(enumerate(onward)))
    swap = functools.partial(lax.ppermute, axis_name="expert", perm=list(enumerate(partner)))
    whole = pl.BlockSpec(memory_space=pltpu.VMEM)

    given = (tokens, expert_ids.T, route_weights.T)
    given = [pltpu.with_memory_space_constraint(x, pltpu.HBM) for x in given]
    half = features // 2 // LANES * tok_rows
    packed = pl.pallas_call(
        functools.partial(pack_rows, num_experts),
        out_shape=[
            jax.ShapeDtypeStruct((rows, LANES), jnp.bfloat16)
            for rows in (half, half + 2 * num_experts)
        ],
        in_specs=[pl.BlockSpec(memory_space=pltpu.HBM)] * 3,
        out_specs=[whole] * 2,
        scratch_shapes=[pltpu.VMEM(x.shape, x.dtype) for x in given[1:]]
        + [pltpu.SemaphoreType.DMA((2 + features // LANES,))],
        compiler_params=pltpu.CompilerParams(vmem_limit_bytes=8 * 1024 * 1024),
        name="pack_rows",
    )(*given)
    away = []
    for x in packed:
        away.append(hop(x))
    own = (gate_up[0], down_t[0])
    swapped = [swap(w) for w in own]
    held = pl.pallas_call(
        load,
        out_shape=[jax.ShapeDtypeStruct(w.shape, w.dtype) for w in own],
        in_specs=[pl.BlockSpec(memory_space=pltpu.HBM)] * 2,
        out_specs=[whole] * 2,
        scratch_shapes=[pltpu.SemaphoreType.DMA((2,))],
        compiler_params=pltpu.CompilerParams(vmem_limit_bytes=2 * 1024 * 1024),
        name="load",
    )(*(pltpu.with_memory_space_constraint(w, pltpu.HBM) for w in own))
    weights = (held, swapped)

    def serve(pieces, picks):
        return pl.pallas_call(
            functools.partial(serve_rows, width, picks, partner),
            out_shape=jax.ShapeDtypeStruct((tok_rows, features), jnp.float32),
            in_specs=[whole] * (len(pieces) + 2 * len(picks)),
            out_specs=whole,
            compiler_params=pltpu.CompilerParams(vmem_limit_bytes=8 * 1024 * 1024),
            name="serve_rows",
        )(*pieces, *(w for which in picks for w in weights[which]))

    def after(arrays, other):
        return [lax.optimization_barrier((x, other))[0] for x in arrays]

    away = after(away, held)
    total = None
    for step in range(1, count):
        here = list(away)
        if step < count - 1:
            away = away if step == 1 else [jnp.concatenate(away)]
            for at, x in enumerate(away):
                away[at] = hop(x)
        more = serve(here, (0, 1))
        away = after(away, more)
        parts = 2 if step >= count - 2 else 1
        more = jnp.split(more, parts)
        if total is not None:
            if len(total) < parts:
                total = jnp.split(total[0], parts)
        sent = []
        for at, x in enumerate(more):
            if total is not None:
                y = after([total[at]], sent)[0] if parts > 1 else total[at]
                x = x + y.astype(jnp.float32)
            sent.append(x.astype(jnp.bfloat16))
        total = []
        for x in sent:
            total.append(hop(x))
    home = serve(packed, (0, 1))
    far = pl.BlockSpec(memory_space=pltpu.HBM)
    out, rows = [], tok_rows // len(total)
    for at, got in enumerate(total):
        out = [
            pl.pallas_call(
                functools.partial(finish, at * rows),
                out_shape=jax.ShapeDtypeStruct(tokens.shape, tokens.dtype),
                in_specs=[whole] * 2 + [far] * len(out),
                out_specs=far,
                input_output_aliases={2: 0} if out else {},
                scratch_shapes=[
                    pltpu.VMEM((rows, features), tokens.dtype),
                    pltpu.SemaphoreType.DMA(()),
                ],
                compiler_params=pltpu.CompilerParams(vmem_limit_bytes=4 * 1024 * 1024),
                name="finish",
            )(home, got, *out)
        ]
    return out[0]


def solution(mesh):
    placed = (
        P(("group", "expert", "token"), None),
        P(("group", "expert", "token"), None),
        P(("group", "expert", "token"), None),
        P("expert", "token", None),
        P("expert", "token", None),
    )

    stops = chip_cycle(mesh)
    cycle = mesh.shape["token"] == 1 and {len(s) for s in stops} == {2} and len(stops) > 2

    def per_device(tokens, expert_ids, route_weights, gate_up, down_t):
        fits = cycle and mesh.shape["expert"] <= 4 * expert_ids.shape[1] and gate_up.shape[0] == 1
        if fits and tokens.shape[0] == LANES and tokens.shape[1] % (2 * LANES) == 0:
            return ring(stops, tokens, expert_ids, route_weights, gate_up, down_t)
        return exchange_rows(tokens, expert_ids, route_weights, gate_up, down_t)

    return jax.shard_map(
        per_device,
        mesh=mesh,
        in_specs=placed,
        out_specs=P(("group", "expert", "token"), None),
        check_vma=False,
    )
```

profile of v0, /device:TPU:0, one launch (start us, length us, event | category | flops | bytes accessed | tf_op | source)
XLA Modules:
  0.0 90.0 jit_solution(10000866815429017134)
XLA Ops:
  0.0 0.5 collective-permute-start
  0.5 1.2 %pack_rows.1 = (bf16[1024,128]{1,0:T(8,128)(2,1)S(1)}, bf16[1056,128]{1,0:T(8,128)(2,1)S(1)}) custom-call(bf16[128,2048]{1,0:T(8,128)(2,1)} %tokens.1, s32[8,128]{1,0:T(8,128)} %bitcast.8, f32[8,128]{1,0:T(8,128)} %bitcast.9), custom_call_target="tpu_custom_call" | custom-call | tf_op jit(solution)/shard_map/pack_rows/pallas_call | solution.py:170
  1.7 3.1 %collective-permute-start.4 = (bf16[1056,128]{1,0:T(8,128)(2,1)S(1)}, bf16[1056,128]{1,0:T(8,128)(2,1)S(1)}, u32[]{:S(2)}, u32[]{:S(2)}) collective-permute-start(bf16[1056,128]{1,0:T(8,128)(2,1)S(1)} %get-tuple-element.21.refs_1_), channel_id=1, source_target_pairs={{0,4},{1,3},{2,0},{3,7},{4,8},{5,1},{6,2},{7,11},{8,12},{9,5},{10,... | collective-permute-start | bytes 811016 | tf_op jit(solution)/shard_map/ppermute | solution.py:185
  4.8 1.6 %collective-permute-start.2 = (bf16[1024,128]{1,0:T(8,128)(2,1)S(1)}, bf16[1024,128]{1,0:T(8,128)(2,1)S(1)}, u32[]{:S(2)}, u32[]{:S(2)}) collective-permute-start(bf16[1024,128]{1,0:T(8,128)(2,1)S(1)} %get-tuple-element.20.refs_0_), channel_id=1, source_target_pairs={{0,4},{1,3},{2,0},{3,7},{4,8},{5,1},{6,2},{7,11},{8,12},{9,5},{10,... | collective-permute-start | bytes 786440 | tf_op jit(solution)/shard_map/ppermute | solution.py:185
  6.4 2.4 %load.1 = (bf16[2048,768]{1,0:T(8,128)(2,1)S(1)}, bf16[2048,384]{1,0:T(8,128)(2,1)S(1)}) custom-call(bf16[2048,768]{1,0:T(8,128)(2,1)} %bitcast.5, bf16[2048,384]{1,0:T(8,128)(2,1)} %bitcast.7), custom_call_target="tpu_custom_call" | custom-call | tf_op jit(solution)/shard_map/load/pallas_call | solution.py:188
  8.8 0.4 collective-permute-done.4.refs_1_
  9.2 2.1 %collective-permute-start.5 = (bf16[1056,128]{1,0:T(8,128)(2,1)S(1)}, bf16[1056,128]{1,0:T(8,128)(2,1)S(1)}, u32[]{:S(2)}, u32[]{:S(2)}) collective-permute-start(bf16[1056,128]{1,0:T(8,128)(2,1)S(1)} %collective-permute-done.4.refs_1_), channel_id=1, source_target_pairs={{0,4},{1,3},{2,0},{3,7},{4,8},{5,1},{6,2},{7,11},{8,12},{9,5},{10,... | collective-permute-start | bytes 811016 | tf_op jit(solution)/shard_map/ppermute | solution.py:219
  11.3 0.7 collective-permute-done.2.refs_0_
  12.0 2.1 %collective-permute-start.3 = (bf16[1024,128]{1,0:T(8,128)(2,1)S(1)}, bf16[1024,128]{1,0:T(8,128)(2,1)S(1)}, u32[]{:S(2)}, u32[]{:S(2)}) collective-permute-start(bf16[1024,128]{1,0:T(8,128)(2,1)S(1)} %collective-permute-done.2.refs_0_), channel_id=1, source_target_pairs={{0,4},{1,3},{2,0},{3,7},{4,8},{5,1},{6,2},{7,11},{8,12},{9,5},{10,... | collective-permute-start | bytes 786440 | tf_op jit(solution)/shard_map/ppermute | solution.py:219
  14.1 2.6 %serve_rows.9 = f32[128,2048]{1,0:T(8,128)S(1)} custom-call(bf16[1024,128]{1,0:T(8,128)(2,1)S(1)} %collective-permute-done.2.refs_0_, bf16[1056,128]{1,0:T(8,128)(2,1)S(1)} %collective-permute-done.4.refs_1_, bf16[2048,768]{1,0:T(8,128)(2,1)S(1)} %get-tuple-element.22.refs_2_.refs_1_, bf16[2048,384]{1,0:T(8,128)(2,1)S(1)} %get-tuple-element.23.refs_3_.refs_2_, ...), custom_call_target="tpu_custom_call" | custom-call | tf_op jit(solution)/shard_map/serve_rows/pallas_call | solution.py:200
  16.7 1.6 %collective-permute-start.11 = (bf16[128,2048]{1,0:T(8,128)(2,1)S(1)}, bf16[128,2048]{1,0:T(8,128)(2,1)S(1)}, u32[]{:S(2)}, u32[]{:S(2)}) collective-permute-start(bf16[128,2048]{1,0:T(8,128)(2,1)S(1)} %convert_element_type.51), channel_id=1, source_target_pairs={{0,4},{1,3},{2,0},{3,7},{4,8},{5,1},{6,2},{7,11},{8,12},{9,5},{10,... | collective-permute-start | bytes 1572872 | tf_op jit(solution)/shard_map/ppermute | solution.py:235
  18.5 2.2 %collective-permute-start.6 = (bf16[2080,128]{1,0:T(8,128)(2,1)S(1)}, bf16[2080,128]{1,0:T(8,128)(2,1)S(1)}, u32[]{:S(2)}, u32[]{:S(2)}) collective-permute-start(bf16[2080,128]{1,0:T(8,128)(2,1)S(1)} %pad_maximum_fusion), channel_id=1, source_target_pairs={{0,4},{1,3},{2,0},{3,7},{4,8},{5,1},{6,2},{7,11},{8,12},{9,5},{10,... | collective-permute-start | bytes 1597448 | tf_op jit(solution)/shard_map/ppermute | solution.py:219
  20.6 2.6 %serve_rows.10 = f32[128,2048]{1,0:T(8,128)S(1)} custom-call(bf16[1024,128]{1,0:T(8,128)(2,1)S(1)} %collective-permute-done.3.refs_0_, bf16[1056,128]{1,0:T(8,128)(2,1)S(1)} %collective-permute-done.5.refs_1_, bf16[2048,768]{1,0:T(8,128)(2,1)S(1)} %get-tuple-element.22.refs_2_.refs_1_, bf16[2048,384]{1,0:T(8,128)(2,1)S(1)} %get-tuple-element.23.refs_3_.refs_2_, ...), custom_call_target="tpu_custom_call" | custom-call | tf_op jit(solution)/shard_map/serve_rows/pallas_call | solution.py:200
  23.2 2.8 %collective-permute-done.11 = bf16[128,2048]{1,0:T(8,128)(2,1)S(1)} collective-permute-done((bf16[128,2048]{1,0:T(8,128)(2,1)S(1)}, bf16[128,2048]{1,0:T(8,128)(2,1)S(1)}, u32[]{:S(2)}, u32[]{:S(2)}) %collective-permute-start.11) | collective-permute-done | bytes 524320 | tf_op jit(solution)/shard_map/ppermute | solution.py:235
  26.0 0.1 add_convert_fusion.3
  26.1 1.6 %collective-permute-start.12 = (bf16[128,2048]{1,0:T(8,128)(2,1)S(1)}, bf16[128,2048]{1,0:T(8,128)(2,1)S(1)}, u32[]{:S(2)}, u32[]{:S(2)}) collective-permute-start(bf16[128,2048]{1,0:T(8,128)(2,1)S(1)} %add_convert_fusion.3), channel_id=1, source_target_pairs={{0,4},{1,3},{2,0},{3,7},{4,8},{5,1},{6,2},{7,11},{8,12},{9,5},{10,... | collective-permute-start | bytes 1572872 | tf_op jit(solution)/shard_map/ppermute | solution.py:235
  27.8 3.9 %collective-permute-done.6.refs_0_ = bf16[2080,128]{1,0:T(8,128)(2,1)S(1)} collective-permute-done((bf16[2080,128]{1,0:T(8,128)(2,1)S(1)}, bf16[2080,128]{1,0:T(8,128)(2,1)S(1)}, u32[]{:S(2)}, u32[]{:S(2)}) %collective-permute-start.6) | collective-permute-done | bytes 532512 | tf_op jit(solution)/shard_map/ppermute | solution.py:219
  31.7 1.6 %collective-permute-start.7 = (bf16[2080,128]{1,0:T(8,128)(2,1)S(1)}, bf16[2080,128]{1,0:T(8,128)(2,1)S(1)}, u32[]{:S(2)}, u32[]{:S(2)}) collective-permute-start(bf16[2080,128]{1,0:T(8,128)(2,1)S(1)} %collective-permute-done.6.refs_0_), channel_id=1, source_target_pairs={{0,4},{1,3},{2,0},{3,7},{4,8},{5,1},{6,2},{7,11},{8,12},{9,5},{10,... | collective-permute-start | bytes 1597448 | tf_op jit(solution)/shard_map/ppermute | solution.py:219
  33.3 2.5 %serve_rows.11 = f32[128,2048]{1,0:T(8,128)S(1)} custom-call(bf16[2080,128]{1,0:T(8,128)(2,1)S(1)} %collective-permute-done.6.refs_0_, bf16[2048,768]{1,0:T(8,128)(2,1)S(1)} %get-tuple-element.22.refs_2_.refs_1_, bf16[2048,384]{1,0:T(8,128)(2,1)S(1)} %get-tuple-element.23.refs_3_.refs_2_, bf16[2048,768]{1,0:T(8,128)(2,1)S(1)} %collective-permute-done.refs_4_.refs_3_, ...), custom_call_target="tpu_custom_call" | custom-call | tf_op jit(solution)/shard_map/serve_rows/pallas_call | solution.py:200
  35.8 1.5 %collective-permute-done.12 = bf16[128,2048]{1,0:T(8,128)(2,1)S(1)} collective-permute-done((bf16[128,2048]{1,0:T(8,128)(2,1)S(1)}, bf16[128,2048]{1,0:T(8,128)(2,1)S(1)}, u32[]{:S(2)}, u32[]{:S(2)}) %collective-permute-start.12) | collective-permute-done | bytes 524320 | tf_op jit(solution)/shard_map/ppermute | solution.py:235
  37.3 0.1 add_convert_fusion.2
  37.4 1.6 %collective-permute-start.13 = (bf16[128,2048]{1,0:T(8,128)(2,1)S(1)}, bf16[128,2048]{1,0:T(8,128)(2,1)S(1)}, u32[]{:S(2)}, u32[]{:S(2)}) collective-permute-start(bf16[128,2048]{1,0:T(8,128)(2,1)S(1)} %add_convert_fusion.2), channel_id=1, source_target_pairs={{0,4},{1,3},{2,0},{3,7},{4,8},{5,1},{6,2},{7,11},{8,12},{9,5},{10,... | collective-permute-start | bytes 1572872 | tf_op jit(solution)/shard_map/ppermute | solution.py:235
  39.0 4.0 %collective-permute-done.7.refs_0_ = bf16[2080,128]{1,0:T(8,128)(2,1)S(1)} collective-permute-done((bf16[2080,128]{1,0:T(8,128)(2,1)S(1)}, bf16[2080,128]{1,0:T(8,128)(2,1)S(1)}, u32[]{:S(2)}, u32[]{:S(2)}) %collective-permute-start.7) | collective-permute-done | bytes 532512 | tf_op jit(solution)/shard_map/ppermute | solution.py:219
  43.0 1.6 %collective-permute-start.8 = (bf16[2080,128]{1,0:T(8,128)(2,1)S(1)}, bf16[2080,128]{1,0:T(8,128)(2,1)S(1)}, u32[]{:S(2)}, u32[]{:S(2)}) collective-permute-start(bf16[2080,128]{1,0:T(8,128)(2,1)S(1)} %collective-permute-done.7.refs_0_), channel_id=1, source_target_pairs={{0,4},{1,3},{2,0},{3,7},{4,8},{5,1},{6,2},{7,11},{8,12},{9,5},{10,... | collective-permute-start | bytes 1597448 | tf_op jit(solution)/shard_map/ppermute | solution.py:219
  44.6 2.6 %serve_rows.12 = f32[128,2048]{1,0:T(8,128)S(1)} custom-call(bf16[2080,128]{1,0:T(8,128)(2,1)S(1)} %collective-permute-done.7.refs_0_, bf16[2048,768]{1,0:T(8,128)(2,1)S(1)} %get-tuple-element.22.refs_2_.refs_1_, bf16[2048,384]{1,0:T(8,128)(2,1)S(1)} %get-tuple-element.23.refs_3_.refs_2_, bf16[2048,768]{1,0:T(8,128)(2,1)S(1)} %collective-permute-done.refs_4_.refs_3_, ...), custom_call_target="tpu_custom_call" | custom-call | tf_op jit(solution)/shard_map/serve_rows/pallas_call | solution.py:200
  47.2 1.5 %collective-permute-done.13 = bf16[128,2048]{1,0:T(8,128)(2,1)S(1)} collective-permute-done((bf16[128,2048]{1,0:T(8,128)(2,1)S(1)}, bf16[128,2048]{1,0:T(8,128)(2,1)S(1)}, u32[]{:S(2)}, u32[]{:S(2)}) %collective-permute-start.13) | collective-permute-done | bytes 524320 | tf_op jit(solution)/shard_map/ppermute | solution.py:235
  48.7 1.6 %collective-permute-start.14 = (bf16[128,2048]{1,0:T(8,128)(2,1)S(1)}, bf16[128,2048]{1,0:T(8,128)(2,1)S(1)}, u32[]{:S(2)}, u32[]{:S(2)}) collective-permute-start(bf16[128,2048]{1,0:T(8,128)(2,1)S(1)} %add_convert_fusion.1), channel_id=1, source_target_pairs={{0,4},{1,3},{2,0},{3,7},{4,8},{5,1},{6,2},{7,11},{8,12},{9,5},{10,... | collective-permute-start | bytes 1572872 | tf_op jit(solution)/shard_map/ppermute | solution.py:235
  50.4 4.0 %collective-permute-done.8.refs_0_ = bf16[2080,128]{1,0:T(8,128)(2,1)S(1)} collective-permute-done((bf16[2080,128]{1,0:T(8,128)(2,1)S(1)}, bf16[2080,128]{1,0:T(8,128)(2,1)S(1)}, u32[]{:S(2)}, u32[]{:S(2)}) %collective-permute-start.8) | collective-permute-done | bytes 532512 | tf_op jit(solution)/shard_map/ppermute | solution.py:219
  54.3 1.6 %collective-permute-start.9 = (bf16[2080,128]{1,0:T(8,128)(2,1)S(1)}, bf16[2080,128]{1,0:T(8,128)(2,1)S(1)}, u32[]{:S(2)}, u32[]{:S(2)}) collective-permute-start(bf16[2080,128]{1,0:T(8,128)(2,1)S(1)} %collective-permute-done.8.refs_0_), channel_id=1, source_target_pairs={{0,4},{1,3},{2,0},{3,7},{4,8},{5,1},{6,2},{7,11},{8,12},{9,5},{10,... | collective-permute-start | bytes 1597448 | tf_op jit(solution)/shard_map/ppermute | solution.py:219
  55.9 2.5 %serve_rows.13 = f32[128,2048]{1,0:T(8,128)S(1)} custom-call(bf16[2080,128]{1,0:T(8,128)(2,1)S(1)} %collective-permute-done.8.refs_0_, bf16[2048,768]{1,0:T(8,128)(2,1)S(1)} %get-tuple-element.22.refs_2_.refs_1_, bf16[2048,384]{1,0:T(8,128)(2,1)S(1)} %get-tuple-element.23.refs_3_.refs_2_, bf16[2048,768]{1,0:T(8,128)(2,1)S(1)} %collective-permute-done.refs_4_.refs_3_, ...), custom_call_target="tpu_custom_call" | custom-call | tf_op jit(solution)/shard_map/serve_rows/pallas_call | solution.py:200
  58.4 1.5 %collective-permute-done.14 = bf16[128,2048]{1,0:T(8,128)(2,1)S(1)} collective-permute-done((bf16[128,2048]{1,0:T(8,128)(2,1)S(1)}, bf16[128,2048]{1,0:T(8,128)(2,1)S(1)}, u32[]{:S(2)}, u32[]{:S(2)}) %collective-permute-start.14) | collective-permute-done | bytes 524320 | tf_op jit(solution)/shard_map/ppermute | solution.py:235
  60.1 1.6 %collective-permute-start.15 = (bf16[128,2048]{1,0:T(8,128)(2,1)S(1)}, bf16[128,2048]{1,0:T(8,128)(2,1)S(1)}, u32[]{:S(2)}, u32[]{:S(2)}) collective-permute-start(bf16[128,2048]{1,0:T(8,128)(2,1)S(1)} %add_convert_fusion), channel_id=1, source_target_pairs={{0,4},{1,3},{2,0},{3,7},{4,8},{5,1},{6,2},{7,11},{8,12},{9,5},{10,... | collective-permute-start | bytes 1572872 | tf_op jit(solution)/shard_map/ppermute | solution.py:235
  61.7 4.0 %collective-permute-done.9.refs_0_ = bf16[2080,128]{1,0:T(8,128)(2,1)S(1)} collective-permute-done((bf16[2080,128]{1,0:T(8,128)(2,1)S(1)}, bf16[2080,128]{1,0:T(8,128)(2,1)S(1)}, u32[]{:S(2)}, u32[]{:S(2)}) %collective-permute-start.9) | collective-permute-done | bytes 532512 | tf_op jit(solution)/shard_map/ppermute | solution.py:219
  65.7 1.6 %collective-permute-start.10 = (bf16[2080,128]{1,0:T(8,128)(2,1)S(1)}, bf16[2080,128]{1,0:T(8,128)(2,1)S(1)}, u32[]{:S(2)}, u32[]{:S(2)}) collective-permute-start(bf16[2080,128]{1,0:T(8,128)(2,1)S(1)} %collective-permute-done.9.refs_0_), channel_id=1, source_target_pairs={{0,4},{1,3},{2,0},{3,7},{4,8},{5,1},{6,2},{7,11},{8,12},{9,5},{10,... | collective-permute-start | bytes 1597448 | tf_op jit(solution)/shard_map/ppermute | solution.py:219
  67.2 2.5 %serve_rows.14 = f32[128,2048]{1,0:T(8,128)S(1)} custom-call(bf16[2080,128]{1,0:T(8,128)(2,1)S(1)} %collective-permute-done.9.refs_0_, bf16[2048,768]{1,0:T(8,128)(2,1)S(1)} %get-tuple-element.22.refs_2_.refs_1_, bf16[2048,384]{1,0:T(8,128)(2,1)S(1)} %get-tuple-element.23.refs_3_.refs_2_, bf16[2048,768]{1,0:T(8,128)(2,1)S(1)} %collective-permute-done.refs_4_.refs_3_, ...), custom_call_target="tpu_custom_call" | custom-call | tf_op jit(solution)/shard_map/serve_rows/pallas_call | solution.py:200
  69.8 1.5 %collective-permute-done.15 = bf16[128,2048]{1,0:T(8,128)(2,1)S(1)} collective-permute-done((bf16[128,2048]{1,0:T(8,128)(2,1)S(1)}, bf16[128,2048]{1,0:T(8,128)(2,1)S(1)}, u32[]{:S(2)}, u32[]{:S(2)}) %collective-permute-start.15) | collective-permute-done | bytes 524320 | tf_op jit(solution)/shard_map/ppermute | solution.py:235
  71.4 1.6 %collective-permute-start.17 = (bf16[64,2048]{1,0:T(8,128)(2,1)S(1)}, bf16[64,2048]{1,0:T(8,128)(2,1)S(1)}, u32[]{:S(2)}, u32[]{:S(2)}) collective-permute-start(bf16[64,2048]{1,0:T(8,128)(2,1)S(1)} %fusion.1), channel_id=1, source_target_pairs={{0,4},{1,3},{2,0},{3,7},{4,8},{5,1},{6,2},{7,11},{8,12},{9,5},{10,... | collective-permute-start | bytes 786440 | tf_op jit(solution)/shard_map/ppermute | solution.py:235
  73.1 1.6 %collective-permute-start.16 = (bf16[64,2048]{1,0:T(8,128)(2,1)S(1)}, bf16[64,2048]{1,0:T(8,128)(2,1)S(1)}, u32[]{:S(2)}, u32[]{:S(2)}) collective-permute-start(bf16[64,2048]{1,0:T(8,128)(2,1)S(1)} %fusion.2), channel_id=1, source_target_pairs={{0,4},{1,3},{2,0},{3,7},{4,8},{5,1},{6,2},{7,11},{8,12},{9,5},{10,... | collective-permute-start | bytes 786440 | tf_op jit(solution)/shard_map/ppermute | solution.py:235
  74.7 2.3 %collective-permute-done.10.refs_0_ = bf16[2080,128]{1,0:T(8,128)(2,1)S(1)} collective-permute-done((bf16[2080,128]{1,0:T(8,128)(2,1)S(1)}, bf16[2080,128]{1,0:T(8,128)(2,1)S(1)}, u32[]{:S(2)}, u32[]{:S(2)}) %collective-permute-start.10) | collective-permute-done | bytes 532512 | tf_op jit(solution)/shard_map/ppermute | solution.py:219
  77.0 2.5 %serve_rows.15 = f32[128,2048]{1,0:T(8,128)S(1)} custom-call(bf16[2080,128]{1,0:T(8,128)(2,1)S(1)} %collective-permute-done.10.refs_0_, bf16[2048,768]{1,0:T(8,128)(2,1)S(1)} %get-tuple-element.22.refs_2_.refs_1_, bf16[2048,384]{1,0:T(8,128)(2,1)S(1)} %get-tuple-element.23.refs_3_.refs_2_, bf16[2048,768]{1,0:T(8,128)(2,1)S(1)} %collective-permute-done.refs_4_.refs_3_, ...), custom_call_target="tpu_custom_call" | custom-call | tf_op jit(solution)/shard_map/serve_rows/pallas_call | solution.py:200
  79.5 0.3 collective-permute-done.17
  79.8 1.6 %collective-permute-start.19 = (bf16[64,2048]{1,0:T(8,128)(2,1)S(1)}, bf16[64,2048]{1,0:T(8,128)(2,1)S(1)}, u32[]{:S(2)}, u32[]{:S(2)}) collective-permute-start(bf16[64,2048]{1,0:T(8,128)(2,1)S(1)} %fusion), channel_id=1, source_target_pairs={{0,4},{1,3},{2,0},{3,7},{4,8},{5,1},{6,2},{7,11},{8,12},{9,5},{10,... | collective-permute-start | bytes 786440 | tf_op jit(solution)/shard_map/ppermute | solution.py:235
  81.5 1.1 %collective-permute-done.16 = bf16[64,2048]{1,0:T(8,128)(2,1)S(1)} collective-permute-done((bf16[64,2048]{1,0:T(8,128)(2,1)S(1)}, bf16[64,2048]{1,0:T(8,128)(2,1)S(1)}, u32[]{:S(2)}, u32[]{:S(2)}) %collective-permute-start.16) | collective-permute-done | bytes 262176 | tf_op jit(solution)/shard_map/ppermute | solution.py:235
  82.7 1.6 %collective-permute-start.18 = (bf16[64,2048]{1,0:T(8,128)(2,1)S(1)}, bf16[64,2048]{1,0:T(8,128)(2,1)S(1)}, u32[]{:S(2)}, u32[]{:S(2)}) collective-permute-start(bf16[64,2048]{1,0:T(8,128)(2,1)S(1)} %fusion.3), channel_id=1, source_target_pairs={{0,4},{1,3},{2,0},{3,7},{4,8},{5,1},{6,2},{7,11},{8,12},{9,5},{10,... | collective-permute-start | bytes 786440 | tf_op jit(solution)/shard_map/ppermute | solution.py:235
  84.3 2.5 %serve_rows.8.home = f32[128,2048]{1,0:T(8,128)S(1)} custom-call(bf16[1024,128]{1,0:T(8,128)(2,1)S(1)} %get-tuple-element.20.refs_0_, bf16[1056,128]{1,0:T(8,128)(2,1)S(1)} %get-tuple-element.21.refs_1_, bf16[2048,768]{1,0:T(8,128)(2,1)S(1)} %get-tuple-element.22.refs_2_.refs_1_, bf16[2048,384]{1,0:T(8,128)(2,1)S(1)} %get-tuple-element.23.refs_3_.refs_2_, ...), custom_call_target="tpu_custom_call" | custom-call | tf_op jit(solution)/shard_map/serve_rows/pallas_call | solution.py:200
  86.8 0.8 finish.2.refs_0_
  87.6 1.5 %collective-permute-done.18.got = bf16[64,2048]{1,0:T(8,128)(2,1)S(1)} collective-permute-done((bf16[64,2048]{1,0:T(8,128)(2,1)S(1)}, bf16[64,2048]{1,0:T(8,128)(2,1)S(1)}, u32[]{:S(2)}, u32[]{:S(2)}) %collective-permute-start.18) | collective-permute-done | bytes 262176 | tf_op jit(solution)/shard_map/ppermute | solution.py:235
  89.1 0.8 finish.3
  (15 shorter events, 0.7 us)
Async XLA Ops:
  0.0 14.1 %collective-permute-start = (bf16[2048,768]{1,0:T(8,128)(2,1)}, bf16[2048,768]{1,0:T(8,128)(2,1)S(1)}, u32[]{:S(2)}, u32[]{:S(2)}) collective-permute-start(bf16[2048,768]{1,0:T(8,128)(2,1)} %bitcast.4), channel_id=1, source_target_pairs={{0,1},{1,0},{2,3},{3,2},{4,5},{5,4},{6,7},{7,6},{8,9},{9,8},{10,11... | collective-permute-start | bytes 9437192 | tf_op jit(solution)/shard_map/ppermute | solution.py:187
  0.5 13.6 %collective-permute-start.1 = (bf16[2048,384]{1,0:T(8,128)(2,1)}, bf16[2048,384]{1,0:T(8,128)(2,1)S(1)}, u32[]{:S(2)}, u32[]{:S(2)}) collective-permute-start(bf16[2048,384]{1,0:T(8,128)(2,1)} %bitcast.6), channel_id=1, source_target_pairs={{0,1},{1,0},{2,3},{3,2},{4,5},{5,4},{6,7},{7,6},{8,9},{9,8},{10,11... | collective-permute-start | bytes 4718600 | tf_op jit(solution)/shard_map/ppermute | solution.py:187
  1.7 7.5 %collective-permute-start.4 = (bf16[1056,128]{1,0:T(8,128)(2,1)S(1)}, bf16[1056,128]{1,0:T(8,128)(2,1)S(1)}, u32[]{:S(2)}, u32[]{:S(2)}) collective-permute-start(bf16[1056,128]{1,0:T(8,128)(2,1)S(1)} %get-tuple-element.21.refs_1_), channel_id=1, source_target_pairs={{0,4},{1,3},{2,0},{3,7},{4,8},{5,1},{6,2},{7,11},{8,12},{9,5},{10,... | collective-permute-start | bytes 811016 | tf_op jit(solution)/shard_map/ppermute | solution.py:185
  4.8 7.2 %collective-permute-start.2 = (bf16[1024,128]{1,0:T(8,128)(2,1)S(1)}, bf16[1024,128]{1,0:T(8,128)(2,1)S(1)}, u32[]{:S(2)}, u32[]{:S(2)}) collective-permute-start(bf16[1024,128]{1,0:T(8,128)(2,1)S(1)} %get-tuple-element.20.refs_0_), channel_id=1, source_target_pairs={{0,4},{1,3},{2,0},{3,7},{4,8},{5,1},{6,2},{7,11},{8,12},{9,5},{10,... | collective-permute-start | bytes 786440 | tf_op jit(solution)/shard_map/ppermute | solution.py:185
  9.2 9.2 %collective-permute-start.5 = (bf16[1056,128]{1,0:T(8,128)(2,1)S(1)}, bf16[1056,128]{1,0:T(8,128)(2,1)S(1)}, u32[]{:S(2)}, u32[]{:S(2)}) collective-permute-start(bf16[1056,128]{1,0:T(8,128)(2,1)S(1)} %collective-permute-done.4.refs_1_), channel_id=1, source_target_pairs={{0,4},{1,3},{2,0},{3,7},{4,8},{5,1},{6,2},{7,11},{8,12},{9,5},{10,... | collective-permute-start | bytes 811016 | tf_op jit(solution)/shard_map/ppermute | solution.py:219
  12.0 6.5 %collective-permute-start.3 = (bf16[1024,128]{1,0:T(8,128)(2,1)S(1)}, bf16[1024,128]{1,0:T(8,128)(2,1)S(1)}, u32[]{:S(2)}, u32[]{:S(2)}) collective-permute-start(bf16[1024,128]{1,0:T(8,128)(2,1)S(1)} %collective-permute-done.2.refs_0_), channel_id=1, source_target_pairs={{0,4},{1,3},{2,0},{3,7},{4,8},{5,1},{6,2},{7,11},{8,12},{9,5},{10,... | collective-permute-start | bytes 786440 | tf_op jit(solution)/shard_map/ppermute | solution.py:219
  16.7 9.2 %collective-permute-start.11 = (bf16[128,2048]{1,0:T(8,128)(2,1)S(1)}, bf16[128,2048]{1,0:T(8,128)(2,1)S(1)}, u32[]{:S(2)}, u32[]{:S(2)}) collective-permute-start(bf16[128,2048]{1,0:T(8,128)(2,1)S(1)} %convert_element_type.51), channel_id=1, source_target_pairs={{0,4},{1,3},{2,0},{3,7},{4,8},{5,1},{6,2},{7,11},{8,12},{9,5},{10,... | collective-permute-start | bytes 1572872 | tf_op jit(solution)/shard_map/ppermute | solution.py:235
  18.5 13.2 %collective-permute-start.6 = (bf16[2080,128]{1,0:T(8,128)(2,1)S(1)}, bf16[2080,128]{1,0:T(8,128)(2,1)S(1)}, u32[]{:S(2)}, u32[]{:S(2)}) collective-permute-start(bf16[2080,128]{1,0:T(8,128)(2,1)S(1)} %pad_maximum_fusion), channel_id=1, source_target_pairs={{0,4},{1,3},{2,0},{3,7},{4,8},{5,1},{6,2},{7,11},{8,12},{9,5},{10,... | collective-permute-start | bytes 1597448 | tf_op jit(solution)/shard_map/ppermute | solution.py:219
  26.1 11.2 %collective-permute-start.12 = (bf16[128,2048]{1,0:T(8,128)(2,1)S(1)}, bf16[128,2048]{1,0:T(8,128)(2,1)S(1)}, u32[]{:S(2)}, u32[]{:S(2)}) collective-permute-start(bf16[128,2048]{1,0:T(8,128)(2,1)S(1)} %add_convert_fusion.3), channel_id=1, source_target_pairs={{0,4},{1,3},{2,0},{3,7},{4,8},{5,1},{6,2},{7,11},{8,12},{9,5},{10,... | collective-permute-start | bytes 1572872 | tf_op jit(solution)/shard_map/ppermute | solution.py:235
  31.7 11.3 %collective-permute-start.7 = (bf16[2080,128]{1,0:T(8,128)(2,1)S(1)}, bf16[2080,128]{1,0:T(8,128)(2,1)S(1)}, u32[]{:S(2)}, u32[]{:S(2)}) collective-permute-start(bf16[2080,128]{1,0:T(8,128)(2,1)S(1)} %collective-permute-done.6.refs_0_), channel_id=1, source_target_pairs={{0,4},{1,3},{2,0},{3,7},{4,8},{5,1},{6,2},{7,11},{8,12},{9,5},{10,... | collective-permute-start | bytes 1597448 | tf_op jit(solution)/shard_map/ppermute | solution.py:219
  37.4 11.2 %collective-permute-start.13 = (bf16[128,2048]{1,0:T(8,128)(2,1)S(1)}, bf16[128,2048]{1,0:T(8,128)(2,1)S(1)}, u32[]{:S(2)}, u32[]{:S(2)}) collective-permute-start(bf16[128,2048]{1,0:T(8,128)(2,1)S(1)} %add_convert_fusion.2), channel_id=1, source_target_pairs={{0,4},{1,3},{2,0},{3,7},{4,8},{5,1},{6,2},{7,11},{8,12},{9,5},{10,... | collective-permute-start | bytes 1572872 | tf_op jit(solution)/shard_map/ppermute | solution.py:235
  43.0 11.3 %collective-permute-start.8 = (bf16[2080,128]{1,0:T(8,128)(2,1)S(1)}, bf16[2080,128]{1,0:T(8,128)(2,1)S(1)}, u32[]{:S(2)}, u32[]{:S(2)}) collective-permute-start(bf16[2080,128]{1,0:T(8,128)(2,1)S(1)} %collective-permute-done.7.refs_0_), channel_id=1, source_target_pairs={{0,4},{1,3},{2,0},{3,7},{4,8},{5,1},{6,2},{7,11},{8,12},{9,5},{10,... | collective-permute-start | bytes 1597448 | tf_op jit(solution)/shard_map/ppermute | solution.py:219
  48.7 11.2 %collective-permute-start.14 = (bf16[128,2048]{1,0:T(8,128)(2,1)S(1)}, bf16[128,2048]{1,0:T(8,128)(2,1)S(1)}, u32[]{:S(2)}, u32[]{:S(2)}) collective-permute-start(bf16[128,2048]{1,0:T(8,128)(2,1)S(1)} %add_convert_fusion.1), channel_id=1, source_target_pairs={{0,4},{1,3},{2,0},{3,7},{4,8},{5,1},{6,2},{7,11},{8,12},{9,5},{10,... | collective-permute-start | bytes 1572872 | tf_op jit(solution)/shard_map/ppermute | solution.py:235
  54.3 11.3 %collective-permute-start.9 = (bf16[2080,128]{1,0:T(8,128)(2,1)S(1)}, bf16[2080,128]{1,0:T(8,128)(2,1)S(1)}, u32[]{:S(2)}, u32[]{:S(2)}) collective-permute-start(bf16[2080,128]{1,0:T(8,128)(2,1)S(1)} %collective-permute-done.8.refs_0_), channel_id=1, source_target_pairs={{0,4},{1,3},{2,0},{3,7},{4,8},{5,1},{6,2},{7,11},{8,12},{9,5},{10,... | collective-permute-start | bytes 1597448 | tf_op jit(solution)/shard_map/ppermute | solution.py:219
  60.1 11.2 %collective-permute-start.15 = (bf16[128,2048]{1,0:T(8,128)(2,1)S(1)}, bf16[128,2048]{1,0:T(8,128)(2,1)S(1)}, u32[]{:S(2)}, u32[]{:S(2)}) collective-permute-start(bf16[128,2048]{1,0:T(8,128)(2,1)S(1)} %add_convert_fusion), channel_id=1, source_target_pairs={{0,4},{1,3},{2,0},{3,7},{4,8},{5,1},{6,2},{7,11},{8,12},{9,5},{10,... | collective-permute-start | bytes 1572872 | tf_op jit(solution)/shard_map/ppermute | solution.py:235
  65.7 11.3 %collective-permute-start.10 = (bf16[2080,128]{1,0:T(8,128)(2,1)S(1)}, bf16[2080,128]{1,0:T(8,128)(2,1)S(1)}, u32[]{:S(2)}, u32[]{:S(2)}) collective-permute-start(bf16[2080,128]{1,0:T(8,128)(2,1)S(1)} %collective-permute-done.9.refs_0_), channel_id=1, source_target_pairs={{0,4},{1,3},{2,0},{3,7},{4,8},{5,1},{6,2},{7,11},{8,12},{9,5},{10,... | collective-permute-start | bytes 1597448 | tf_op jit(solution)/shard_map/ppermute | solution.py:219
  71.4 8.4 %collective-permute-start.17 = (bf16[64,2048]{1,0:T(8,128)(2,1)S(1)}, bf16[64,2048]{1,0:T(8,128)(2,1)S(1)}, u32[]{:S(2)}, u32[]{:S(2)}) collective-permute-start(bf16[64,2048]{1,0:T(8,128)(2,1)S(1)} %fusion.1), channel_id=1, source_target_pairs={{0,4},{1,3},{2,0},{3,7},{4,8},{5,1},{6,2},{7,11},{8,12},{9,5},{10,... | collective-permute-start | bytes 786440 | tf_op jit(solution)/shard_map/ppermute | solution.py:235
  73.1 9.5 %collective-permute-start.16 = (bf16[64,2048]{1,0:T(8,128)(2,1)S(1)}, bf16[64,2048]{1,0:T(8,128)(2,1)S(1)}, u32[]{:S(2)}, u32[]{:S(2)}) collective-permute-start(bf16[64,2048]{1,0:T(8,128)(2,1)S(1)} %fusion.2), channel_id=1, source_target_pairs={{0,4},{1,3},{2,0},{3,7},{4,8},{5,1},{6,2},{7,11},{8,12},{9,5},{10,... | collective-permute-start | bytes 786440 | tf_op jit(solution)/shard_map/ppermute | solution.py:235
  79.8 7.0 %collective-permute-start.19 = (bf16[64,2048]{1,0:T(8,128)(2,1)S(1)}, bf16[64,2048]{1,0:T(8,128)(2,1)S(1)}, u32[]{:S(2)}, u32[]{:S(2)}) collective-permute-start(bf16[64,2048]{1,0:T(8,128)(2,1)S(1)} %fusion), channel_id=1, source_target_pairs={{0,4},{1,3},{2,0},{3,7},{4,8},{5,1},{6,2},{7,11},{8,12},{9,5},{10,... | collective-permute-start | bytes 786440 | tf_op jit(solution)/shard_map/ppermute | solution.py:235
  82.7 6.4 %collective-permute-start.18 = (bf16[64,2048]{1,0:T(8,128)(2,1)S(1)}, bf16[64,2048]{1,0:T(8,128)(2,1)S(1)}, u32[]{:S(2)}, u32[]{:S(2)}) collective-permute-start(bf16[64,2048]{1,0:T(8,128)(2,1)S(1)} %fusion.3), channel_id=1, source_target_pairs={{0,4},{1,3},{2,0},{3,7},{4,8},{5,1},{6,2},{7,11},{8,12},{9,5},{10,... | collective-permute-start | bytes 786440 | tf_op jit(solution)/shard_map/ppermute | solution.py:235
where the time goes:
time: 90.2 us; the launch traced here: 90 us
  starting transfers between devices  32.6 us (36%)
  waiting for transfers between devices  30.8 us (34%)
  Pallas kernels  25.4 us (28%)
    pallas_call x8, Pallas kernels, serve(): pl.pallas_call(functools.partial(serve_rows, width, picks, partner), out_...  20.4 us
    ppermute x7, waiting for transfers between devices, ring(): away[at] = hop(x)  18.1 us
    ppermute x9, starting transfers between devices, ring(): total.append(hop(x))  14.7 us
    ppermute x7, starting transfers between devices, ring(): away[at] = hop(x)  12.7 us
    ppermute x9, waiting for transfers between devices, ring(): total.append(hop(x))  11.5 us
    ppermute x2, starting transfers between devices, ring(): away.append(hop(x))  4.68 us
    pallas_call x1, Pallas kernels, ring(): pl.pallas_call(load, out_shape=[jax.ShapeDtypeStruct(w.shape, w.dtype) fo...  2.37 us
  transfers between devices with their start and end apart: 20, of which 16 were waited for; matrix products, arithmetic and copies ran while one was open for 1% of the time, Pallas kernels for 27%

commit v1 on v0

--- a/solution.py
+++ b/solution.py
@@ -70,19 +70,29 @@
 LANES = 128
 
 
-def pack_rows(num_experts, tokens, ids_far, weights_far, out_a, out_b, ids, weights, done):
-    outs = (out_a, out_b)
-    tok_rows, features = tokens.shape
-    half = features // 2
-    pairs = [(ids_far, ids), (weights_far, weights)]
-    for start in range(0, features, LANES):
-        at = start % half // LANES * tok_rows
-        pairs.append(
-            (tokens.at[:, start : start + LANES], outs[start // half].at[at : at + tok_rows])
-        )
+def start_copies(pairs, done):
     copies = [pltpu.make_async_copy(a, b, done.at[i]) for i, (a, b) in enumerate(pairs)]
     for copy in copies:
         copy.start()
+    return copies
+
+
+def column_blocks(tokens, start, out):
+    tok_rows = tokens.shape[0]
+    for at in range(0, out.shape[0] - tok_rows + 1, tok_rows):
+        lane = start + at // tok_rows * LANES
+        yield tokens.at[:, lane : lane + LANES], out.at[at : at + tok_rows]
+
+
+def pack_rows(tokens, out, done):
+    for copy in start_copies(column_blocks(tokens, 0, out), done):
+        copy.wait()
+
+
+def pack_shares(num_experts, tokens, ids_far, weights_far, out, ids, weights, done):
+    tok_rows, features = tokens.shape
+    pairs = [(ids_far, ids), (weights_far, weights)]
+    copies = start_copies([*pairs, *column_blocks(tokens, features // 2, out)], done)
     for copy in copies[:2]:
         copy.wait()
     place = lax.broadcasted_iota(jnp.int32, (num_experts, tok_rows), 0)
@@ -92,39 +102,33 @@
         share += jnp.where(named, weights[choice : choice + 1], 0.0)
     high = share.astype(jnp.bfloat16).astype(jnp.float32)
     both = jnp.concatenate([high, share - high], axis=0)
-    out_b[half // LANES * tok_rows :] = both.astype(jnp.bfloat16)
+    out[-2 * num_experts :] = both.astype(jnp.bfloat16)
     for copy in copies[2:]:
         copy.wait()
 
 
 def load(*refs):
     count = len(refs) // 2
-    done = refs[-1]
-    copies = [pltpu.make_async_copy(refs[i], refs[count + i], done.at[i]) for i in range(count)]
-    for copy in copies:
-        copy.start()
-    for copy in copies:
+    for copy in start_copies(zip(refs[:count], refs[count : 2 * count]), refs[-1]):
         copy.wait()
 
 
-def serve_rows(width, picks, partner, *refs):
-    pieces, refs, out = refs[: -1 - 2 * len(picks)], refs[-1 - 2 * len(picks) : -1], refs[-1]
-    tok_rows, _ = out.shape
+def serve_rows(width, tok_rows, first, partner, *refs):
+    pieces, refs, out = refs[:-5], refs[-5:-1], refs[-1]
+    last = first + out.shape[0]
     num_experts = len(partner)
     rows = [
-        piece[at : at + tok_rows]
+        piece[at + first : at + last]
         for piece in pieces
         for at in range(0, piece.shape[0] - tok_rows + 1, tok_rows)
     ]
     rows = jnp.concatenate(rows, axis=1)
-    shares = jnp.transpose(pieces[-1][-2 * num_experts :].astype(jnp.float32))
+    shares = jnp.transpose(pieces[-1][-2 * num_experts :].astype(jnp.float32))[first:last]
     lanes = lax.broadcasted_iota(jnp.int32, shares.shape, 1)
     me = lax.axis_index("expert")
     other = sum(jnp.where(me == e, partner[e], 0) for e in range(num_experts))
     total = None
-    for place, which in enumerate(picks):
-        gate, down = refs[2 * place], refs[2 * place + 1]
-        expert = (me, other)[which]
+    for expert, gate, down in ((me, *refs[:2]), (other, *refs[2:])):
         share = jnp.where((lanes == expert) | (lanes == expert + num_experts), shares, 0.0)
         share = jnp.sum(share, axis=1, keepdims=True)
         pre = jnp.dot(rows, gate[...], preferred_element_type=jnp.float32)
@@ -164,22 +168,35 @@
     swap = functools.partial(lax.ppermute, axis_name="expert", perm=list(enumerate(partner)))
     whole = pl.BlockSpec(memory_space=pltpu.VMEM)
 
+    far = pl.BlockSpec(memory_space=pltpu.HBM)
     given = (tokens, expert_ids.T, route_weights.T)
     given = [pltpu.with_memory_space_constraint(x, pltpu.HBM) for x in given]
     half = features // 2 // LANES * tok_rows
-    packed = pl.pallas_call(
-        functools.partial(pack_rows, num_experts),
-        out_shape=[
-            jax.ShapeDtypeStruct((rows, LANES), jnp.bfloat16)
-            for rows in (half, half + 2 * num_experts)
-        ],
-        in_specs=[pl.BlockSpec(memory_space=pltpu.HBM)] * 3,
-        out_specs=[whole] * 2,
-        scratch_shapes=[pltpu.VMEM(x.shape, x.dtype) for x in given[1:]]
-        + [pltpu.SemaphoreType.DMA((2 + features // LANES,))],
-        compiler_params=pltpu.CompilerParams(vmem_limit_bytes=8 * 1024 * 1024),
-        name="pack_rows",
-    )(*given)
+    blocks = half // tok_rows
+    small = pltpu.CompilerParams(vmem_limit_bytes=4 * 1024 * 1024)
+    packed = [
+        pl.pallas_call(
+            pack_rows,
+            out_shape=jax.ShapeDtypeStruct((half, LANES), jnp.bfloat16),
+            in_specs=[far],
+            out_specs=whole,
+            scratch_shapes=[pltpu.SemaphoreType.DMA((blocks,))],
+            compiler_params=small,
+            name="pack_rows",
+        )(given[0])
+    ]
+    packed.append(
+        pl.pallas_call(
+            functools.partial(pack_shares, num_experts),
+            out_shape=jax.ShapeDtypeStruct((half + 2 * num_experts, LANES), jnp.bfloat16),
+            in_specs=[far] * 3,
+            out_specs=whole,
+            scratch_shapes=[pltpu.VMEM(x.shape, x.dtype) for x in given[1:]]
+            + [pltpu.SemaphoreType.DMA((2 + blocks,))],
+            compiler_params=small,
+            name="pack_shares",
+        )(*given)
+    )
     away = []
     for x in packed:
         away.append(hop(x))
@@ -194,17 +211,17 @@
         compiler_params=pltpu.CompilerParams(vmem_limit_bytes=2 * 1024 * 1024),
         name="load",
     )(*(pltpu.with_memory_space_constraint(w, pltpu.HBM) for w in own))
-    weights = (held, swapped)
-
-    def serve(pieces, picks):
+    weights = (*held, *swapped)
+
+    def serve(pieces, first, rows):
         return pl.pallas_call(
-            functools.partial(serve_rows, width, picks, partner),
-            out_shape=jax.ShapeDtypeStruct((tok_rows, features), jnp.float32),
-            in_specs=[whole] * (len(pieces) + 2 * len(picks)),
+            functools.partial(serve_rows, width, tok_rows, first, partner),
+            out_shape=jax.ShapeDtypeStruct((rows, features), jnp.float32),
+            in_specs=[whole] * (len(pieces) + len(weights)),
             out_specs=whole,
             compiler_params=pltpu.CompilerParams(vmem_limit_bytes=8 * 1024 * 1024),
             name="serve_rows",
-        )(*pieces, *(w for which in picks for w in weights[which]))
+        )(*pieces, *weights)
 
     def after(arrays, other):
         return [lax.optimization_barrier((x, other))[0] for x in arrays]
@@ -217,13 +234,18 @@
             away = away if step == 1 else [jnp.concatenate(away)]
             for at, x in enumerate(away):
                 away[at] = hop(x)
-        more = serve(here, (0, 1))
-        away = after(away, more)
-        parts = 2 if step >= count - 2 else 1
-        more = jnp.split(more, parts)
-        if total is not None:
-            if len(total) < parts:
-                total = jnp.split(total[0], parts)
+        parts = 2 if step == 1 or step >= count - 2 else 1
+        if step == 1:
+            more = []
+            for at in range(parts):
+                more.append(serve(here, at * tok_rows // parts, tok_rows // parts))
+            away = after(away, tuple(more))
+        else:
+            more = serve(here, 0, tok_rows)
+            away = after(away, more)
+            more = jnp.split(more, parts)
+        if total is not None and len(total) != parts:
+            total = jnp.split(total[0], parts) if len(total) < parts else [jnp.concatenate(total)]
         sent = []
         for at, x in enumerate(more):
             if total is not None:
@@ -233,8 +255,7 @@
         total = []
         for x in sent:
             total.append(hop(x))
-    home = serve(packed, (0, 1))
-    far = pl.BlockSpec(memory_space=pltpu.HBM)
+    home = serve(packed, 0, tok_rows)
     out, rows = [], tok_rows // len(total)
     for at, got in enumerate(total):
         out = [
@@ -248,7 +269,7 @@
                     pltpu.VMEM((rows, features), tokens.dtype),
                     pltpu.SemaphoreType.DMA(()),
                 ],
-                compiler_params=pltpu.CompilerParams(vmem_limit_bytes=4 * 1024 * 1024),
+                compiler_params=small,
                 name="finish",
             )(home, got, *out)
         ]
@@ -265,7 +286,7 @@
     )
 
     stops = chip_cycle(mesh)
-    cycle = mesh.shape["token"] == 1 and {len(s) for s in stops} == {2} and len(stops) > 2
+    cycle = mesh.shape["token"] == 1 and {len(s) for s in stops} == {2} and len(stops) > 4
 
     def per_device(tokens, expert_ids, route_weights, gate_up, down_t):
         fits = cycle and mesh.shape["expert"] <= 4 * expert_ids.shape[1] and gate_up.shape[0] == 1

time: 90.2 us -> 95.4 us (1.058)
  Pallas kernels: 25.4 us -> 29 us
  waiting for transfers between devices: 30.8 us -> 32.1 us
    ppermute x9 -> x10, waiting for transfers between devices: 11.5 us -> 15.5 us  [ring(): total.append(hop(x))]
    pallas_call x9 -> x11, Pallas kernels: 21.5 us -> 25.1 us  [the longest x9 23.1 us: serve(): pl.pallas_call(functools.partial(serve_rows, width, tok_rows, first, part...]
    ppermute x7, waiting for transfers between devices: 18.1 us -> 15.8 us  [ring(): away[at] = hop(x)]
    ppermute x9 -> x10, starting transfers between devices: 14.7 us -> 16.2 us  [ring(): total.append(hop(x))]
    ppermute x7, starting transfers between devices: 12.7 us -> 11.4 us  [ring(): away[at] = hop(x)]
  transfers between devices with their start and end apart: 20 -> 21, of which waited for: 16 -> 13; matrix products, arithmetic and copies ran while one was open for 1% -> 1% of each run, Pallas kernels for 27% -> 30%
where the time goes in v1:
time: 95.4 us; the launch traced here: 95.1 us
  starting transfers between devices  32.9 us (34%)
  waiting for transfers between devices  32.1 us (34%)
  Pallas kernels  29 us (30%)
    pallas_call x9, Pallas kernels, serve(): pl.pallas_call(functools.partial(serve_rows, width, tok_rows, first, part...  23.1 us
    ppermute x10, starting transfers between devices, ring(): total.append(hop(x))  16.2 us
    ppermute x7, waiting for transfers between devices, ring(): away[at] = hop(x)  15.8 us
    ppermute x10, waiting for transfers between devices, ring(): total.append(hop(x))  15.5 us
    ppermute x7, starting transfers between devices, ring(): away[at] = hop(x)  11.4 us
    ppermute x2, starting transfers between devices, ring(): away.append(hop(x))  4.73 us
    pallas_call x1, Pallas kernels, ring(): pl.pallas_call(load, out_shape=[jax.ShapeDtypeStruct(w.shape, w.dtype) fo...  2.37 us
  transfers between devices with their start and end apart: 21, of which 13 were waited for; matrix products, arithmetic and copies ran while one was open for 1% of the time, Pallas kernels for 30%

profile of v1, /device:TPU:0, one launch (start us, length us, event | category | flops | bytes accessed | tf_op | source)
XLA Modules:
  0.0 95.1 jit_solution(13696174965606634855)
XLA Ops:
  0.0 0.5 collective-permute-start
  0.5 1.0 %pack_shares.1.refs_1_ = bf16[1056,128]{1,0:T(8,128)(2,1)S(1)} custom-call(bf16[128,2048]{1,0:T(8,128)(2,1)} %tokens.3, s32[8,128]{1,0:T(8,128)} %bitcast.8, f32[8,128]{1,0:T(8,128)} %bitcast.9), custom_call_target="tpu_custom_call" | custom-call | tf_op jit(solution)/shard_map/pack_shares/pallas_call | solution.py:189
  1.5 3.1 %collective-permute-start.4 = (bf16[1056,128]{1,0:T(8,128)(2,1)S(1)}, bf16[1056,128]{1,0:T(8,128)(2,1)S(1)}, u32[]{:S(2)}, u32[]{:S(2)}) collective-permute-start(bf16[1056,128]{1,0:T(8,128)(2,1)S(1)} %pack_shares.1.refs_1_), channel_id=1, source_target_pairs={{0,4},{1,3},{2,0},{3,7},{4,8},{5,1},{6,2},{7,11},{8,12},{9,5},{10,... | collective-permute-start | bytes 811016 | tf_op jit(solution)/shard_map/ppermute | solution.py:202
  4.6 0.9 pack_rows.1.refs_0_
  5.6 1.6 %collective-permute-start.2 = (bf16[1024,128]{1,0:T(8,128)(2,1)S(1)}, bf16[1024,128]{1,0:T(8,128)(2,1)S(1)}, u32[]{:S(2)}, u32[]{:S(2)}) collective-permute-start(bf16[1024,128]{1,0:T(8,128)(2,1)S(1)} %pack_rows.1.refs_0_), channel_id=1, source_target_pairs={{0,4},{1,3},{2,0},{3,7},{4,8},{5,1},{6,2},{7,11},{8,12},{9,5},{10,... | collective-permute-start | bytes 786440 | tf_op jit(solution)/shard_map/ppermute | solution.py:202
  7.2 2.4 %load.1 = (bf16[2048,768]{1,0:T(8,128)(2,1)S(1)}, bf16[2048,384]{1,0:T(8,128)(2,1)S(1)}) custom-call(bf16[2048,768]{1,0:T(8,128)(2,1)} %bitcast.5, bf16[2048,384]{1,0:T(8,128)(2,1)} %bitcast.7), custom_call_target="tpu_custom_call" | custom-call | tf_op jit(solution)/shard_map/load/pallas_call | solution.py:205
  9.6 1.6 %collective-permute-start.5 = (bf16[1056,128]{1,0:T(8,128)(2,1)S(1)}, bf16[1056,128]{1,0:T(8,128)(2,1)S(1)}, u32[]{:S(2)}, u32[]{:S(2)}) collective-permute-start(bf16[1056,128]{1,0:T(8,128)(2,1)S(1)} %collective-permute-done.4.refs_1_), channel_id=1, source_target_pairs={{0,4},{1,3},{2,0},{3,7},{4,8},{5,1},{6,2},{7,11},{8,12},{9,5},{10,... | collective-permute-start | bytes 811016 | tf_op jit(solution)/shard_map/ppermute | solution.py:236
  11.2 0.8 collective-permute-done.2.refs_0_
  12.0 1.9 %collective-permute-start.3 = (bf16[1024,128]{1,0:T(8,128)(2,1)S(1)}, bf16[1024,128]{1,0:T(8,128)(2,1)S(1)}, u32[]{:S(2)}, u32[]{:S(2)}) collective-permute-start(bf16[1024,128]{1,0:T(8,128)(2,1)S(1)} %collective-permute-done.2.refs_0_), channel_id=1, source_target_pairs={{0,4},{1,3},{2,0},{3,7},{4,8},{5,1},{6,2},{7,11},{8,12},{9,5},{10,... | collective-permute-start | bytes 786440 | tf_op jit(solution)/shard_map/ppermute | solution.py:236
  13.9 2.6 %serve_rows.10 = f32[64,2048]{1,0:T(8,128)S(1)} custom-call(bf16[1024,128]{1,0:T(8,128)(2,1)S(1)} %collective-permute-done.2.refs_0_, bf16[1056,128]{1,0:T(8,128)(2,1)S(1)} %collective-permute-done.4.refs_1_, bf16[2048,768]{1,0:T(8,128)(2,1)S(1)} %get-tuple-element.18.refs_2_.refs_1_, bf16[2048,384]{1,0:T(8,128)(2,1)S(1)} %get-tuple-element.19.refs_3_.refs_2_, ...), custom_call_target="tpu_custom_call" | custom-call | tf_op jit(solution)/shard_map/serve_rows/pallas_call | solution.py:217
  16.6 2.6 %serve_rows.11 = f32[64,2048]{1,0:T(8,128)S(1)} custom-call(bf16[1024,128]{1,0:T(8,128)(2,1)S(1)} %collective-permute-done.2.refs_0_, bf16[1056,128]{1,0:T(8,128)(2,1)S(1)} %collective-permute-done.4.refs_1_, bf16[2048,768]{1,0:T(8,128)(2,1)S(1)} %get-tuple-element.18.refs_2_.refs_1_, bf16[2048,384]{1,0:T(8,128)(2,1)S(1)} %get-tuple-element.19.refs_3_.refs_2_, ...), custom_call_target="tpu_custom_call" | custom-call | tf_op jit(solution)/shard_map/serve_rows/pallas_call | solution.py:217
  19.3 1.6 %collective-permute-start.12 = (bf16[64,2048]{1,0:T(8,128)(2,1)S(1)}, bf16[64,2048]{1,0:T(8,128)(2,1)S(1)}, u32[]{:S(2)}, u32[]{:S(2)}) collective-permute-start(bf16[64,2048]{1,0:T(8,128)(2,1)S(1)} %convert_element_type.55), channel_id=1, source_target_pairs={{0,4},{1,3},{2,0},{3,7},{4,8},{5,1},{6,2},{7,11},{8,12},{9,5},{10,... | collective-permute-start | bytes 786440 | tf_op jit(solution)/shard_map/ppermute | solution.py:257
  20.9 1.6 %collective-permute-start.11 = (bf16[64,2048]{1,0:T(8,128)(2,1)S(1)}, bf16[64,2048]{1,0:T(8,128)(2,1)S(1)}, u32[]{:S(2)}, u32[]{:S(2)}) collective-permute-start(bf16[64,2048]{1,0:T(8,128)(2,1)S(1)} %convert_element_type.54), channel_id=1, source_target_pairs={{0,4},{1,3},{2,0},{3,7},{4,8},{5,1},{6,2},{7,11},{8,12},{9,5},{10,... | collective-permute-start | bytes 786440 | tf_op jit(solution)/shard_map/ppermute | solution.py:257
  22.6 1.5 %collective-permute-start.6 = (bf16[2080,128]{1,0:T(8,128)(2,1)S(1)}, bf16[2080,128]{1,0:T(8,128)(2,1)S(1)}, u32[]{:S(2)}, u32[]{:S(2)}) collective-permute-start(bf16[2080,128]{1,0:T(8,128)(2,1)S(1)} %pad_maximum_fusion), channel_id=1, source_target_pairs={{0,4},{1,3},{2,0},{3,7},{4,8},{5,1},{6,2},{7,11},{8,12},{9,5},{10,... | collective-permute-start | bytes 1597448 | tf_op jit(solution)/shard_map/ppermute | solution.py:236
  24.1 2.5 %serve_rows.12 = f32[128,2048]{1,0:T(8,128)S(1)} custom-call(bf16[1024,128]{1,0:T(8,128)(2,1)S(1)} %collective-permute-done.3.refs_0_, bf16[1056,128]{1,0:T(8,128)(2,1)S(1)} %collective-permute-done.5.refs_1_, bf16[2048,768]{1,0:T(8,128)(2,1)S(1)} %get-tuple-element.18.refs_2_.refs_1_, bf16[2048,384]{1,0:T(8,128)(2,1)S(1)} %get-tuple-element.19.refs_3_.refs_2_, ...), custom_call_target="tpu_custom_call" | custom-call | tf_op jit(solution)/shard_map/serve_rows/pallas_call | solution.py:217
  26.7 1.9 %collective-permute-done.11 = bf16[64,2048]{1,0:T(8,128)(2,1)S(1)} collective-permute-done((bf16[64,2048]{1,0:T(8,128)(2,1)S(1)}, bf16[64,2048]{1,0:T(8,128)(2,1)S(1)}, u32[]{:S(2)}, u32[]{:S(2)}) %collective-permute-start.11) | collective-permute-done | bytes 262176 | tf_op jit(solution)/shard_map/ppermute | solution.py:257
  28.7 1.6 %collective-permute-start.13 = (bf16[128,2048]{1,0:T(8,128)(2,1)S(1)}, bf16[128,2048]{1,0:T(8,128)(2,1)S(1)}, u32[]{:S(2)}, u32[]{:S(2)}) collective-permute-start(bf16[128,2048]{1,0:T(8,128)(2,1)S(1)} %add_convert_fusion.3), channel_id=1, source_target_pairs={{0,4},{1,3},{2,0},{3,7},{4,8},{5,1},{6,2},{7,11},{8,12},{9,5},{10,... | collective-permute-start | bytes 1572872 | tf_op jit(solution)/shard_map/ppermute | solution.py:257
  30.3 4.0 %collective-permute-done.6.refs_0_ = bf16[2080,128]{1,0:T(8,128)(2,1)S(1)} collective-permute-done((bf16[2080,128]{1,0:T(8,128)(2,1)S(1)}, bf16[2080,128]{1,0:T(8,128)(2,1)S(1)}, u32[]{:S(2)}, u32[]{:S(2)}) %collective-permute-start.6) | collective-permute-done | bytes 532512 | tf_op jit(solution)/shard_map/ppermute | solution.py:236
  34.2 1.6 %collective-permute-start.7 = (bf16[2080,128]{1,0:T(8,128)(2,1)S(1)}, bf16[2080,128]{1,0:T(8,128)(2,1)S(1)}, u32[]{:S(2)}, u32[]{:S(2)}) collective-permute-start(bf16[2080,128]{1,0:T(8,128)(2,1)S(1)} %collective-permute-done.6.refs_0_), channel_id=1, source_target_pairs={{0,4},{1,3},{2,0},{3,7},{4,8},{5,1},{6,2},{7,11},{8,12},{9,5},{10,... | collective-permute-start | bytes 1597448 | tf_op jit(solution)/shard_map/ppermute | solution.py:236
  35.8 2.6 %serve_rows.13 = f32[128,2048]{1,0:T(8,128)S(1)} custom-call(bf16[2080,128]{1,0:T(8,128)(2,1)S(1)} %collective-permute-done.6.refs_0_, bf16[2048,768]{1,0:T(8,128)(2,1)S(1)} %get-tuple-element.18.refs_2_.refs_1_, bf16[2048,384]{1,0:T(8,128)(2,1)S(1)} %get-tuple-element.19.refs_3_.refs_2_, bf16[2048,768]{1,0:T(8,128)(2,1)S(1)} %collective-permute-done.refs_4_.refs_3_, ...), custom_call_target="tpu_custom_call" | custom-call | tf_op jit(solution)/shard_map/serve_rows/pallas_call | solution.py:217
  38.4 1.5 %collective-permute-done.13 = bf16[128,2048]{1,0:T(8,128)(2,1)S(1)} collective-permute-done((bf16[128,2048]{1,0:T(8,128)(2,1)S(1)}, bf16[128,2048]{1,0:T(8,128)(2,1)S(1)}, u32[]{:S(2)}, u32[]{:S(2)}) %collective-permute-start.13) | collective-permute-done | bytes 524320 | tf_op jit(solution)/shard_map/ppermute | solution.py:257
  39.9 0.1 add_convert_fusion.2
  40.0 1.6 %collective-permute-start.14 = (bf16[128,2048]{1,0:T(8,128)(2,1)S(1)}, bf16[128,2048]{1,0:T(8,128)(2,1)S(1)}, u32[]{:S(2)}, u32[]{:S(2)}) collective-permute-start(bf16[128,2048]{1,0:T(8,128)(2,1)S(1)} %add_convert_fusion.2), channel_id=1, source_target_pairs={{0,4},{1,3},{2,0},{3,7},{4,8},{5,1},{6,2},{7,11},{8,12},{9,5},{10,... | collective-permute-start | bytes 1572872 | tf_op jit(solution)/shard_map/ppermute | solution.py:257
  41.6 3.9 %collective-permute-done.7.refs_0_ = bf16[2080,128]{1,0:T(8,128)(2,1)S(1)} collective-permute-done((bf16[2080,128]{1,0:T(8,128)(2,1)S(1)}, bf16[2080,128]{1,0:T(8,128)(2,1)S(1)}, u32[]{:S(2)}, u32[]{:S(2)}) %collective-permute-start.7) | collective-permute-done | bytes 532512 | tf_op jit(solution)/shard_map/ppermute | solution.py:236
  45.6 1.6 %collective-permute-start.8 = (bf16[2080,128]{1,0:T(8,128)(2,1)S(1)}, bf16[2080,128]{1,0:T(8,128)(2,1)S(1)}, u32[]{:S(2)}, u32[]{:S(2)}) collective-permute-start(bf16[2080,128]{1,0:T(8,128)(2,1)S(1)} %collective-permute-done.7.refs_0_), channel_id=1, source_target_pairs={{0,4},{1,3},{2,0},{3,7},{4,8},{5,1},{6,2},{7,11},{8,12},{9,5},{10,... | collective-permute-start | bytes 1597448 | tf_op jit(solution)/shard_map/ppermute | solution.py:236
  47.1 2.5 %serve_rows.14 = f32[128,2048]{1,0:T(8,128)S(1)} custom-call(bf16[2080,128]{1,0:T(8,128)(2,1)S(1)} %collective-permute-done.7.refs_0_, bf16[2048,768]{1,0:T(8,128)(2,1)S(1)} %get-tuple-element.18.refs_2_.refs_1_, bf16[2048,384]{1,0:T(8,128)(2,1)S(1)} %get-tuple-element.19.refs_3_.refs_2_, bf16[2048,768]{1,0:T(8,128)(2,1)S(1)} %collective-permute-done.refs_4_.refs_3_, ...), custom_call_target="tpu_custom_call" | custom-call | tf_op jit(solution)/shard_map/serve_rows/pallas_call | solution.py:217
  49.7 1.5 %collective-permute-done.14 = bf16[128,2048]{1,0:T(8,128)(2,1)S(1)} collective-permute-done((bf16[128,2048]{1,0:T(8,128)(2,1)S(1)}, bf16[128,2048]{1,0:T(8,128)(2,1)S(1)}, u32[]{:S(2)}, u32[]{:S(2)}) %collective-permute-start.14) | collective-permute-done | bytes 524320 | tf_op jit(solution)/shard_map/ppermute | solution.py:257
  51.3 1.6 %collective-permute-start.15 = (bf16[128,2048]{1,0:T(8,128)(2,1)S(1)}, bf16[128,2048]{1,0:T(8,128)(2,1)S(1)}, u32[]{:S(2)}, u32[]{:S(2)}) collective-permute-start(bf16[128,2048]{1,0:T(8,128)(2,1)S(1)} %add_convert_fusion.1), channel_id=1, source_target_pairs={{0,4},{1,3},{2,0},{3,7},{4,8},{5,1},{6,2},{7,11},{8,12},{9,5},{10,... | collective-permute-start | bytes 1572872 | tf_op jit(solution)/shard_map/ppermute | solution.py:257
  52.9 4.0 %collective-permute-done.8.refs_0_ = bf16[2080,128]{1,0:T(8,128)(2,1)S(1)} collective-permute-done((bf16[2080,128]{1,0:T(8,128)(2,1)S(1)}, bf16[2080,128]{1,0:T(8,128)(2,1)S(1)}, u32[]{:S(2)}, u32[]{:S(2)}) %collective-permute-start.8) | collective-permute-done | bytes 532512 | tf_op jit(solution)/shard_map/ppermute | solution.py:236
  56.9 1.6 %collective-permute-start.9 = (bf16[2080,128]{1,0:T(8,128)(2,1)S(1)}, bf16[2080,128]{1,0:T(8,128)(2,1)S(1)}, u32[]{:S(2)}, u32[]{:S(2)}) collective-permute-start(bf16[2080,128]{1,0:T(8,128)(2,1)S(1)} %collective-permute-done.8.refs_0_), channel_id=1, source_target_pairs={{0,4},{1,3},{2,0},{3,7},{4,8},{5,1},{6,2},{7,11},{8,12},{9,5},{10,... | collective-permute-start | bytes 1597448 | tf_op jit(solution)/shard_map/ppermute | solution.py:236
  58.5 2.6 %serve_rows.15 = f32[128,2048]{1,0:T(8,128)S(1)} custom-call(bf16[2080,128]{1,0:T(8,128)(2,1)S(1)} %collective-permute-done.8.refs_0_, bf16[2048,768]{1,0:T(8,128)(2,1)S(1)} %get-tuple-element.18.refs_2_.refs_1_, bf16[2048,384]{1,0:T(8,128)(2,1)S(1)} %get-tuple-element.19.refs_3_.refs_2_, bf16[2048,768]{1,0:T(8,128)(2,1)S(1)} %collective-permute-done.refs_4_.refs_3_, ...), custom_call_target="tpu_custom_call" | custom-call | tf_op jit(solution)/shard_map/serve_rows/pallas_call | solution.py:217
  61.0 1.5 %collective-permute-done.15 = bf16[128,2048]{1,0:T(8,128)(2,1)S(1)} collective-permute-done((bf16[128,2048]{1,0:T(8,128)(2,1)S(1)}, bf16[128,2048]{1,0:T(8,128)(2,1)S(1)}, u32[]{:S(2)}, u32[]{:S(2)}) %collective-permute-start.15) | collective-permute-done | bytes 524320 | tf_op jit(solution)/shard_map/ppermute | solution.py:257
  62.6 1.6 %collective-permute-start.16 = (bf16[128,2048]{1,0:T(8,128)(2,1)S(1)}, bf16[128,2048]{1,0:T(8,128)(2,1)S(1)}, u32[]{:S(2)}, u32[]{:S(2)}) collective-permute-start(bf16[128,2048]{1,0:T(8,128)(2,1)S(1)} %add_convert_fusion), channel_id=1, source_target_pairs={{0,4},{1,3},{2,0},{3,7},{4,8},{5,1},{6,2},{7,11},{8,12},{9,5},{10,... | collective-permute-start | bytes 1572872 | tf_op jit(solution)/shard_map/ppermute | solution.py:257
  64.2 4.0 %collective-permute-done.9.refs_0_ = bf16[2080,128]{1,0:T(8,128)(2,1)S(1)} collective-permute-done((bf16[2080,128]{1,0:T(8,128)(2,1)S(1)}, bf16[2080,128]{1,0:T(8,128)(2,1)S(1)}, u32[]{:S(2)}, u32[]{:S(2)}) %collective-permute-start.9) | collective-permute-done | bytes 532512 | tf_op jit(solution)/shard_map/ppermute | solution.py:236
  68.2 1.6 %collective-permute-start.10 = (bf16[2080,128]{1,0:T(8,128)(2,1)S(1)}, bf16[2080,128]{1,0:T(8,128)(2,1)S(1)}, u32[]{:S(2)}, u32[]{:S(2)}) collective-permute-start(bf16[2080,128]{1,0:T(8,128)(2,1)S(1)} %collective-permute-done.9.refs_0_), channel_id=1, source_target_pairs={{0,4},{1,3},{2,0},{3,7},{4,8},{5,1},{6,2},{7,11},{8,12},{9,5},{10,... | collective-permute-start | bytes 1597448 | tf_op jit(solution)/shard_map/ppermute | solution.py:236
  69.8 2.6 %serve_rows.16 = f32[128,2048]{1,0:T(8,128)S(1)} custom-call(bf16[2080,128]{1,0:T(8,128)(2,1)S(1)} %collective-permute-done.9.refs_0_, bf16[2048,768]{1,0:T(8,128)(2,1)S(1)} %get-tuple-element.18.refs_2_.refs_1_, bf16[2048,384]{1,0:T(8,128)(2,1)S(1)} %get-tuple-element.19.refs_3_.refs_2_, bf16[2048,768]{1,0:T(8,128)(2,1)S(1)} %collective-permute-done.refs_4_.refs_3_, ...), custom_call_target="tpu_custom_call" | custom-call | tf_op jit(solution)/shard_map/serve_rows/pallas_call | solution.py:217
  72.4 1.5 %collective-permute-done.16 = bf16[128,2048]{1,0:T(8,128)(2,1)S(1)} collective-permute-done((bf16[128,2048]{1,0:T(8,128)(2,1)S(1)}, bf16[128,2048]{1,0:T(8,128)(2,1)S(1)}, u32[]{:S(2)}, u32[]{:S(2)}) %collective-permute-start.16) | collective-permute-done | bytes 524320 | tf_op jit(solution)/shard_map/ppermute | solution.py:257
  73.9 1.6 %collective-permute-start.18 = (bf16[64,2048]{1,0:T(8,128)(2,1)S(1)}, bf16[64,2048]{1,0:T(8,128)(2,1)S(1)}, u32[]{:S(2)}, u32[]{:S(2)}) collective-permute-start(bf16[64,2048]{1,0:T(8,128)(2,1)S(1)} %fusion.1), channel_id=1, source_target_pairs={{0,4},{1,3},{2,0},{3,7},{4,8},{5,1},{6,2},{7,11},{8,12},{9,5},{10,... | collective-permute-start | bytes 786440 | tf_op jit(solution)/shard_map/ppermute | solution.py:257
  75.6 1.6 %collective-permute-start.17 = (bf16[64,2048]{1,0:T(8,128)(2,1)S(1)}, bf16[64,2048]{1,0:T(8,128)(2,1)S(1)}, u32[]{:S(2)}, u32[]{:S(2)}) collective-permute-start(bf16[64,2048]{1,0:T(8,128)(2,1)S(1)} %fusion.2), channel_id=1, source_target_pairs={{0,4},{1,3},{2,0},{3,7},{4,8},{5,1},{6,2},{7,11},{8,12},{9,5},{10,... | collective-permute-start | bytes 786440 | tf_op jit(solution)/shard_map/ppermute | solution.py:257
  77.3 5.1 %collective-permute-done.18 = bf16[64,2048]{1,0:T(8,128)(2,1)S(1)} collective-permute-done((bf16[64,2048]{1,0:T(8,128)(2,1)S(1)}, bf16[64,2048]{1,0:T(8,128)(2,1)S(1)}, u32[]{:S(2)}, u32[]{:S(2)}) %collective-permute-start.18) | collective-permute-done | bytes 262176 | tf_op jit(solution)/shard_map/ppermute | solution.py:257
  82.4 2.5 %serve_rows.17 = f32[128,2048]{1,0:T(8,128)S(1)} custom-call(bf16[2080,128]{1,0:T(8,128)(2,1)S(1)} %collective-permute-done.10.refs_0_, bf16[2048,768]{1,0:T(8,128)(2,1)S(1)} %get-tuple-element.18.refs_2_.refs_1_, bf16[2048,384]{1,0:T(8,128)(2,1)S(1)} %get-tuple-element.19.refs_3_.refs_2_, bf16[2048,768]{1,0:T(8,128)(2,1)S(1)} %collective-permute-done.refs_4_.refs_3_, ...), custom_call_target="tpu_custom_call" | custom-call | tf_op jit(solution)/shard_map/serve_rows/pallas_call | solution.py:217
  85.0 1.6 %collective-permute-start.20 = (bf16[64,2048]{1,0:T(8,128)(2,1)S(1)}, bf16[64,2048]{1,0:T(8,128)(2,1)S(1)}, u32[]{:S(2)}, u32[]{:S(2)}) collective-permute-start(bf16[64,2048]{1,0:T(8,128)(2,1)S(1)} %fusion), channel_id=1, source_target_pairs={{0,4},{1,3},{2,0},{3,7},{4,8},{5,1},{6,2},{7,11},{8,12},{9,5},{10,... | collective-permute-start | bytes 786440 | tf_op jit(solution)/shard_map/ppermute | solution.py:257
  86.7 1.6 %collective-permute-start.19 = (bf16[64,2048]{1,0:T(8,128)(2,1)S(1)}, bf16[64,2048]{1,0:T(8,128)(2,1)S(1)}, u32[]{:S(2)}, u32[]{:S(2)}) collective-permute-start(bf16[64,2048]{1,0:T(8,128)(2,1)S(1)} %fusion.3), channel_id=1, source_target_pairs={{0,4},{1,3},{2,0},{3,7},{4,8},{5,1},{6,2},{7,11},{8,12},{9,5},{10,... | collective-permute-start | bytes 786440 | tf_op jit(solution)/shard_map/ppermute | solution.py:257
  88.3 2.5 %serve_rows.9.home = f32[128,2048]{1,0:T(8,128)S(1)} custom-call(bf16[1024,128]{1,0:T(8,128)(2,1)S(1)} %pack_rows.1.refs_0_, bf16[1056,128]{1,0:T(8,128)(2,1)S(1)} %pack_shares.1.refs_1_, bf16[2048,768]{1,0:T(8,128)(2,1)S(1)} %get-tuple-element.18.refs_2_.refs_1_, bf16[2048,384]{1,0:T(8,128)(2,1)S(1)} %get-tuple-element.19.refs_3_.refs_2_, ...), custom_call_target="tpu_custom_call" | custom-call | tf_op jit(solution)/shard_map/serve_rows/pallas_call | solution.py:217
  90.8 0.6 collective-permute-done.20.got
  91.4 0.8 finish.2.refs_0_
  92.2 2.0 %collective-permute-done.19.got = bf16[64,2048]{1,0:T(8,128)(2,1)S(1)} collective-permute-done((bf16[64,2048]{1,0:T(8,128)(2,1)S(1)}, bf16[64,2048]{1,0:T(8,128)(2,1)S(1)}, u32[]{:S(2)}, u32[]{:S(2)}) %collective-permute-start.19) | collective-permute-done | bytes 262176 | tf_op jit(solution)/shard_map/ppermute | solution.py:257
  94.2 0.8 finish.3
  (20 shorter events, 0.7 us)
Async XLA Ops:
  0.0 13.9 %collective-permute-start = (bf16[2048,768]{1,0:T(8,128)(2,1)}, bf16[2048,768]{1,0:T(8,128)(2,1)S(1)}, u32[]{:S(2)}, u32[]{:S(2)}) collective-permute-start(bf16[2048,768]{1,0:T(8,128)(2,1)} %bitcast.4), channel_id=1, source_target_pairs={{0,1},{1,0},{2,3},{3,2},{4,5},{5,4},{6,7},{7,6},{8,9},{9,8},{10,11... | collective-permute-start | bytes 9437192 | tf_op jit(solution)/shard_map/ppermute | solution.py:204
  0.5 13.4 %collective-permute-start.1 = (bf16[2048,384]{1,0:T(8,128)(2,1)}, bf16[2048,384]{1,0:T(8,128)(2,1)S(1)}, u32[]{:S(2)}, u32[]{:S(2)}) collective-permute-start(bf16[2048,384]{1,0:T(8,128)(2,1)} %bitcast.6), channel_id=1, source_target_pairs={{0,1},{1,0},{2,3},{3,2},{4,5},{5,4},{6,7},{7,6},{8,9},{9,8},{10,11... | collective-permute-start | bytes 4718600 | tf_op jit(solution)/shard_map/ppermute | solution.py:204
  1.5 8.1 %collective-permute-start.4 = (bf16[1056,128]{1,0:T(8,128)(2,1)S(1)}, bf16[1056,128]{1,0:T(8,128)(2,1)S(1)}, u32[]{:S(2)}, u32[]{:S(2)}) collective-permute-start(bf16[1056,128]{1,0:T(8,128)(2,1)S(1)} %pack_shares.1.refs_1_), channel_id=1, source_target_pairs={{0,4},{1,3},{2,0},{3,7},{4,8},{5,1},{6,2},{7,11},{8,12},{9,5},{10,... | collective-permute-start | bytes 811016 | tf_op jit(solution)/shard_map/ppermute | solution.py:202
  5.6 6.4 %collective-permute-start.2 = (bf16[1024,128]{1,0:T(8,128)(2,1)S(1)}, bf16[1024,128]{1,0:T(8,128)(2,1)S(1)}, u32[]{:S(2)}, u32[]{:S(2)}) collective-permute-start(bf16[1024,128]{1,0:T(8,128)(2,1)S(1)} %pack_rows.1.refs_0_), channel_id=1, source_target_pairs={{0,4},{1,3},{2,0},{3,7},{4,8},{5,1},{6,2},{7,11},{8,12},{9,5},{10,... | collective-permute-start | bytes 786440 | tf_op jit(solution)/shard_map/ppermute | solution.py:202
  9.6 9.7 %collective-permute-start.5 = (bf16[1056,128]{1,0:T(8,128)(2,1)S(1)}, bf16[1056,128]{1,0:T(8,128)(2,1)S(1)}, u32[]{:S(2)}, u32[]{:S(2)}) collective-permute-start(bf16[1056,128]{1,0:T(8,128)(2,1)S(1)} %collective-permute-done.4.refs_1_), channel_id=1, source_target_pairs={{0,4},{1,3},{2,0},{3,7},{4,8},{5,1},{6,2},{7,11},{8,12},{9,5},{10,... | collective-permute-start | bytes 811016 | tf_op jit(solution)/shard_map/ppermute | solution.py:236
  12.0 7.3 %collective-permute-start.3 = (bf16[1024,128]{1,0:T(8,128)(2,1)S(1)}, bf16[1024,128]{1,0:T(8,128)(2,1)S(1)}, u32[]{:S(2)}, u32[]{:S(2)}) collective-permute-start(bf16[1024,128]{1,0:T(8,128)(2,1)S(1)} %collective-permute-done.2.refs_0_), channel_id=1, source_target_pairs={{0,4},{1,3},{2,0},{3,7},{4,8},{5,1},{6,2},{7,11},{8,12},{9,5},{10,... | collective-permute-start | bytes 786440 | tf_op jit(solution)/shard_map/ppermute | solution.py:236
  19.3 7.3 %collective-permute-start.12 = (bf16[64,2048]{1,0:T(8,128)(2,1)S(1)}, bf16[64,2048]{1,0:T(8,128)(2,1)S(1)}, u32[]{:S(2)}, u32[]{:S(2)}) collective-permute-start(bf16[64,2048]{1,0:T(8,128)(2,1)S(1)} %convert_element_type.55), channel_id=1, source_target_pairs={{0,4},{1,3},{2,0},{3,7},{4,8},{5,1},{6,2},{7,11},{8,12},{9,5},{10,... | collective-permute-start | bytes 786440 | tf_op jit(solution)/shard_map/ppermute | solution.py:257
  20.9 7.6 %collective-permute-start.11 = (bf16[64,2048]{1,0:T(8,128)(2,1)S(1)}, bf16[64,2048]{1,0:T(8,128)(2,1)S(1)}, u32[]{:S(2)}, u32[]{:S(2)}) collective-permute-start(bf16[64,2048]{1,0:T(8,128)(2,1)S(1)} %convert_element_type.54), channel_id=1, source_target_pairs={{0,4},{1,3},{2,0},{3,7},{4,8},{5,1},{6,2},{7,11},{8,12},{9,5},{10,... | collective-permute-start | bytes 786440 | tf_op jit(solution)/shard_map/ppermute | solution.py:257
  22.6 11.7 %collective-permute-start.6 = (bf16[2080,128]{1,0:T(8,128)(2,1)S(1)}, bf16[2080,128]{1,0:T(8,128)(2,1)S(1)}, u32[]{:S(2)}, u32[]{:S(2)}) collective-permute-start(bf16[2080,128]{1,0:T(8,128)(2,1)S(1)} %pad_maximum_fusion), channel_id=1, source_target_pairs={{0,4},{1,3},{2,0},{3,7},{4,8},{5,1},{6,2},{7,11},{8,12},{9,5},{10,... | collective-permute-start | bytes 1597448 | tf_op jit(solution)/shard_map/ppermute | solution.py:236
  28.7 11.2 %collective-permute-start.13 = (bf16[128,2048]{1,0:T(8,128)(2,1)S(1)}, bf16[128,2048]{1,0:T(8,128)(2,1)S(1)}, u32[]{:S(2)}, u32[]{:S(2)}) collective-permute-start(bf16[128,2048]{1,0:T(8,128)(2,1)S(1)} %add_convert_fusion.3), channel_id=1, source_target_pairs={{0,4},{1,3},{2,0},{3,7},{4,8},{5,1},{6,2},{7,11},{8,12},{9,5},{10,... | collective-permute-start | bytes 1572872 | tf_op jit(solution)/shard_map/ppermute | solution.py:257
  34.2 11.3 %collective-permute-start.7 = (bf16[2080,128]{1,0:T(8,128)(2,1)S(1)}, bf16[2080,128]{1,0:T(8,128)(2,1)S(1)}, u32[]{:S(2)}, u32[]{:S(2)}) collective-permute-start(bf16[2080,128]{1,0:T(8,128)(2,1)S(1)} %collective-permute-done.6.refs_0_), channel_id=1, source_target_pairs={{0,4},{1,3},{2,0},{3,7},{4,8},{5,1},{6,2},{7,11},{8,12},{9,5},{10,... | collective-permute-start | bytes 1597448 | tf_op jit(solution)/shard_map/ppermute | solution.py:236
  40.0 11.2 %collective-permute-start.14 = (bf16[128,2048]{1,0:T(8,128)(2,1)S(1)}, bf16[128,2048]{1,0:T(8,128)(2,1)S(1)}, u32[]{:S(2)}, u32[]{:S(2)}) collective-permute-start(bf16[128,2048]{1,0:T(8,128)(2,1)S(1)} %add_convert_fusion.2), channel_id=1, source_target_pairs={{0,4},{1,3},{2,0},{3,7},{4,8},{5,1},{6,2},{7,11},{8,12},{9,5},{10,... | collective-permute-start | bytes 1572872 | tf_op jit(solution)/shard_map/ppermute | solution.py:257
  45.6 11.3 %collective-permute-start.8 = (bf16[2080,128]{1,0:T(8,128)(2,1)S(1)}, bf16[2080,128]{1,0:T(8,128)(2,1)S(1)}, u32[]{:S(2)}, u32[]{:S(2)}) collective-permute-start(bf16[2080,128]{1,0:T(8,128)(2,1)S(1)} %collective-permute-done.7.refs_0_), channel_id=1, source_target_pairs={{0,4},{1,3},{2,0},{3,7},{4,8},{5,1},{6,2},{7,11},{8,12},{9,5},{10,... | collective-permute-start | bytes 1597448 | tf_op jit(solution)/shard_map/ppermute | solution.py:236
  51.3 11.2 %collective-permute-start.15 = (bf16[128,2048]{1,0:T(8,128)(2,1)S(1)}, bf16[128,2048]{1,0:T(8,128)(2,1)S(1)}, u32[]{:S(2)}, u32[]{:S(2)}) collective-permute-start(bf16[128,2048]{1,0:T(8,128)(2,1)S(1)} %add_convert_fusion.1), channel_id=1, source_target_pairs={{0,4},{1,3},{2,0},{3,7},{4,8},{5,1},{6,2},{7,11},{8,12},{9,5},{10,... | collective-permute-start | bytes 1572872 | tf_op jit(solution)/shard_map/ppermute | solution.py:257
  56.9 11.3 %collective-permute-start.9 = (bf16[2080,128]{1,0:T(8,128)(2,1)S(1)}, bf16[2080,128]{1,0:T(8,128)(2,1)S(1)}, u32[]{:S(2)}, u32[]{:S(2)}) collective-permute-start(bf16[2080,128]{1,0:T(8,128)(2,1)S(1)} %collective-permute-done.8.refs_0_), channel_id=1, source_target_pairs={{0,4},{1,3},{2,0},{3,7},{4,8},{5,1},{6,2},{7,11},{8,12},{9,5},{10,... | collective-permute-start | bytes 1597448 | tf_op jit(solution)/shard_map/ppermute | solution.py:236
  62.6 11.2 %collective-permute-start.16 = (bf16[128,2048]{1,0:T(8,128)(2,1)S(1)}, bf16[128,2048]{1,0:T(8,128)(2,1)S(1)}, u32[]{:S(2)}, u32[]{:S(2)}) collective-permute-start(bf16[128,2048]{1,0:T(8,128)(2,1)S(1)} %add_convert_fusion), channel_id=1, source_target_pairs={{0,4},{1,3},{2,0},{3,7},{4,8},{5,1},{6,2},{7,11},{8,12},{9,5},{10,... | collective-permute-start | bytes 1572872 | tf_op jit(solution)/shard_map/ppermute | solution.py:257
  68.2 14.1 %collective-permute-start.10 = (bf16[2080,128]{1,0:T(8,128)(2,1)S(1)}, bf16[2080,128]{1,0:T(8,128)(2,1)S(1)}, u32[]{:S(2)}, u32[]{:S(2)}) collective-permute-start(bf16[2080,128]{1,0:T(8,128)(2,1)S(1)} %collective-permute-done.9.refs_0_), channel_id=1, source_target_pairs={{0,4},{1,3},{2,0},{3,7},{4,8},{5,1},{6,2},{7,11},{8,12},{9,5},{10,... | collective-permute-start | bytes 1597448 | tf_op jit(solution)/shard_map/ppermute | solution.py:236
  73.9 8.4 %collective-permute-start.18 = (bf16[64,2048]{1,0:T(8,128)(2,1)S(1)}, bf16[64,2048]{1,0:T(8,128)(2,1)S(1)}, u32[]{:S(2)}, u32[]{:S(2)}) collective-permute-start(bf16[64,2048]{1,0:T(8,128)(2,1)S(1)} %fusion.1), channel_id=1, source_target_pairs={{0,4},{1,3},{2,0},{3,7},{4,8},{5,1},{6,2},{7,11},{8,12},{9,5},{10,... | collective-permute-start | bytes 786440 | tf_op jit(solution)/shard_map/ppermute | solution.py:257
  75.6 11.0 %collective-permute-start.17 = (bf16[64,2048]{1,0:T(8,128)(2,1)S(1)}, bf16[64,2048]{1,0:T(8,128)(2,1)S(1)}, u32[]{:S(2)}, u32[]{:S(2)}) collective-permute-start(bf16[64,2048]{1,0:T(8,128)(2,1)S(1)} %fusion.2), channel_id=1, source_target_pairs={{0,4},{1,3},{2,0},{3,7},{4,8},{5,1},{6,2},{7,11},{8,12},{9,5},{10,... | collective-permute-start | bytes 786440 | tf_op jit(solution)/shard_map/ppermute | solution.py:257
  85.0 6.4 %collective-permute-start.20 = (bf16[64,2048]{1,0:T(8,128)(2,1)S(1)}, bf16[64,2048]{1,0:T(8,128)(2,1)S(1)}, u32[]{:S(2)}, u32[]{:S(2)}) collective-permute-start(bf16[64,2048]{1,0:T(8,128)(2,1)S(1)} %fusion), channel_id=1, source_target_pairs={{0,4},{1,3},{2,0},{3,7},{4,8},{5,1},{6,2},{7,11},{8,12},{9,5},{10,... | collective-permute-start | bytes 786440 | tf_op jit(solution)/shard_map/ppermute | solution.py:257
  86.7 7.5 %collective-permute-start.19 = (bf16[64,2048]{1,0:T(8,128)(2,1)S(1)}, bf16[64,2048]{1,0:T(8,128)(2,1)S(1)}, u32[]{:S(2)}, u32[]{:S(2)}) collective-permute-start(bf16[64,2048]{1,0:T(8,128)(2,1)S(1)} %fusion.3), channel_id=1, source_target_pairs={{0,4},{1,3},{2,0},{3,7},{4,8},{5,1},{6,2},{7,11},{8,12},{9,5},{10,... | collective-permute-start | bytes 786440 | tf_op jit(solution)/shard_map/ppermute | solution.py:257

commit v2 on v0

--- a/solution.py
+++ b/solution.py
@@ -109,7 +109,7 @@
 
 def serve_rows(width, picks, partner, *refs):
     pieces, refs, out = refs[: -1 - 2 * len(picks)], refs[-1 - 2 * len(picks) : -1], refs[-1]
-    tok_rows, _ = out.shape
+    tok_rows, features = out.shape
     num_experts = len(partner)
     rows = [
         piece[at : at + tok_rows]
@@ -121,7 +121,7 @@
     lanes = lax.broadcasted_iota(jnp.int32, shares.shape, 1)
     me = lax.axis_index("expert")
     other = sum(jnp.where(me == e, partner[e], 0) for e in range(num_experts))
-    total = None
+    experts = []
     for place, which in enumerate(picks):
         gate, down = refs[2 * place], refs[2 * place + 1]
         expert = (me, other)[which]
@@ -129,16 +129,21 @@
         share = jnp.sum(share, axis=1, keepdims=True)
         pre = jnp.dot(rows, gate[...], preferred_element_type=jnp.float32)
         gated, up = pre[:, :width], pre[:, width:]
-        hidden = gated / (1.0 + jnp.exp(-gated)) * up
-        part = lax.dot_general(
-            hidden.astype(jnp.bfloat16),
-            down[...],
-            (((1,), (1,)), ((), ())),
-            preferred_element_type=jnp.float32,
-        )
-        part = share * part.astype(jnp.bfloat16).astype(jnp.float32)
-        total = part if total is None else total + part
-    out[...] = total
+        hidden = (gated / (1.0 + jnp.exp(-gated)) * up).astype(jnp.bfloat16)
+        experts.append((share, hidden, down))
+    columns = 4 * LANES
+    for start in range(0, features, columns):
+        chunk, total = slice(start, min(start + columns, features)), None
+        for share, hidden, down in experts:
+            part = lax.dot_general(
+                hidden,
+                down[chunk],
+                (((1,), (1,)), ((), ())),
+                preferred_element_type=jnp.float32,
+            )
+            part = share * part.astype(jnp.bfloat16).astype(jnp.float32)
+            total = part if total is None else total + part
+        out[:, chunk] = total
 
 
 def finish(at, home, got, *refs):

time: 90.2 us -> 89.7 us (level)
  Pallas kernels: 25.4 us -> 21.3 us
  waiting for transfers between devices: 30.8 us -> 34.7 us
    pallas_call x8, Pallas kernels: 20.4 us -> 16.2 us  [serve(): pl.pallas_call(functools.partial(serve_rows, width, picks, partner), out_...]
    ppermute x9, waiting for transfers between devices: 11.5 us -> 14.9 us  [ring(): total.append(hop(x))]
  transfers between devices with their start and end apart: 20 -> 20, of which waited for: 16 -> 16; matrix products, arithmetic and copies ran while one was open for 1% -> 1% of each run, Pallas kernels for 27% -> 23%
where the time goes in v2:
time: 89.7 us; the launch traced here: 89.5 us
  waiting for transfers between devices  34.7 us (39%)
  starting transfers between devices  32.3 us (36%)
  Pallas kernels  21.3 us (24%)
    ppermute x7, waiting for transfers between devices, ring(): away[at] = hop(x)  18.8 us
    pallas_call x8, Pallas kernels, serve(): pl.pallas_call(functools.partial(serve_rows, width, picks, partner), out_...  16.2 us
    ppermute x9, waiting for transfers between devices, ring(): total.append(hop(x))  14.9 us
    ppermute x9, starting transfers between devices, ring(): total.append(hop(x))  14.5 us
    ppermute x7, starting transfers between devices, ring(): away[at] = hop(x)  12.6 us
    ppermute x2, starting transfers between devices, ring(): away.append(hop(x))  4.68 us
    pallas_call x1, Pallas kernels, ring(): pl.pallas_call(load, out_shape=[jax.ShapeDtypeStruct(w.shape, w.dtype) fo...  2.37 us
  transfers between devices with their start and end apart: 20, of which 16 were waited for; matrix products, arithmetic and copies ran while one was open for 1% of the time, Pallas kernels for 23%

profile of v2, /device:TPU:0, one launch (start us, length us, event | category | flops | bytes accessed | tf_op | source)
XLA Modules:
  0.0 89.5 jit_solution(926683093393019322)
XLA Ops:
  0.0 0.5 collective-permute-start
  0.5 1.2 %pack_rows.1 = (bf16[1024,128]{1,0:T(8,128)(2,1)S(1)}, bf16[1056,128]{1,0:T(8,128)(2,1)S(1)}) custom-call(bf16[128,2048]{1,0:T(8,128)(2,1)} %tokens.1, s32[8,128]{1,0:T(8,128)} %bitcast.8, f32[8,128]{1,0:T(8,128)} %bitcast.9), custom_call_target="tpu_custom_call" | custom-call | tf_op jit(solution)/shard_map/pack_rows/pallas_call | solution.py:175
  1.7 3.1 %collective-permute-start.4 = (bf16[1056,128]{1,0:T(8,128)(2,1)S(1)}, bf16[1056,128]{1,0:T(8,128)(2,1)S(1)}, u32[]{:S(2)}, u32[]{:S(2)}) collective-permute-start(bf16[1056,128]{1,0:T(8,128)(2,1)S(1)} %get-tuple-element.21.refs_1_), channel_id=1, source_target_pairs={{0,4},{1,3},{2,0},{3,7},{4,8},{5,1},{6,2},{7,11},{8,12},{9,5},{10,... | collective-permute-start | bytes 811016 | tf_op jit(solution)/shard_map/ppermute | solution.py:190
  4.8 1.6 %collective-permute-start.2 = (bf16[1024,128]{1,0:T(8,128)(2,1)S(1)}, bf16[1024,128]{1,0:T(8,128)(2,1)S(1)}, u32[]{:S(2)}, u32[]{:S(2)}) collective-permute-start(bf16[1024,128]{1,0:T(8,128)(2,1)S(1)} %get-tuple-element.20.refs_0_), channel_id=1, source_target_pairs={{0,4},{1,3},{2,0},{3,7},{4,8},{5,1},{6,2},{7,11},{8,12},{9,5},{10,... | collective-permute-start | bytes 786440 | tf_op jit(solution)/shard_map/ppermute | solution.py:190
  6.4 2.4 %load.1 = (bf16[2048,768]{1,0:T(8,128)(2,1)S(1)}, bf16[2048,384]{1,0:T(8,128)(2,1)S(1)}) custom-call(bf16[2048,768]{1,0:T(8,128)(2,1)} %bitcast.5, bf16[2048,384]{1,0:T(8,128)(2,1)} %bitcast.7), custom_call_target="tpu_custom_call" | custom-call | tf_op jit(solution)/shard_map/load/pallas_call | solution.py:193
  8.8 0.4 collective-permute-done.4.refs_1_
  9.2 2.1 %collective-permute-start.5 = (bf16[1056,128]{1,0:T(8,128)(2,1)S(1)}, bf16[1056,128]{1,0:T(8,128)(2,1)S(1)}, u32[]{:S(2)}, u32[]{:S(2)}) collective-permute-start(bf16[1056,128]{1,0:T(8,128)(2,1)S(1)} %collective-permute-done.4.refs_1_), channel_id=1, source_target_pairs={{0,4},{1,3},{2,0},{3,7},{4,8},{5,1},{6,2},{7,11},{8,12},{9,5},{10,... | collective-permute-start | bytes 811016 | tf_op jit(solution)/shard_map/ppermute | solution.py:224
  11.3 0.7 collective-permute-done.2.refs_0_
  12.0 2.1 %collective-permute-start.3 = (bf16[1024,128]{1,0:T(8,128)(2,1)S(1)}, bf16[1024,128]{1,0:T(8,128)(2,1)S(1)}, u32[]{:S(2)}, u32[]{:S(2)}) collective-permute-start(bf16[1024,128]{1,0:T(8,128)(2,1)S(1)} %collective-permute-done.2.refs_0_), channel_id=1, source_target_pairs={{0,4},{1,3},{2,0},{3,7},{4,8},{5,1},{6,2},{7,11},{8,12},{9,5},{10,... | collective-permute-start | bytes 786440 | tf_op jit(solution)/shard_map/ppermute | solution.py:224
  14.1 2.1 %serve_rows.9 = f32[128,2048]{1,0:T(8,128)S(1)} custom-call(bf16[1024,128]{1,0:T(8,128)(2,1)S(1)} %collective-permute-done.2.refs_0_, bf16[1056,128]{1,0:T(8,128)(2,1)S(1)} %collective-permute-done.4.refs_1_, bf16[2048,768]{1,0:T(8,128)(2,1)S(1)} %get-tuple-element.22.refs_2_.refs_1_, bf16[2048,384]{1,0:T(8,128)(2,1)S(1)} %get-tuple-element.23.refs_3_.refs_2_, ...), custom_call_target="tpu_custom_call" | custom-call | tf_op jit(solution)/shard_map/serve_rows/pallas_call | solution.py:205
  16.2 1.6 %collective-permute-start.11 = (bf16[128,2048]{1,0:T(8,128)(2,1)S(1)}, bf16[128,2048]{1,0:T(8,128)(2,1)S(1)}, u32[]{:S(2)}, u32[]{:S(2)}) collective-permute-start(bf16[128,2048]{1,0:T(8,128)(2,1)S(1)} %convert_element_type.51), channel_id=1, source_target_pairs={{0,4},{1,3},{2,0},{3,7},{4,8},{5,1},{6,2},{7,11},{8,12},{9,5},{10,... | collective-permute-start | bytes 1572872 | tf_op jit(solution)/shard_map/ppermute | solution.py:240
  17.9 0.6 collective-permute-done.3.refs_0_
  18.5 2.2 %collective-permute-start.6 = (bf16[2080,128]{1,0:T(8,128)(2,1)S(1)}, bf16[2080,128]{1,0:T(8,128)(2,1)S(1)}, u32[]{:S(2)}, u32[]{:S(2)}) collective-permute-start(bf16[2080,128]{1,0:T(8,128)(2,1)S(1)} %pad_maximum_fusion), channel_id=1, source_target_pairs={{0,4},{1,3},{2,0},{3,7},{4,8},{5,1},{6,2},{7,11},{8,12},{9,5},{10,... | collective-permute-start | bytes 1597448 | tf_op jit(solution)/shard_map/ppermute | solution.py:224
  20.6 2.1 %serve_rows.10 = f32[128,2048]{1,0:T(8,128)S(1)} custom-call(bf16[1024,128]{1,0:T(8,128)(2,1)S(1)} %collective-permute-done.3.refs_0_, bf16[1056,128]{1,0:T(8,128)(2,1)S(1)} %collective-permute-done.5.refs_1_, bf16[2048,768]{1,0:T(8,128)(2,1)S(1)} %get-tuple-element.22.refs_2_.refs_1_, bf16[2048,384]{1,0:T(8,128)(2,1)S(1)} %get-tuple-element.23.refs_3_.refs_2_, ...), custom_call_target="tpu_custom_call" | custom-call | tf_op jit(solution)/shard_map/serve_rows/pallas_call | solution.py:205
  22.7 2.8 %collective-permute-done.11 = bf16[128,2048]{1,0:T(8,128)(2,1)S(1)} collective-permute-done((bf16[128,2048]{1,0:T(8,128)(2,1)S(1)}, bf16[128,2048]{1,0:T(8,128)(2,1)S(1)}, u32[]{:S(2)}, u32[]{:S(2)}) %collective-permute-start.11) | collective-permute-done | bytes 524320 | tf_op jit(solution)/shard_map/ppermute | solution.py:240
  25.5 0.1 add_convert_fusion.3
  25.6 1.6 %collective-permute-start.12 = (bf16[128,2048]{1,0:T(8,128)(2,1)S(1)}, bf16[128,2048]{1,0:T(8,128)(2,1)S(1)}, u32[]{:S(2)}, u32[]{:S(2)}) collective-permute-start(bf16[128,2048]{1,0:T(8,128)(2,1)S(1)} %add_convert_fusion.3), channel_id=1, source_target_pairs={{0,4},{1,3},{2,0},{3,7},{4,8},{5,1},{6,2},{7,11},{8,12},{9,5},{10,... | collective-permute-start | bytes 1572872 | tf_op jit(solution)/shard_map/ppermute | solution.py:240
  27.2 4.0 %collective-permute-done.6.refs_0_ = bf16[2080,128]{1,0:T(8,128)(2,1)S(1)} collective-permute-done((bf16[2080,128]{1,0:T(8,128)(2,1)S(1)}, bf16[2080,128]{1,0:T(8,128)(2,1)S(1)}, u32[]{:S(2)}, u32[]{:S(2)}) %collective-permute-start.6) | collective-permute-done | bytes 532512 | tf_op jit(solution)/shard_map/ppermute | solution.py:224
  31.2 1.6 %collective-permute-start.7 = (bf16[2080,128]{1,0:T(8,128)(2,1)S(1)}, bf16[2080,128]{1,0:T(8,128)(2,1)S(1)}, u32[]{:S(2)}, u32[]{:S(2)}) collective-permute-start(bf16[2080,128]{1,0:T(8,128)(2,1)S(1)} %collective-permute-done.6.refs_0_), channel_id=1, source_target_pairs={{0,4},{1,3},{2,0},{3,7},{4,8},{5,1},{6,2},{7,11},{8,12},{9,5},{10,... | collective-permute-start | bytes 1597448 | tf_op jit(solution)/shard_map/ppermute | solution.py:224
  32.7 2.0 %serve_rows.11 = f32[128,2048]{1,0:T(8,128)S(1)} custom-call(bf16[2080,128]{1,0:T(8,128)(2,1)S(1)} %collective-permute-done.6.refs_0_, bf16[2048,768]{1,0:T(8,128)(2,1)S(1)} %get-tuple-element.22.refs_2_.refs_1_, bf16[2048,384]{1,0:T(8,128)(2,1)S(1)} %get-tuple-element.23.refs_3_.refs_2_, bf16[2048,768]{1,0:T(8,128)(2,1)S(1)} %collective-permute-done.refs_4_.refs_3_, ...), custom_call_target="tpu_custom_call" | custom-call | tf_op jit(solution)/shard_map/serve_rows/pallas_call | solution.py:205
  34.7 2.1 %collective-permute-done.12 = bf16[128,2048]{1,0:T(8,128)(2,1)S(1)} collective-permute-done((bf16[128,2048]{1,0:T(8,128)(2,1)S(1)}, bf16[128,2048]{1,0:T(8,128)(2,1)S(1)}, u32[]{:S(2)}, u32[]{:S(2)}) %collective-permute-start.12) | collective-permute-done | bytes 524320 | tf_op jit(solution)/shard_map/ppermute | solution.py:240
  36.9 1.6 %collective-permute-start.13 = (bf16[128,2048]{1,0:T(8,128)(2,1)S(1)}, bf16[128,2048]{1,0:T(8,128)(2,1)S(1)}, u32[]{:S(2)}, u32[]{:S(2)}) collective-permute-start(bf16[128,2048]{1,0:T(8,128)(2,1)S(1)} %add_convert_fusion.2), channel_id=1, source_target_pairs={{0,4},{1,3},{2,0},{3,7},{4,8},{5,1},{6,2},{7,11},{8,12},{9,5},{10,... | collective-permute-start | bytes 1572872 | tf_op jit(solution)/shard_map/ppermute | solution.py:240
  38.5 4.0 %collective-permute-done.7.refs_0_ = bf16[2080,128]{1,0:T(8,128)(2,1)S(1)} collective-permute-done((bf16[2080,128]{1,0:T(8,128)(2,1)S(1)}, bf16[2080,128]{1,0:T(8,128)(2,1)S(1)}, u32[]{:S(2)}, u32[]{:S(2)}) %collective-permute-start.7) | collective-permute-done | bytes 532512 | tf_op jit(solution)/shard_map/ppermute | solution.py:224
  42.5 1.6 %collective-permute-start.8 = (bf16[2080,128]{1,0:T(8,128)(2,1)S(1)}, bf16[2080,128]{1,0:T(8,128)(2,1)S(1)}, u32[]{:S(2)}, u32[]{:S(2)}) collective-permute-start(bf16[2080,128]{1,0:T(8,128)(2,1)S(1)} %collective-permute-done.7.refs_0_), channel_id=1, source_target_pairs={{0,4},{1,3},{2,0},{3,7},{4,8},{5,1},{6,2},{7,11},{8,12},{9,5},{10,... | collective-permute-start | bytes 1597448 | tf_op jit(solution)/shard_map/ppermute | solution.py:224
  44.1 2.1 %serve_rows.12 = f32[128,2048]{1,0:T(8,128)S(1)} custom-call(bf16[2080,128]{1,0:T(8,128)(2,1)S(1)} %collective-permute-done.7.refs_0_, bf16[2048,768]{1,0:T(8,128)(2,1)S(1)} %get-tuple-element.22.refs_2_.refs_1_, bf16[2048,384]{1,0:T(8,128)(2,1)S(1)} %get-tuple-element.23.refs_3_.refs_2_, bf16[2048,768]{1,0:T(8,128)(2,1)S(1)} %collective-permute-done.refs_4_.refs_3_, ...), custom_call_target="tpu_custom_call" | custom-call | tf_op jit(solution)/shard_map/serve_rows/pallas_call | solution.py:205
  46.1 2.0 %collective-permute-done.13 = bf16[128,2048]{1,0:T(8,128)(2,1)S(1)} collective-permute-done((bf16[128,2048]{1,0:T(8,128)(2,1)S(1)}, bf16[128,2048]{1,0:T(8,128)(2,1)S(1)}, u32[]{:S(2)}, u32[]{:S(2)}) %collective-permute-start.13) | collective-permute-done | bytes 524320 | tf_op jit(solution)/shard_map/ppermute | solution.py:240
  48.2 1.6 %collective-permute-start.14 = (bf16[128,2048]{1,0:T(8,128)(2,1)S(1)}, bf16[128,2048]{1,0:T(8,128)(2,1)S(1)}, u32[]{:S(2)}, u32[]{:S(2)}) collective-permute-start(bf16[128,2048]{1,0:T(8,128)(2,1)S(1)} %add_convert_fusion.1), channel_id=1, source_target_pairs={{0,4},{1,3},{2,0},{3,7},{4,8},{5,1},{6,2},{7,11},{8,12},{9,5},{10,... | collective-permute-start | bytes 1572872 | tf_op jit(solution)/shard_map/ppermute | solution.py:240
  49.8 4.0 %collective-permute-done.8.refs_0_ = bf16[2080,128]{1,0:T(8,128)(2,1)S(1)} collective-permute-done((bf16[2080,128]{1,0:T(8,128)(2,1)S(1)}, bf16[2080,128]{1,0:T(8,128)(2,1)S(1)}, u32[]{:S(2)}, u32[]{:S(2)}) %collective-permute-start.8) | collective-permute-done | bytes 532512 | tf_op jit(solution)/shard_map/ppermute | solution.py:224
  53.8 1.6 %collective-permute-start.9 = (bf16[2080,128]{1,0:T(8,128)(2,1)S(1)}, bf16[2080,128]{1,0:T(8,128)(2,1)S(1)}, u32[]{:S(2)}, u32[]{:S(2)}) collective-permute-start(bf16[2080,128]{1,0:T(8,128)(2,1)S(1)} %collective-permute-done.8.refs_0_), channel_id=1, source_target_pairs={{0,4},{1,3},{2,0},{3,7},{4,8},{5,1},{6,2},{7,11},{8,12},{9,5},{10,... | collective-permute-start | bytes 1597448 | tf_op jit(solution)/shard_map/ppermute | solution.py:224
  55.4 2.0 %serve_rows.13 = f32[128,2048]{1,0:T(8,128)S(1)} custom-call(bf16[2080,128]{1,0:T(8,128)(2,1)S(1)} %collective-permute-done.8.refs_0_, bf16[2048,768]{1,0:T(8,128)(2,1)S(1)} %get-tuple-element.22.refs_2_.refs_1_, bf16[2048,384]{1,0:T(8,128)(2,1)S(1)} %get-tuple-element.23.refs_3_.refs_2_, bf16[2048,768]{1,0:T(8,128)(2,1)S(1)} %collective-permute-done.refs_4_.refs_3_, ...), custom_call_target="tpu_custom_call" | custom-call | tf_op jit(solution)/shard_map/serve_rows/pallas_call | solution.py:205
  57.4 2.1 %collective-permute-done.14 = bf16[128,2048]{1,0:T(8,128)(2,1)S(1)} collective-permute-done((bf16[128,2048]{1,0:T(8,128)(2,1)S(1)}, bf16[128,2048]{1,0:T(8,128)(2,1)S(1)}, u32[]{:S(2)}, u32[]{:S(2)}) %collective-permute-start.14) | collective-permute-done | bytes 524320 | tf_op jit(solution)/shard_map/ppermute | solution.py:240
  59.5 1.6 %collective-permute-start.15 = (bf16[128,2048]{1,0:T(8,128)(2,1)S(1)}, bf16[128,2048]{1,0:T(8,128)(2,1)S(1)}, u32[]{:S(2)}, u32[]{:S(2)}) collective-permute-start(bf16[128,2048]{1,0:T(8,128)(2,1)S(1)} %add_convert_fusion), channel_id=1, source_target_pairs={{0,4},{1,3},{2,0},{3,7},{4,8},{5,1},{6,2},{7,11},{8,12},{9,5},{10,... | collective-permute-start | bytes 1572872 | tf_op jit(solution)/shard_map/ppermute | solution.py:240
  61.2 4.0 %collective-permute-done.9.refs_0_ = bf16[2080,128]{1,0:T(8,128)(2,1)S(1)} collective-permute-done((bf16[2080,128]{1,0:T(8,128)(2,1)S(1)}, bf16[2080,128]{1,0:T(8,128)(2,1)S(1)}, u32[]{:S(2)}, u32[]{:S(2)}) %collective-permute-start.9) | collective-permute-done | bytes 532512 | tf_op jit(solution)/shard_map/ppermute | solution.py:224
  65.1 1.6 %collective-permute-start.10 = (bf16[2080,128]{1,0:T(8,128)(2,1)S(1)}, bf16[2080,128]{1,0:T(8,128)(2,1)S(1)}, u32[]{:S(2)}, u32[]{:S(2)}) collective-permute-start(bf16[2080,128]{1,0:T(8,128)(2,1)S(1)} %collective-permute-done.9.refs_0_), channel_id=1, source_target_pairs={{0,4},{1,3},{2,0},{3,7},{4,8},{5,1},{6,2},{7,11},{8,12},{9,5},{10,... | collective-permute-start | bytes 1597448 | tf_op jit(solution)/shard_map/ppermute | solution.py:224
  66.7 2.0 %serve_rows.14 = f32[128,2048]{1,0:T(8,128)S(1)} custom-call(bf16[2080,128]{1,0:T(8,128)(2,1)S(1)} %collective-permute-done.9.refs_0_, bf16[2048,768]{1,0:T(8,128)(2,1)S(1)} %get-tuple-element.22.refs_2_.refs_1_, bf16[2048,384]{1,0:T(8,128)(2,1)S(1)} %get-tuple-element.23.refs_3_.refs_2_, bf16[2048,768]{1,0:T(8,128)(2,1)S(1)} %collective-permute-done.refs_4_.refs_3_, ...), custom_call_target="tpu_custom_call" | custom-call | tf_op jit(solution)/shard_map/serve_rows/pallas_call | solution.py:205
  68.7 2.1 %collective-permute-done.15 = bf16[128,2048]{1,0:T(8,128)(2,1)S(1)} collective-permute-done((bf16[128,2048]{1,0:T(8,128)(2,1)S(1)}, bf16[128,2048]{1,0:T(8,128)(2,1)S(1)}, u32[]{:S(2)}, u32[]{:S(2)}) %collective-permute-start.15) | collective-permute-done | bytes 524320 | tf_op jit(solution)/shard_map/ppermute | solution.py:240
  70.9 1.6 %collective-permute-start.17 = (bf16[64,2048]{1,0:T(8,128)(2,1)S(1)}, bf16[64,2048]{1,0:T(8,128)(2,1)S(1)}, u32[]{:S(2)}, u32[]{:S(2)}) collective-permute-start(bf16[64,2048]{1,0:T(8,128)(2,1)S(1)} %fusion.1), channel_id=1, source_target_pairs={{0,4},{1,3},{2,0},{3,7},{4,8},{5,1},{6,2},{7,11},{8,12},{9,5},{10,... | collective-permute-start | bytes 786440 | tf_op jit(solution)/shard_map/ppermute | solution.py:240
  72.6 1.6 %collective-permute-start.16 = (bf16[64,2048]{1,0:T(8,128)(2,1)S(1)}, bf16[64,2048]{1,0:T(8,128)(2,1)S(1)}, u32[]{:S(2)}, u32[]{:S(2)}) collective-permute-start(bf16[64,2048]{1,0:T(8,128)(2,1)S(1)} %fusion.2), channel_id=1, source_target_pairs={{0,4},{1,3},{2,0},{3,7},{4,8},{5,1},{6,2},{7,11},{8,12},{9,5},{10,... | collective-permute-start | bytes 786440 | tf_op jit(solution)/shard_map/ppermute | solution.py:240
  74.2 2.3 %collective-permute-done.10.refs_0_ = bf16[2080,128]{1,0:T(8,128)(2,1)S(1)} collective-permute-done((bf16[2080,128]{1,0:T(8,128)(2,1)S(1)}, bf16[2080,128]{1,0:T(8,128)(2,1)S(1)}, u32[]{:S(2)}, u32[]{:S(2)}) %collective-permute-start.10) | collective-permute-done | bytes 532512 | tf_op jit(solution)/shard_map/ppermute | solution.py:224
  76.5 2.0 %serve_rows.15 = f32[128,2048]{1,0:T(8,128)S(1)} custom-call(bf16[2080,128]{1,0:T(8,128)(2,1)S(1)} %collective-permute-done.10.refs_0_, bf16[2048,768]{1,0:T(8,128)(2,1)S(1)} %get-tuple-element.22.refs_2_.refs_1_, bf16[2048,384]{1,0:T(8,128)(2,1)S(1)} %get-tuple-element.23.refs_3_.refs_2_, bf16[2048,768]{1,0:T(8,128)(2,1)S(1)} %collective-permute-done.refs_4_.refs_3_, ...), custom_call_target="tpu_custom_call" | custom-call | tf_op jit(solution)/shard_map/serve_rows/pallas_call | solution.py:205
  78.5 0.8 collective-permute-done.17
  79.3 1.6 %collective-permute-start.19 = (bf16[64,2048]{1,0:T(8,128)(2,1)S(1)}, bf16[64,2048]{1,0:T(8,128)(2,1)S(1)}, u32[]{:S(2)}, u32[]{:S(2)}) collective-permute-start(bf16[64,2048]{1,0:T(8,128)(2,1)S(1)} %fusion), channel_id=1, source_target_pairs={{0,4},{1,3},{2,0},{3,7},{4,8},{5,1},{6,2},{7,11},{8,12},{9,5},{10,... | collective-permute-start | bytes 786440 | tf_op jit(solution)/shard_map/ppermute | solution.py:240
  81.0 1.1 %collective-permute-done.16 = bf16[64,2048]{1,0:T(8,128)(2,1)S(1)} collective-permute-done((bf16[64,2048]{1,0:T(8,128)(2,1)S(1)}, bf16[64,2048]{1,0:T(8,128)(2,1)S(1)}, u32[]{:S(2)}, u32[]{:S(2)}) %collective-permute-start.16) | collective-permute-done | bytes 262176 | tf_op jit(solution)/shard_map/ppermute | solution.py:240
  82.2 1.6 %collective-permute-start.18 = (bf16[64,2048]{1,0:T(8,128)(2,1)S(1)}, bf16[64,2048]{1,0:T(8,128)(2,1)S(1)}, u32[]{:S(2)}, u32[]{:S(2)}) collective-permute-start(bf16[64,2048]{1,0:T(8,128)(2,1)S(1)} %fusion.3), channel_id=1, source_target_pairs={{0,4},{1,3},{2,0},{3,7},{4,8},{5,1},{6,2},{7,11},{8,12},{9,5},{10,... | collective-permute-start | bytes 786440 | tf_op jit(solution)/shard_map/ppermute | solution.py:240
  83.8 2.0 %serve_rows.8.home = f32[128,2048]{1,0:T(8,128)S(1)} custom-call(bf16[1024,128]{1,0:T(8,128)(2,1)S(1)} %get-tuple-element.20.refs_0_, bf16[1056,128]{1,0:T(8,128)(2,1)S(1)} %get-tuple-element.21.refs_1_, bf16[2048,768]{1,0:T(8,128)(2,1)S(1)} %get-tuple-element.22.refs_2_.refs_1_, bf16[2048,384]{1,0:T(8,128)(2,1)S(1)} %get-tuple-element.23.refs_3_.refs_2_, ...), custom_call_target="tpu_custom_call" | custom-call | tf_op jit(solution)/shard_map/serve_rows/pallas_call | solution.py:205
  85.8 0.8 finish.2.refs_0_
  86.6 2.0 %collective-permute-done.18.got = bf16[64,2048]{1,0:T(8,128)(2,1)S(1)} collective-permute-done((bf16[64,2048]{1,0:T(8,128)(2,1)S(1)}, bf16[64,2048]{1,0:T(8,128)(2,1)S(1)}, u32[]{:S(2)}, u32[]{:S(2)}) %collective-permute-start.18) | collective-permute-done | bytes 262176 | tf_op jit(solution)/shard_map/ppermute | solution.py:240
  88.6 0.8 finish.3
  (15 shorter events, 0.7 us)
Async XLA Ops:
  0.0 14.1 %collective-permute-start = (bf16[2048,768]{1,0:T(8,128)(2,1)}, bf16[2048,768]{1,0:T(8,128)(2,1)S(1)}, u32[]{:S(2)}, u32[]{:S(2)}) collective-permute-start(bf16[2048,768]{1,0:T(8,128)(2,1)} %bitcast.4), channel_id=1, source_target_pairs={{0,1},{1,0},{2,3},{3,2},{4,5},{5,4},{6,7},{7,6},{8,9},{9,8},{10,11... | collective-permute-start | bytes 9437192 | tf_op jit(solution)/shard_map/ppermute | solution.py:192
  0.5 13.6 %collective-permute-start.1 = (bf16[2048,384]{1,0:T(8,128)(2,1)}, bf16[2048,384]{1,0:T(8,128)(2,1)S(1)}, u32[]{:S(2)}, u32[]{:S(2)}) collective-permute-start(bf16[2048,384]{1,0:T(8,128)(2,1)} %bitcast.6), channel_id=1, source_target_pairs={{0,1},{1,0},{2,3},{3,2},{4,5},{5,4},{6,7},{7,6},{8,9},{9,8},{10,11... | collective-permute-start | bytes 4718600 | tf_op jit(solution)/shard_map/ppermute | solution.py:192
  1.7 7.5 %collective-permute-start.4 = (bf16[1056,128]{1,0:T(8,128)(2,1)S(1)}, bf16[1056,128]{1,0:T(8,128)(2,1)S(1)}, u32[]{:S(2)}, u32[]{:S(2)}) collective-permute-start(bf16[1056,128]{1,0:T(8,128)(2,1)S(1)} %get-tuple-element.21.refs_1_), channel_id=1, source_target_pairs={{0,4},{1,3},{2,0},{3,7},{4,8},{5,1},{6,2},{7,11},{8,12},{9,5},{10,... | collective-permute-start | bytes 811016 | tf_op jit(solution)/shard_map/ppermute | solution.py:190
  4.8 7.2 %collective-permute-start.2 = (bf16[1024,128]{1,0:T(8,128)(2,1)S(1)}, bf16[1024,128]{1,0:T(8,128)(2,1)S(1)}, u32[]{:S(2)}, u32[]{:S(2)}) collective-permute-start(bf16[1024,128]{1,0:T(8,128)(2,1)S(1)} %get-tuple-element.20.refs_0_), channel_id=1, source_target_pairs={{0,4},{1,3},{2,0},{3,7},{4,8},{5,1},{6,2},{7,11},{8,12},{9,5},{10,... | collective-permute-start | bytes 786440 | tf_op jit(solution)/shard_map/ppermute | solution.py:190
  9.2 8.7 %collective-permute-start.5 = (bf16[1056,128]{1,0:T(8,128)(2,1)S(1)}, bf16[1056,128]{1,0:T(8,128)(2,1)S(1)}, u32[]{:S(2)}, u32[]{:S(2)}) collective-permute-start(bf16[1056,128]{1,0:T(8,128)(2,1)S(1)} %collective-permute-done.4.refs_1_), channel_id=1, source_target_pairs={{0,4},{1,3},{2,0},{3,7},{4,8},{5,1},{6,2},{7,11},{8,12},{9,5},{10,... | collective-permute-start | bytes 811016 | tf_op jit(solution)/shard_map/ppermute | solution.py:224
  12.0 6.5 %collective-permute-start.3 = (bf16[1024,128]{1,0:T(8,128)(2,1)S(1)}, bf16[1024,128]{1,0:T(8,128)(2,1)S(1)}, u32[]{:S(2)}, u32[]{:S(2)}) collective-permute-start(bf16[1024,128]{1,0:T(8,128)(2,1)S(1)} %collective-permute-done.2.refs_0_), channel_id=1, source_target_pairs={{0,4},{1,3},{2,0},{3,7},{4,8},{5,1},{6,2},{7,11},{8,12},{9,5},{10,... | collective-permute-start | bytes 786440 | tf_op jit(solution)/shard_map/ppermute | solution.py:224
  16.2 9.2 %collective-permute-start.11 = (bf16[128,2048]{1,0:T(8,128)(2,1)S(1)}, bf16[128,2048]{1,0:T(8,128)(2,1)S(1)}, u32[]{:S(2)}, u32[]{:S(2)}) collective-permute-start(bf16[128,2048]{1,0:T(8,128)(2,1)S(1)} %convert_element_type.51), channel_id=1, source_target_pairs={{0,4},{1,3},{2,0},{3,7},{4,8},{5,1},{6,2},{7,11},{8,12},{9,5},{10,... | collective-permute-start | bytes 1572872 | tf_op jit(solution)/shard_map/ppermute | solution.py:240
  18.5 12.7 %collective-permute-start.6 = (bf16[2080,128]{1,0:T(8,128)(2,1)S(1)}, bf16[2080,128]{1,0:T(8,128)(2,1)S(1)}, u32[]{:S(2)}, u32[]{:S(2)}) collective-permute-start(bf16[2080,128]{1,0:T(8,128)(2,1)S(1)} %pad_maximum_fusion), channel_id=1, source_target_pairs={{0,4},{1,3},{2,0},{3,7},{4,8},{5,1},{6,2},{7,11},{8,12},{9,5},{10,... | collective-permute-start | bytes 1597448 | tf_op jit(solution)/shard_map/ppermute | solution.py:224
  25.6 11.2 %collective-permute-start.12 = (bf16[128,2048]{1,0:T(8,128)(2,1)S(1)}, bf16[128,2048]{1,0:T(8,128)(2,1)S(1)}, u32[]{:S(2)}, u32[]{:S(2)}) collective-permute-start(bf16[128,2048]{1,0:T(8,128)(2,1)S(1)} %add_convert_fusion.3), channel_id=1, source_target_pairs={{0,4},{1,3},{2,0},{3,7},{4,8},{5,1},{6,2},{7,11},{8,12},{9,5},{10,... | collective-permute-start | bytes 1572872 | tf_op jit(solution)/shard_map/ppermute | solution.py:240
  31.2 11.3 %collective-permute-start.7 = (bf16[2080,128]{1,0:T(8,128)(2,1)S(1)}, bf16[2080,128]{1,0:T(8,128)(2,1)S(1)}, u32[]{:S(2)}, u32[]{:S(2)}) collective-permute-start(bf16[2080,128]{1,0:T(8,128)(2,1)S(1)} %collective-permute-done.6.refs_0_), channel_id=1, source_target_pairs={{0,4},{1,3},{2,0},{3,7},{4,8},{5,1},{6,2},{7,11},{8,12},{9,5},{10,... | collective-permute-start | bytes 1597448 | tf_op jit(solution)/shard_map/ppermute | solution.py:224
  36.9 11.2 %collective-permute-start.13 = (bf16[128,2048]{1,0:T(8,128)(2,1)S(1)}, bf16[128,2048]{1,0:T(8,128)(2,1)S(1)}, u32[]{:S(2)}, u32[]{:S(2)}) collective-permute-start(bf16[128,2048]{1,0:T(8,128)(2,1)S(1)} %add_convert_fusion.2), channel_id=1, source_target_pairs={{0,4},{1,3},{2,0},{3,7},{4,8},{5,1},{6,2},{7,11},{8,12},{9,5},{10,... | collective-permute-start | bytes 1572872 | tf_op jit(solution)/shard_map/ppermute | solution.py:240
  42.5 11.3 %collective-permute-start.8 = (bf16[2080,128]{1,0:T(8,128)(2,1)S(1)}, bf16[2080,128]{1,0:T(8,128)(2,1)S(1)}, u32[]{:S(2)}, u32[]{:S(2)}) collective-permute-start(bf16[2080,128]{1,0:T(8,128)(2,1)S(1)} %collective-permute-done.7.refs_0_), channel_id=1, source_target_pairs={{0,4},{1,3},{2,0},{3,7},{4,8},{5,1},{6,2},{7,11},{8,12},{9,5},{10,... | collective-permute-start | bytes 1597448 | tf_op jit(solution)/shard_map/ppermute | solution.py:224
  48.2 11.2 %collective-permute-start.14 = (bf16[128,2048]{1,0:T(8,128)(2,1)S(1)}, bf16[128,2048]{1,0:T(8,128)(2,1)S(1)}, u32[]{:S(2)}, u32[]{:S(2)}) collective-permute-start(bf16[128,2048]{1,0:T(8,128)(2,1)S(1)} %add_convert_fusion.1), channel_id=1, source_target_pairs={{0,4},{1,3},{2,0},{3,7},{4,8},{5,1},{6,2},{7,11},{8,12},{9,5},{10,... | collective-permute-start | bytes 1572872 | tf_op jit(solution)/shard_map/ppermute | solution.py:240
  53.8 11.3 %collective-permute-start.9 = (bf16[2080,128]{1,0:T(8,128)(2,1)S(1)}, bf16[2080,128]{1,0:T(8,128)(2,1)S(1)}, u32[]{:S(2)}, u32[]{:S(2)}) collective-permute-start(bf16[2080,128]{1,0:T(8,128)(2,1)S(1)} %collective-permute-done.8.refs_0_), channel_id=1, source_target_pairs={{0,4},{1,3},{2,0},{3,7},{4,8},{5,1},{6,2},{7,11},{8,12},{9,5},{10,... | collective-permute-start | bytes 1597448 | tf_op jit(solution)/shard_map/ppermute | solution.py:224
  59.5 11.2 %collective-permute-start.15 = (bf16[128,2048]{1,0:T(8,128)(2,1)S(1)}, bf16[128,2048]{1,0:T(8,128)(2,1)S(1)}, u32[]{:S(2)}, u32[]{:S(2)}) collective-permute-start(bf16[128,2048]{1,0:T(8,128)(2,1)S(1)} %add_convert_fusion), channel_id=1, source_target_pairs={{0,4},{1,3},{2,0},{3,7},{4,8},{5,1},{6,2},{7,11},{8,12},{9,5},{10,... | collective-permute-start | bytes 1572872 | tf_op jit(solution)/shard_map/ppermute | solution.py:240
  65.1 11.3 %collective-permute-start.10 = (bf16[2080,128]{1,0:T(8,128)(2,1)S(1)}, bf16[2080,128]{1,0:T(8,128)(2,1)S(1)}, u32[]{:S(2)}, u32[]{:S(2)}) collective-permute-start(bf16[2080,128]{1,0:T(8,128)(2,1)S(1)} %collective-permute-done.9.refs_0_), channel_id=1, source_target_pairs={{0,4},{1,3},{2,0},{3,7},{4,8},{5,1},{6,2},{7,11},{8,12},{9,5},{10,... | collective-permute-start | bytes 1597448 | tf_op jit(solution)/shard_map/ppermute | solution.py:224
  70.9 8.4 %collective-permute-start.17 = (bf16[64,2048]{1,0:T(8,128)(2,1)S(1)}, bf16[64,2048]{1,0:T(8,128)(2,1)S(1)}, u32[]{:S(2)}, u32[]{:S(2)}) collective-permute-start(bf16[64,2048]{1,0:T(8,128)(2,1)S(1)} %fusion.1), channel_id=1, source_target_pairs={{0,4},{1,3},{2,0},{3,7},{4,8},{5,1},{6,2},{7,11},{8,12},{9,5},{10,... | collective-permute-start | bytes 786440 | tf_op jit(solution)/shard_map/ppermute | solution.py:240
  72.6 9.5 %collective-permute-start.16 = (bf16[64,2048]{1,0:T(8,128)(2,1)S(1)}, bf16[64,2048]{1,0:T(8,128)(2,1)S(1)}, u32[]{:S(2)}, u32[]{:S(2)}) collective-permute-start(bf16[64,2048]{1,0:T(8,128)(2,1)S(1)} %fusion.2), channel_id=1, source_target_pairs={{0,4},{1,3},{2,0},{3,7},{4,8},{5,1},{6,2},{7,11},{8,12},{9,5},{10,... | collective-permute-start | bytes 786440 | tf_op jit(solution)/shard_map/ppermute | solution.py:240
  79.3 6.4 %collective-permute-start.19 = (bf16[64,2048]{1,0:T(8,128)(2,1)S(1)}, bf16[64,2048]{1,0:T(8,128)(2,1)S(1)}, u32[]{:S(2)}, u32[]{:S(2)}) collective-permute-start(bf16[64,2048]{1,0:T(8,128)(2,1)S(1)} %fusion), channel_id=1, source_target_pairs={{0,4},{1,3},{2,0},{3,7},{4,8},{5,1},{6,2},{7,11},{8,12},{9,5},{10,... | collective-permute-start | bytes 786440 | tf_op jit(solution)/shard_map/ppermute | solution.py:240
  82.2 6.4 %collective-permute-start.18 = (bf16[64,2048]{1,0:T(8,128)(2,1)S(1)}, bf16[64,2048]{1,0:T(8,128)(2,1)S(1)}, u32[]{:S(2)}, u32[]{:S(2)}) collective-permute-start(bf16[64,2048]{1,0:T(8,128)(2,1)S(1)} %fusion.3), channel_id=1, source_target_pairs={{0,4},{1,3},{2,0},{3,7},{4,8},{5,1},{6,2},{7,11},{8,12},{9,5},{10,... | collective-permute-start | bytes 786440 | tf_op jit(solution)/shard_map/ppermute | solution.py:240

commit v3 on v2

--- a/solution.py
+++ b/solution.py
@@ -70,19 +70,29 @@
 LANES = 128
 
 
-def pack_rows(num_experts, tokens, ids_far, weights_far, out_a, out_b, ids, weights, done):
-    outs = (out_a, out_b)
-    tok_rows, features = tokens.shape
-    half = features // 2
-    pairs = [(ids_far, ids), (weights_far, weights)]
-    for start in range(0, features, LANES):
-        at = start % half // LANES * tok_rows
-        pairs.append(
-            (tokens.at[:, start : start + LANES], outs[start // half].at[at : at + tok_rows])
-        )
+def start_copies(pairs, done):
     copies = [pltpu.make_async_copy(a, b, done.at[i]) for i, (a, b) in enumerate(pairs)]
     for copy in copies:
         copy.start()
+    return copies
+
+
+def column_blocks(tokens, start, out):
+    tok_rows = tokens.shape[0]
+    for at in range(0, out.shape[0] - tok_rows + 1, tok_rows):
+        lane = start + at // tok_rows * LANES
+        yield tokens.at[:, lane : lane + LANES], out.at[at : at + tok_rows]
+
+
+def pack_rows(tokens, out, done):
+    for copy in start_copies(column_blocks(tokens, 0, out), done):
+        copy.wait()
+
+
+def pack_shares(num_experts, tokens, ids_far, weights_far, out, ids, weights, done):
+    tok_rows, features = tokens.shape
+    pairs = [(ids_far, ids), (weights_far, weights)]
+    copies = start_copies([*pairs, *column_blocks(tokens, features // 2, out)], done)
     for copy in copies[:2]:
         copy.wait()
     place = lax.broadcasted_iota(jnp.int32, (num_experts, tok_rows), 0)
@@ -92,7 +102,7 @@
         share += jnp.where(named, weights[choice : choice + 1], 0.0)
     high = share.astype(jnp.bfloat16).astype(jnp.float32)
     both = jnp.concatenate([high, share - high], axis=0)
-    out_b[half // LANES * tok_rows :] = both.astype(jnp.bfloat16)
+    out[-2 * num_experts :] = both.astype(jnp.bfloat16)
     for copy in copies[2:]:
         copy.wait()
 
@@ -105,6 +115,22 @@
         copy.start()
     for copy in copies:
         copy.wait()
+
+
+def turn_back(places, held, own, mine, rest):
+    some = mine.shape[0]
+    me = lax.axis_index("expert")
+    place = sum(jnp.where(me == e, place, 0) for e, place in enumerate(places))
+
+    @pl.when(place == 0)
+    def _():
+        mine[...] = own[:some]
+
+    @pl.when(place != 0)
+    def _():
+        mine[...] = held[:some]
+
+    rest[...] = held[some:]
 
 
 def serve_rows(width, picks, partner, *refs):
@@ -161,30 +187,47 @@
     count = len(stops)
     partner = [0] * num_experts
     onward = [0] * num_experts
+    back = [0] * num_experts
+    places = [0] * num_experts
     for s in range(count):
         for place, turn in ((0, 1), (1, -1)):
             partner[stops[s][place]] = stops[s][1 - place]
             onward[stops[s][place]] = stops[(s + turn) % count][place]
+            back[stops[s][place]] = stops[(s - 1) % count][place]
+            places[stops[s][place]] = place
     hop = functools.partial(lax.ppermute, axis_name="expert", perm=list(enumerate(onward)))
     swap = functools.partial(lax.ppermute, axis_name="expert", perm=list(enumerate(partner)))
     whole = pl.BlockSpec(memory_space=pltpu.VMEM)
 
+    far = pl.BlockSpec(memory_space=pltpu.HBM)
     given = (tokens, expert_ids.T, route_weights.T)
     given = [pltpu.with_memory_space_constraint(x, pltpu.HBM) for x in given]
     half = features // 2 // LANES * tok_rows
-    packed = pl.pallas_call(
-        functools.partial(pack_rows, num_experts),
-        out_shape=[
-            jax.ShapeDtypeStruct((rows, LANES), jnp.bfloat16)
-            for rows in (half, half + 2 * num_experts)
-        ],
-        in_specs=[pl.BlockSpec(memory_space=pltpu.HBM)] * 3,
-        out_specs=[whole] * 2,
-        scratch_shapes=[pltpu.VMEM(x.shape, x.dtype) for x in given[1:]]
-        + [pltpu.SemaphoreType.DMA((2 + features // LANES,))],
-        compiler_params=pltpu.CompilerParams(vmem_limit_bytes=8 * 1024 * 1024),
-        name="pack_rows",
-    )(*given)
+    blocks = half // tok_rows
+    small = pltpu.CompilerParams(vmem_limit_bytes=4 * 1024 * 1024)
+    packed = [
+        pl.pallas_call(
+            pack_rows,
+            out_shape=jax.ShapeDtypeStruct((half, LANES), jnp.bfloat16),
+            in_specs=[far],
+            out_specs=whole,
+            scratch_shapes=[pltpu.SemaphoreType.DMA((blocks,))],
+            compiler_params=small,
+            name="pack_rows",
+        )(given[0])
+    ]
+    packed.append(
+        pl.pallas_call(
+            functools.partial(pack_shares, num_experts),
+            out_shape=jax.ShapeDtypeStruct((half + 2 * num_experts, LANES), jnp.bfloat16),
+            in_specs=[far] * 3,
+            out_specs=whole,
+            scratch_shapes=[pltpu.VMEM(x.shape, x.dtype) for x in given[1:]]
+            + [pltpu.SemaphoreType.DMA((2 + blocks,))],
+            compiler_params=small,
+            name="pack_shares",
+        )(*given)
+    )
     away = []
     for x in packed:
         away.append(hop(x))
@@ -215,13 +258,28 @@
         return [lax.optimization_barrier((x, other))[0] for x in arrays]
 
     away = after(away, held)
+    some = features // LANES * 5 // 16 * tok_rows
     total = None
     for step in range(1, count):
         here = list(away)
         if step < count - 1:
             away = away if step == 1 else [jnp.concatenate(away)]
-            for at, x in enumerate(away):
-                away[at] = hop(x)
+            if step == count - 2:
+                mine, rest = pl.pallas_call(
+                    functools.partial(turn_back, places),
+                    out_shape=[
+                        jax.ShapeDtypeStruct((rows, LANES), jnp.bfloat16)
+                        for rows in (some, away[0].shape[0] - some)
+                    ],
+                    in_specs=[whole] * 2,
+                    out_specs=[whole] * 2,
+                    compiler_params=pltpu.CompilerParams(vmem_limit_bytes=2 * 1024 * 1024),
+                    name="turn_back",
+                )(away[0], packed[0])
+                away = [lax.ppermute(mine, "expert", list(enumerate(back))), hop(rest)]
+            else:
+                for at, x in enumerate(away):
+                    away[at] = hop(x)
         more = serve(here, (0, 1))
         away = after(away, more)
         parts = 2 if step >= count - 2 else 1
@@ -270,7 +328,7 @@
     )
 
     stops = chip_cycle(mesh)
-    cycle = mesh.shape["token"] == 1 and {len(s) for s in stops} == {2} and len(stops) > 2
+    cycle = mesh.shape["token"] == 1 and {len(s) for s in stops} == {2} and len(stops) > 4
 
     def per_device(tokens, expert_ids, route_weights, gate_up, down_t):
         fits = cycle and mesh.shape["expert"] <= 4 * expert_ids.shape[1] and gate_up.shape[0] == 1

time: 89.7 us -> 93.6 us (1.043)
  waiting for transfers between devices: 34.7 us -> 38.1 us
    ppermute x0 -> x2, waiting for transfers between devices: none -> 5.45 us  [ring(): away = [lax.ppermute(mine, 'expert', list(enumerate(back))), hop(rest)]]
    ppermute x7 -> x6, starting transfers between devices: 12.6 us -> 9.91 us  [ring(): away[at] = hop(x)]
    ppermute x0 -> x2, starting transfers between devices: none -> 2.08 us  [ring(): away = [lax.ppermute(mine, 'expert', list(enumerate(back))), hop(rest)]]
    ppermute x7 -> x6, waiting for transfers between devices: 18.8 us -> 17 us  [ring(): away[at] = hop(x)]
    pallas_call x1 -> x3, Pallas kernels: 1.19 us -> 2 us  [the longest x1 1.02 us: ring(): pl.pallas_call(functools.partial(pack_shares, num_experts), out_shape=jax...]
  transfers between devices with their start and end apart: 20 -> 21, of which waited for: 16 -> 15; matrix products, arithmetic and copies ran while one was open for 1% -> 1% of each run, Pallas kernels for 23% -> 23%
where the time goes in v3:
time: 93.6 us; the launch traced here: 93.3 us
  waiting for transfers between devices  38.1 us (41%)
  starting transfers between devices  32 us (34%)
  Pallas kernels  22 us (24%)
    ppermute x6, waiting for transfers between devices, ring(): away[at] = hop(x)  17 us
    pallas_call x8, Pallas kernels, serve(): pl.pallas_call(functools.partial(serve_rows, width, picks, partner), out_...  16.1 us
    ppermute x9, waiting for transfers between devices, ring(): total.append(hop(x))  14.9 us
    ppermute x9, starting transfers between devices, ring(): total.append(hop(x))  14.7 us
    ppermute x6, starting transfers between devices, ring(): away[at] = hop(x)  9.91 us
    ppermute x2, waiting for transfers between devices, ring(): away = [lax.ppermute(mine, 'expert', list(enumerate(back))), hop(rest)]  5.45 us
    ppermute x2, starting transfers between devices, ring(): away.append(hop(x))  4.73 us
    pallas_call x1, Pallas kernels, ring(): pl.pallas_call(load, out_shape=[jax.ShapeDtypeStruct(w.shape, w.dtype) fo...  2.37 us
  transfers between devices with their start and end apart: 21, of which 15 were waited for; matrix products, arithmetic and copies ran while one was open for 1% of the time, Pallas kernels for 23%

profile of v3, /device:TPU:0, one launch (start us, length us, event | category | flops | bytes accessed | tf_op | source)
XLA Modules:
  0.0 93.3 jit_solution(2820406331085608993)
XLA Ops:
  0.0 0.5 collective-permute-start
  0.5 1.0 %pack_shares.1.refs_1_ = bf16[1056,128]{1,0:T(8,128)(2,1)S(1)} custom-call(bf16[128,2048]{1,0:T(8,128)(2,1)} %tokens.3, s32[8,128]{1,0:T(8,128)} %bitcast.8, f32[8,128]{1,0:T(8,128)} %bitcast.9), custom_call_target="tpu_custom_call" | custom-call | tf_op jit(solution)/shard_map/pack_shares/pallas_call | solution.py:220
  1.5 3.1 %collective-permute-start.4 = (bf16[1056,128]{1,0:T(8,128)(2,1)S(1)}, bf16[1056,128]{1,0:T(8,128)(2,1)S(1)}, u32[]{:S(2)}, u32[]{:S(2)}) collective-permute-start(bf16[1056,128]{1,0:T(8,128)(2,1)S(1)} %pack_shares.1.refs_1_), channel_id=1, source_target_pairs={{0,4},{1,3},{2,0},{3,7},{4,8},{5,1},{6,2},{7,11},{8,12},{9,5},{10,... | collective-permute-start | bytes 811016 | tf_op jit(solution)/shard_map/ppermute | solution.py:233
  4.6 0.9 %pack_rows.1.refs_0_.own = bf16[1024,128]{1,0:T(8,128)(2,1)S(1)} custom-call(bf16[128,2048]{1,0:T(8,128)(2,1)} %tokens.3), custom_call_target="tpu_custom_call" | custom-call | tf_op jit(solution)/shard_map/pack_rows/pallas_call | solution.py:209
  5.6 1.6 %collective-permute-start.2 = (bf16[1024,128]{1,0:T(8,128)(2,1)S(1)}, bf16[1024,128]{1,0:T(8,128)(2,1)S(1)}, u32[]{:S(2)}, u32[]{:S(2)}) collective-permute-start(bf16[1024,128]{1,0:T(8,128)(2,1)S(1)} %pack_rows.1.refs_0_.own), channel_id=1, source_target_pairs={{0,4},{1,3},{2,0},{3,7},{4,8},{5,1},{6,2},{7,11},{8,12},{9,5},{10,... | collective-permute-start | bytes 786440 | tf_op jit(solution)/shard_map/ppermute | solution.py:233
  7.2 2.4 %load.1 = (bf16[2048,768]{1,0:T(8,128)(2,1)S(1)}, bf16[2048,384]{1,0:T(8,128)(2,1)S(1)}) custom-call(bf16[2048,768]{1,0:T(8,128)(2,1)} %bitcast.5, bf16[2048,384]{1,0:T(8,128)(2,1)} %bitcast.7), custom_call_target="tpu_custom_call" | custom-call | tf_op jit(solution)/shard_map/load/pallas_call | solution.py:236
  9.6 1.6 %collective-permute-start.5 = (bf16[1056,128]{1,0:T(8,128)(2,1)S(1)}, bf16[1056,128]{1,0:T(8,128)(2,1)S(1)}, u32[]{:S(2)}, u32[]{:S(2)}) collective-permute-start(bf16[1056,128]{1,0:T(8,128)(2,1)S(1)} %collective-permute-done.4.refs_1_), channel_id=1, source_target_pairs={{0,4},{1,3},{2,0},{3,7},{4,8},{5,1},{6,2},{7,11},{8,12},{9,5},{10,... | collective-permute-start | bytes 811016 | tf_op jit(solution)/shard_map/ppermute | solution.py:282
  11.2 0.8 collective-permute-done.2.refs_0_
  12.0 1.9 %collective-permute-start.3 = (bf16[1024,128]{1,0:T(8,128)(2,1)S(1)}, bf16[1024,128]{1,0:T(8,128)(2,1)S(1)}, u32[]{:S(2)}, u32[]{:S(2)}) collective-permute-start(bf16[1024,128]{1,0:T(8,128)(2,1)S(1)} %collective-permute-done.2.refs_0_), channel_id=1, source_target_pairs={{0,4},{1,3},{2,0},{3,7},{4,8},{5,1},{6,2},{7,11},{8,12},{9,5},{10,... | collective-permute-start | bytes 786440 | tf_op jit(solution)/shard_map/ppermute | solution.py:282
  13.9 2.0 %serve_rows.9 = f32[128,2048]{1,0:T(8,128)S(1)} custom-call(bf16[1024,128]{1,0:T(8,128)(2,1)S(1)} %collective-permute-done.2.refs_0_, bf16[1056,128]{1,0:T(8,128)(2,1)S(1)} %collective-permute-done.4.refs_1_, bf16[2048,768]{1,0:T(8,128)(2,1)S(1)} %get-tuple-element.21.refs_2_.refs_1_, bf16[2048,384]{1,0:T(8,128)(2,1)S(1)} %get-tuple-element.22.refs_3_.refs_2_, ...), custom_call_target="tpu_custom_call" | custom-call | tf_op jit(solution)/shard_map/serve_rows/pallas_call | solution.py:248
  16.0 1.6 %collective-permute-start.12 = (bf16[128,2048]{1,0:T(8,128)(2,1)S(1)}, bf16[128,2048]{1,0:T(8,128)(2,1)S(1)}, u32[]{:S(2)}, u32[]{:S(2)}) collective-permute-start(bf16[128,2048]{1,0:T(8,128)(2,1)S(1)} %convert_element_type.51), channel_id=1, source_target_pairs={{0,4},{1,3},{2,0},{3,7},{4,8},{5,1},{6,2},{7,11},{8,12},{9,5},{10,... | collective-permute-start | bytes 1572872 | tf_op jit(solution)/shard_map/ppermute | solution.py:298
  17.7 1.3 %collective-permute-done.3.refs_0_ = bf16[1024,128]{1,0:T(8,128)(2,1)S(1)} collective-permute-done((bf16[1024,128]{1,0:T(8,128)(2,1)S(1)}, bf16[1024,128]{1,0:T(8,128)(2,1)S(1)}, u32[]{:S(2)}, u32[]{:S(2)}) %collective-permute-start.3) | collective-permute-done | bytes 262176 | tf_op jit(solution)/shard_map/ppermute | solution.py:282
  19.0 1.6 %collective-permute-start.6 = (bf16[2080,128]{1,0:T(8,128)(2,1)S(1)}, bf16[2080,128]{1,0:T(8,128)(2,1)S(1)}, u32[]{:S(2)}, u32[]{:S(2)}) collective-permute-start(bf16[2080,128]{1,0:T(8,128)(2,1)S(1)} %pad_maximum_fusion), channel_id=1, source_target_pairs={{0,4},{1,3},{2,0},{3,7},{4,8},{5,1},{6,2},{7,11},{8,12},{9,5},{10,... | collective-permute-start | bytes 1597448 | tf_op jit(solution)/shard_map/ppermute | solution.py:282
  20.6 2.0 %serve_rows.10 = f32[128,2048]{1,0:T(8,128)S(1)} custom-call(bf16[1024,128]{1,0:T(8,128)(2,1)S(1)} %collective-permute-done.3.refs_0_, bf16[1056,128]{1,0:T(8,128)(2,1)S(1)} %collective-permute-done.5.refs_1_, bf16[2048,768]{1,0:T(8,128)(2,1)S(1)} %get-tuple-element.21.refs_2_.refs_1_, bf16[2048,384]{1,0:T(8,128)(2,1)S(1)} %get-tuple-element.22.refs_3_.refs_2_, ...), custom_call_target="tpu_custom_call" | custom-call | tf_op jit(solution)/shard_map/serve_rows/pallas_call | solution.py:248
  22.6 2.6 %collective-permute-done.12 = bf16[128,2048]{1,0:T(8,128)(2,1)S(1)} collective-permute-done((bf16[128,2048]{1,0:T(8,128)(2,1)S(1)}, bf16[128,2048]{1,0:T(8,128)(2,1)S(1)}, u32[]{:S(2)}, u32[]{:S(2)}) %collective-permute-start.12) | collective-permute-done | bytes 524320 | tf_op jit(solution)/shard_map/ppermute | solution.py:298
  25.4 1.6 %collective-permute-start.13 = (bf16[128,2048]{1,0:T(8,128)(2,1)S(1)}, bf16[128,2048]{1,0:T(8,128)(2,1)S(1)}, u32[]{:S(2)}, u32[]{:S(2)}) collective-permute-start(bf16[128,2048]{1,0:T(8,128)(2,1)S(1)} %add_convert_fusion.3), channel_id=1, source_target_pairs={{0,4},{1,3},{2,0},{3,7},{4,8},{5,1},{6,2},{7,11},{8,12},{9,5},{10,... | collective-permute-start | bytes 1572872 | tf_op jit(solution)/shard_map/ppermute | solution.py:298
  27.0 3.9 %collective-permute-done.6.refs_0_ = bf16[2080,128]{1,0:T(8,128)(2,1)S(1)} collective-permute-done((bf16[2080,128]{1,0:T(8,128)(2,1)S(1)}, bf16[2080,128]{1,0:T(8,128)(2,1)S(1)}, u32[]{:S(2)}, u32[]{:S(2)}) %collective-permute-start.6) | collective-permute-done | bytes 532512 | tf_op jit(solution)/shard_map/ppermute | solution.py:282
  31.0 1.6 %collective-permute-start.7 = (bf16[2080,128]{1,0:T(8,128)(2,1)S(1)}, bf16[2080,128]{1,0:T(8,128)(2,1)S(1)}, u32[]{:S(2)}, u32[]{:S(2)}) collective-permute-start(bf16[2080,128]{1,0:T(8,128)(2,1)S(1)} %collective-permute-done.6.refs_0_), channel_id=1, source_target_pairs={{0,4},{1,3},{2,0},{3,7},{4,8},{5,1},{6,2},{7,11},{8,12},{9,5},{10,... | collective-permute-start | bytes 1597448 | tf_op jit(solution)/shard_map/ppermute | solution.py:282
  32.5 2.0 %serve_rows.11 = f32[128,2048]{1,0:T(8,128)S(1)} custom-call(bf16[2080,128]{1,0:T(8,128)(2,1)S(1)} %collective-permute-done.6.refs_0_, bf16[2048,768]{1,0:T(8,128)(2,1)S(1)} %get-tuple-element.21.refs_2_.refs_1_, bf16[2048,384]{1,0:T(8,128)(2,1)S(1)} %get-tuple-element.22.refs_3_.refs_2_, bf16[2048,768]{1,0:T(8,128)(2,1)S(1)} %collective-permute-done.refs_4_.refs_3_, ...), custom_call_target="tpu_custom_call" | custom-call | tf_op jit(solution)/shard_map/serve_rows/pallas_call | solution.py:248
  34.5 2.1 %collective-permute-done.13 = bf16[128,2048]{1,0:T(8,128)(2,1)S(1)} collective-permute-done((bf16[128,2048]{1,0:T(8,128)(2,1)S(1)}, bf16[128,2048]{1,0:T(8,128)(2,1)S(1)}, u32[]{:S(2)}, u32[]{:S(2)}) %collective-permute-start.13) | collective-permute-done | bytes 524320 | tf_op jit(solution)/shard_map/ppermute | solution.py:298
  36.7 1.6 %collective-permute-start.14 = (bf16[128,2048]{1,0:T(8,128)(2,1)S(1)}, bf16[128,2048]{1,0:T(8,128)(2,1)S(1)}, u32[]{:S(2)}, u32[]{:S(2)}) collective-permute-start(bf16[128,2048]{1,0:T(8,128)(2,1)S(1)} %add_convert_fusion.2), channel_id=1, source_target_pairs={{0,4},{1,3},{2,0},{3,7},{4,8},{5,1},{6,2},{7,11},{8,12},{9,5},{10,... | collective-permute-start | bytes 1572872 | tf_op jit(solution)/shard_map/ppermute | solution.py:298
  38.4 3.9 %collective-permute-done.7.refs_0_ = bf16[2080,128]{1,0:T(8,128)(2,1)S(1)} collective-permute-done((bf16[2080,128]{1,0:T(8,128)(2,1)S(1)}, bf16[2080,128]{1,0:T(8,128)(2,1)S(1)}, u32[]{:S(2)}, u32[]{:S(2)}) %collective-permute-start.7) | collective-permute-done | bytes 532512 | tf_op jit(solution)/shard_map/ppermute | solution.py:282
  42.3 1.6 %collective-permute-start.8 = (bf16[2080,128]{1,0:T(8,128)(2,1)S(1)}, bf16[2080,128]{1,0:T(8,128)(2,1)S(1)}, u32[]{:S(2)}, u32[]{:S(2)}) collective-permute-start(bf16[2080,128]{1,0:T(8,128)(2,1)S(1)} %collective-permute-done.7.refs_0_), channel_id=1, source_target_pairs={{0,4},{1,3},{2,0},{3,7},{4,8},{5,1},{6,2},{7,11},{8,12},{9,5},{10,... | collective-permute-start | bytes 1597448 | tf_op jit(solution)/shard_map/ppermute | solution.py:282
  43.9 2.0 %serve_rows.12 = f32[128,2048]{1,0:T(8,128)S(1)} custom-call(bf16[2080,128]{1,0:T(8,128)(2,1)S(1)} %collective-permute-done.7.refs_0_, bf16[2048,768]{1,0:T(8,128)(2,1)S(1)} %get-tuple-element.21.refs_2_.refs_1_, bf16[2048,384]{1,0:T(8,128)(2,1)S(1)} %get-tuple-element.22.refs_3_.refs_2_, bf16[2048,768]{1,0:T(8,128)(2,1)S(1)} %collective-permute-done.refs_4_.refs_3_, ...), custom_call_target="tpu_custom_call" | custom-call | tf_op jit(solution)/shard_map/serve_rows/pallas_call | solution.py:248
  45.9 2.0 %collective-permute-done.14 = bf16[128,2048]{1,0:T(8,128)(2,1)S(1)} collective-permute-done((bf16[128,2048]{1,0:T(8,128)(2,1)S(1)}, bf16[128,2048]{1,0:T(8,128)(2,1)S(1)}, u32[]{:S(2)}, u32[]{:S(2)}) %collective-permute-start.14) | collective-permute-done | bytes 524320 | tf_op jit(solution)/shard_map/ppermute | solution.py:298
  48.0 1.6 %collective-permute-start.15 = (bf16[128,2048]{1,0:T(8,128)(2,1)S(1)}, bf16[128,2048]{1,0:T(8,128)(2,1)S(1)}, u32[]{:S(2)}, u32[]{:S(2)}) collective-permute-start(bf16[128,2048]{1,0:T(8,128)(2,1)S(1)} %add_convert_fusion.1), channel_id=1, source_target_pairs={{0,4},{1,3},{2,0},{3,7},{4,8},{5,1},{6,2},{7,11},{8,12},{9,5},{10,... | collective-permute-start | bytes 1572872 | tf_op jit(solution)/shard_map/ppermute | solution.py:298
  49.7 3.9 %collective-permute-done.8.refs_0_ = bf16[2080,128]{1,0:T(8,128)(2,1)S(1)} collective-permute-done((bf16[2080,128]{1,0:T(8,128)(2,1)S(1)}, bf16[2080,128]{1,0:T(8,128)(2,1)S(1)}, u32[]{:S(2)}, u32[]{:S(2)}) %collective-permute-start.8) | collective-permute-done | bytes 532512 | tf_op jit(solution)/shard_map/ppermute | solution.py:282
  53.6 1.6 %collective-permute-start.9 = (bf16[2080,128]{1,0:T(8,128)(2,1)S(1)}, bf16[2080,128]{1,0:T(8,128)(2,1)S(1)}, u32[]{:S(2)}, u32[]{:S(2)}) collective-permute-start(bf16[2080,128]{1,0:T(8,128)(2,1)S(1)} %collective-permute-done.8.refs_0_), channel_id=1, source_target_pairs={{0,4},{1,3},{2,0},{3,7},{4,8},{5,1},{6,2},{7,11},{8,12},{9,5},{10,... | collective-permute-start | bytes 1597448 | tf_op jit(solution)/shard_map/ppermute | solution.py:282
  55.2 2.0 %serve_rows.13 = f32[128,2048]{1,0:T(8,128)S(1)} custom-call(bf16[2080,128]{1,0:T(8,128)(2,1)S(1)} %collective-permute-done.8.refs_0_, bf16[2048,768]{1,0:T(8,128)(2,1)S(1)} %get-tuple-element.21.refs_2_.refs_1_, bf16[2048,384]{1,0:T(8,128)(2,1)S(1)} %get-tuple-element.22.refs_3_.refs_2_, bf16[2048,768]{1,0:T(8,128)(2,1)S(1)} %collective-permute-done.refs_4_.refs_3_, ...), custom_call_target="tpu_custom_call" | custom-call | tf_op jit(solution)/shard_map/serve_rows/pallas_call | solution.py:248
  57.2 2.0 %collective-permute-done.15 = bf16[128,2048]{1,0:T(8,128)(2,1)S(1)} collective-permute-done((bf16[128,2048]{1,0:T(8,128)(2,1)S(1)}, bf16[128,2048]{1,0:T(8,128)(2,1)S(1)}, u32[]{:S(2)}, u32[]{:S(2)}) %collective-permute-start.15) | collective-permute-done | bytes 524320 | tf_op jit(solution)/shard_map/ppermute | solution.py:298
  59.4 1.6 %collective-permute-start.16 = (bf16[128,2048]{1,0:T(8,128)(2,1)S(1)}, bf16[128,2048]{1,0:T(8,128)(2,1)S(1)}, u32[]{:S(2)}, u32[]{:S(2)}) collective-permute-start(bf16[128,2048]{1,0:T(8,128)(2,1)S(1)} %add_convert_fusion), channel_id=1, source_target_pairs={{0,4},{1,3},{2,0},{3,7},{4,8},{5,1},{6,2},{7,11},{8,12},{9,5},{10,... | collective-permute-start | bytes 1572872 | tf_op jit(solution)/shard_map/ppermute | solution.py:298
  61.0 3.9 %collective-permute-done.9.held.refs_0_ = bf16[2080,128]{1,0:T(8,128)(2,1)S(1)} collective-permute-done((bf16[2080,128]{1,0:T(8,128)(2,1)S(1)}, bf16[2080,128]{1,0:T(8,128)(2,1)S(1)}, u32[]{:S(2)}, u32[]{:S(2)}) %collective-permute-start.9) | collective-permute-done | bytes 532512 | tf_op jit(solution)/shard_map/ppermute | solution.py:282
  65.0 1.6 %collective-permute-start.11 = (bf16[1440,128]{1,0:T(8,128)(2,1)S(1)}, bf16[1440,128]{1,0:T(8,128)(2,1)S(1)}, u32[]{:S(2)}, u32[]{:S(2)}) collective-permute-start(bf16[1440,128]{1,0:T(8,128)(2,1)S(1)} %get-tuple-element.33), channel_id=1, source_target_pairs={{0,4},{1,3},{2,0},{3,7},{4,8},{5,1},{6,2},{7,11},{8,12},{9,5},{10,... | collective-permute-start | bytes 1105928 | tf_op jit(solution)/shard_map/ppermute | solution.py:279
  66.6 0.4 collective-permute-start.10
  67.1 2.0 %serve_rows.14 = f32[128,2048]{1,0:T(8,128)S(1)} custom-call(bf16[2080,128]{1,0:T(8,128)(2,1)S(1)} %collective-permute-done.9.held.refs_0_, bf16[2048,768]{1,0:T(8,128)(2,1)S(1)} %get-tuple-element.21.refs_2_.refs_1_, bf16[2048,384]{1,0:T(8,128)(2,1)S(1)} %get-tuple-element.22.refs_3_.refs_2_, bf16[2048,768]{1,0:T(8,128)(2,1)S(1)} %collective-permute-done.refs_4_.refs_3_, ...), custom_call_target="tpu_custom_call" | custom-call | tf_op jit(solution)/shard_map/serve_rows/pallas_call | solution.py:248
  69.0 4.6 %collective-permute-done.10.refs_0_ = bf16[640,128]{1,0:T(8,128)(2,1)S(1)} collective-permute-done((bf16[640,128]{1,0:T(8,128)(2,1)S(1)}, bf16[640,128]{1,0:T(8,128)(2,1)S(1)}, u32[]{:S(2)}, u32[]{:S(2)}) %collective-permute-start.10) | collective-permute-done | bytes 163872 | tf_op jit(solution)/shard_map/ppermute | solution.py:279
  73.7 0.8 collective-permute-done.11.refs_1_
  74.5 2.0 %serve_rows.15 = f32[128,2048]{1,0:T(8,128)S(1)} custom-call(bf16[640,128]{1,0:T(8,128)(2,1)S(1)} %collective-permute-done.10.refs_0_, bf16[1440,128]{1,0:T(8,128)(2,1)S(1)} %collective-permute-done.11.refs_1_, bf16[2048,768]{1,0:T(8,128)(2,1)S(1)} %get-tuple-element.21.refs_2_.refs_1_, bf16[2048,384]{1,0:T(8,128)(2,1)S(1)} %get-tuple-element.22.refs_3_.refs_2_, ...), custom_call_target="tpu_custom_call" | custom-call | tf_op jit(solution)/shard_map/serve_rows/pallas_call | solution.py:248
  76.7 1.6 %collective-permute-start.18 = (bf16[64,2048]{1,0:T(8,128)(2,1)S(1)}, bf16[64,2048]{1,0:T(8,128)(2,1)S(1)}, u32[]{:S(2)}, u32[]{:S(2)}) collective-permute-start(bf16[64,2048]{1,0:T(8,128)(2,1)S(1)} %fusion.1), channel_id=1, source_target_pairs={{0,4},{1,3},{2,0},{3,7},{4,8},{5,1},{6,2},{7,11},{8,12},{9,5},{10,... | collective-permute-start | bytes 786440 | tf_op jit(solution)/shard_map/ppermute | solution.py:298
  78.4 1.6 %collective-permute-start.17 = (bf16[64,2048]{1,0:T(8,128)(2,1)S(1)}, bf16[64,2048]{1,0:T(8,128)(2,1)S(1)}, u32[]{:S(2)}, u32[]{:S(2)}) collective-permute-start(bf16[64,2048]{1,0:T(8,128)(2,1)S(1)} %fusion.2), channel_id=1, source_target_pairs={{0,4},{1,3},{2,0},{3,7},{4,8},{5,1},{6,2},{7,11},{8,12},{9,5},{10,... | collective-permute-start | bytes 786440 | tf_op jit(solution)/shard_map/ppermute | solution.py:298
  80.0 3.1 %collective-permute-done.18 = bf16[64,2048]{1,0:T(8,128)(2,1)S(1)} collective-permute-done((bf16[64,2048]{1,0:T(8,128)(2,1)S(1)}, bf16[64,2048]{1,0:T(8,128)(2,1)S(1)}, u32[]{:S(2)}, u32[]{:S(2)}) %collective-permute-start.18) | collective-permute-done | bytes 262176 | tf_op jit(solution)/shard_map/ppermute | solution.py:298
  83.2 1.6 %collective-permute-start.20 = (bf16[64,2048]{1,0:T(8,128)(2,1)S(1)}, bf16[64,2048]{1,0:T(8,128)(2,1)S(1)}, u32[]{:S(2)}, u32[]{:S(2)}) collective-permute-start(bf16[64,2048]{1,0:T(8,128)(2,1)S(1)} %fusion), channel_id=1, source_target_pairs={{0,4},{1,3},{2,0},{3,7},{4,8},{5,1},{6,2},{7,11},{8,12},{9,5},{10,... | collective-permute-start | bytes 786440 | tf_op jit(solution)/shard_map/ppermute | solution.py:298
  84.8 1.1 %collective-permute-done.17 = bf16[64,2048]{1,0:T(8,128)(2,1)S(1)} collective-permute-done((bf16[64,2048]{1,0:T(8,128)(2,1)S(1)}, bf16[64,2048]{1,0:T(8,128)(2,1)S(1)}, u32[]{:S(2)}, u32[]{:S(2)}) %collective-permute-start.17) | collective-permute-done | bytes 262176 | tf_op jit(solution)/shard_map/ppermute | solution.py:298
  86.0 1.6 %collective-permute-start.19 = (bf16[64,2048]{1,0:T(8,128)(2,1)S(1)}, bf16[64,2048]{1,0:T(8,128)(2,1)S(1)}, u32[]{:S(2)}, u32[]{:S(2)}) collective-permute-start(bf16[64,2048]{1,0:T(8,128)(2,1)S(1)} %fusion.3), channel_id=1, source_target_pairs={{0,4},{1,3},{2,0},{3,7},{4,8},{5,1},{6,2},{7,11},{8,12},{9,5},{10,... | collective-permute-start | bytes 786440 | tf_op jit(solution)/shard_map/ppermute | solution.py:298
  87.6 2.0 %serve_rows.8.home = f32[128,2048]{1,0:T(8,128)S(1)} custom-call(bf16[1024,128]{1,0:T(8,128)(2,1)S(1)} %pack_rows.1.refs_0_.own, bf16[1056,128]{1,0:T(8,128)(2,1)S(1)} %pack_shares.1.refs_1_, bf16[2048,768]{1,0:T(8,128)(2,1)S(1)} %get-tuple-element.21.refs_2_.refs_1_, bf16[2048,384]{1,0:T(8,128)(2,1)S(1)} %get-tuple-element.22.refs_3_.refs_2_, ...), custom_call_target="tpu_custom_call" | custom-call | tf_op jit(solution)/shard_map/serve_rows/pallas_call | solution.py:248
  89.7 0.8 finish.2.refs_0_
  90.4 1.9 %collective-permute-done.19.got = bf16[64,2048]{1,0:T(8,128)(2,1)S(1)} collective-permute-done((bf16[64,2048]{1,0:T(8,128)(2,1)S(1)}, bf16[64,2048]{1,0:T(8,128)(2,1)S(1)}, u32[]{:S(2)}, u32[]{:S(2)}) %collective-permute-start.19) | collective-permute-done | bytes 262176 | tf_op jit(solution)/shard_map/ppermute | solution.py:298
  92.4 0.8 finish.3
  (19 shorter events, 1.0 us)
Async XLA Ops:
  0.0 13.9 %collective-permute-start = (bf16[2048,768]{1,0:T(8,128)(2,1)}, bf16[2048,768]{1,0:T(8,128)(2,1)S(1)}, u32[]{:S(2)}, u32[]{:S(2)}) collective-permute-start(bf16[2048,768]{1,0:T(8,128)(2,1)} %bitcast.4), channel_id=1, source_target_pairs={{0,1},{1,0},{2,3},{3,2},{4,5},{5,4},{6,7},{7,6},{8,9},{9,8},{10,11... | collective-permute-start | bytes 9437192 | tf_op jit(solution)/shard_map/ppermute | solution.py:235
  0.5 13.4 %collective-permute-start.1 = (bf16[2048,384]{1,0:T(8,128)(2,1)}, bf16[2048,384]{1,0:T(8,128)(2,1)S(1)}, u32[]{:S(2)}, u32[]{:S(2)}) collective-permute-start(bf16[2048,384]{1,0:T(8,128)(2,1)} %bitcast.6), channel_id=1, source_target_pairs={{0,1},{1,0},{2,3},{3,2},{4,5},{5,4},{6,7},{7,6},{8,9},{9,8},{10,11... | collective-permute-start | bytes 4718600 | tf_op jit(solution)/shard_map/ppermute | solution.py:235
  1.5 8.1 %collective-permute-start.4 = (bf16[1056,128]{1,0:T(8,128)(2,1)S(1)}, bf16[1056,128]{1,0:T(8,128)(2,1)S(1)}, u32[]{:S(2)}, u32[]{:S(2)}) collective-permute-start(bf16[1056,128]{1,0:T(8,128)(2,1)S(1)} %pack_shares.1.refs_1_), channel_id=1, source_target_pairs={{0,4},{1,3},{2,0},{3,7},{4,8},{5,1},{6,2},{7,11},{8,12},{9,5},{10,... | collective-permute-start | bytes 811016 | tf_op jit(solution)/shard_map/ppermute | solution.py:233
  5.6 6.4 %collective-permute-start.2 = (bf16[1024,128]{1,0:T(8,128)(2,1)S(1)}, bf16[1024,128]{1,0:T(8,128)(2,1)S(1)}, u32[]{:S(2)}, u32[]{:S(2)}) collective-permute-start(bf16[1024,128]{1,0:T(8,128)(2,1)S(1)} %pack_rows.1.refs_0_.own), channel_id=1, source_target_pairs={{0,4},{1,3},{2,0},{3,7},{4,8},{5,1},{6,2},{7,11},{8,12},{9,5},{10,... | collective-permute-start | bytes 786440 | tf_op jit(solution)/shard_map/ppermute | solution.py:233
  9.6 8.0 %collective-permute-start.5 = (bf16[1056,128]{1,0:T(8,128)(2,1)S(1)}, bf16[1056,128]{1,0:T(8,128)(2,1)S(1)}, u32[]{:S(2)}, u32[]{:S(2)}) collective-permute-start(bf16[1056,128]{1,0:T(8,128)(2,1)S(1)} %collective-permute-done.4.refs_1_), channel_id=1, source_target_pairs={{0,4},{1,3},{2,0},{3,7},{4,8},{5,1},{6,2},{7,11},{8,12},{9,5},{10,... | collective-permute-start | bytes 811016 | tf_op jit(solution)/shard_map/ppermute | solution.py:282
  12.0 6.9 %collective-permute-start.3 = (bf16[1024,128]{1,0:T(8,128)(2,1)S(1)}, bf16[1024,128]{1,0:T(8,128)(2,1)S(1)}, u32[]{:S(2)}, u32[]{:S(2)}) collective-permute-start(bf16[1024,128]{1,0:T(8,128)(2,1)S(1)} %collective-permute-done.2.refs_0_), channel_id=1, source_target_pairs={{0,4},{1,3},{2,0},{3,7},{4,8},{5,1},{6,2},{7,11},{8,12},{9,5},{10,... | collective-permute-start | bytes 786440 | tf_op jit(solution)/shard_map/ppermute | solution.py:282
  16.0 9.2 %collective-permute-start.12 = (bf16[128,2048]{1,0:T(8,128)(2,1)S(1)}, bf16[128,2048]{1,0:T(8,128)(2,1)S(1)}, u32[]{:S(2)}, u32[]{:S(2)}) collective-permute-start(bf16[128,2048]{1,0:T(8,128)(2,1)S(1)} %convert_element_type.51), channel_id=1, source_target_pairs={{0,4},{1,3},{2,0},{3,7},{4,8},{5,1},{6,2},{7,11},{8,12},{9,5},{10,... | collective-permute-start | bytes 1572872 | tf_op jit(solution)/shard_map/ppermute | solution.py:298
  19.0 12.0 %collective-permute-start.6 = (bf16[2080,128]{1,0:T(8,128)(2,1)S(1)}, bf16[2080,128]{1,0:T(8,128)(2,1)S(1)}, u32[]{:S(2)}, u32[]{:S(2)}) collective-permute-start(bf16[2080,128]{1,0:T(8,128)(2,1)S(1)} %pad_maximum_fusion), channel_id=1, source_target_pairs={{0,4},{1,3},{2,0},{3,7},{4,8},{5,1},{6,2},{7,11},{8,12},{9,5},{10,... | collective-permute-start | bytes 1597448 | tf_op jit(solution)/shard_map/ppermute | solution.py:282
  25.4 11.2 %collective-permute-start.13 = (bf16[128,2048]{1,0:T(8,128)(2,1)S(1)}, bf16[128,2048]{1,0:T(8,128)(2,1)S(1)}, u32[]{:S(2)}, u32[]{:S(2)}) collective-permute-start(bf16[128,2048]{1,0:T(8,128)(2,1)S(1)} %add_convert_fusion.3), channel_id=1, source_target_pairs={{0,4},{1,3},{2,0},{3,7},{4,8},{5,1},{6,2},{7,11},{8,12},{9,5},{10,... | collective-permute-start | bytes 1572872 | tf_op jit(solution)/shard_map/ppermute | solution.py:298
  31.0 11.3 %collective-permute-start.7 = (bf16[2080,128]{1,0:T(8,128)(2,1)S(1)}, bf16[2080,128]{1,0:T(8,128)(2,1)S(1)}, u32[]{:S(2)}, u32[]{:S(2)}) collective-permute-start(bf16[2080,128]{1,0:T(8,128)(2,1)S(1)} %collective-permute-done.6.refs_0_), channel_id=1, source_target_pairs={{0,4},{1,3},{2,0},{3,7},{4,8},{5,1},{6,2},{7,11},{8,12},{9,5},{10,... | collective-permute-start | bytes 1597448 | tf_op jit(solution)/shard_map/ppermute | solution.py:282
  36.7 11.2 %collective-permute-start.14 = (bf16[128,2048]{1,0:T(8,128)(2,1)S(1)}, bf16[128,2048]{1,0:T(8,128)(2,1)S(1)}, u32[]{:S(2)}, u32[]{:S(2)}) collective-permute-start(bf16[128,2048]{1,0:T(8,128)(2,1)S(1)} %add_convert_fusion.2), channel_id=1, source_target_pairs={{0,4},{1,3},{2,0},{3,7},{4,8},{5,1},{6,2},{7,11},{8,12},{9,5},{10,... | collective-permute-start | bytes 1572872 | tf_op jit(solution)/shard_map/ppermute | solution.py:298
  42.3 11.3 %collective-permute-start.8 = (bf16[2080,128]{1,0:T(8,128)(2,1)S(1)}, bf16[2080,128]{1,0:T(8,128)(2,1)S(1)}, u32[]{:S(2)}, u32[]{:S(2)}) collective-permute-start(bf16[2080,128]{1,0:T(8,128)(2,1)S(1)} %collective-permute-done.7.refs_0_), channel_id=1, source_target_pairs={{0,4},{1,3},{2,0},{3,7},{4,8},{5,1},{6,2},{7,11},{8,12},{9,5},{10,... | collective-permute-start | bytes 1597448 | tf_op jit(solution)/shard_map/ppermute | solution.py:282
  48.0 11.2 %collective-permute-start.15 = (bf16[128,2048]{1,0:T(8,128)(2,1)S(1)}, bf16[128,2048]{1,0:T(8,128)(2,1)S(1)}, u32[]{:S(2)}, u32[]{:S(2)}) collective-permute-start(bf16[128,2048]{1,0:T(8,128)(2,1)S(1)} %add_convert_fusion.1), channel_id=1, source_target_pairs={{0,4},{1,3},{2,0},{3,7},{4,8},{5,1},{6,2},{7,11},{8,12},{9,5},{10,... | collective-permute-start | bytes 1572872 | tf_op jit(solution)/shard_map/ppermute | solution.py:298
  53.6 11.3 %collective-permute-start.9 = (bf16[2080,128]{1,0:T(8,128)(2,1)S(1)}, bf16[2080,128]{1,0:T(8,128)(2,1)S(1)}, u32[]{:S(2)}, u32[]{:S(2)}) collective-permute-start(bf16[2080,128]{1,0:T(8,128)(2,1)S(1)} %collective-permute-done.8.refs_0_), channel_id=1, source_target_pairs={{0,4},{1,3},{2,0},{3,7},{4,8},{5,1},{6,2},{7,11},{8,12},{9,5},{10,... | collective-permute-start | bytes 1597448 | tf_op jit(solution)/shard_map/ppermute | solution.py:282
  59.4 17.2 %collective-permute-start.16 = (bf16[128,2048]{1,0:T(8,128)(2,1)S(1)}, bf16[128,2048]{1,0:T(8,128)(2,1)S(1)}, u32[]{:S(2)}, u32[]{:S(2)}) collective-permute-start(bf16[128,2048]{1,0:T(8,128)(2,1)S(1)} %add_convert_fusion), channel_id=1, source_target_pairs={{0,4},{1,3},{2,0},{3,7},{4,8},{5,1},{6,2},{7,11},{8,12},{9,5},{10,... | collective-permute-start | bytes 1572872 | tf_op jit(solution)/shard_map/ppermute | solution.py:298
  65.0 9.5 %collective-permute-start.11 = (bf16[1440,128]{1,0:T(8,128)(2,1)S(1)}, bf16[1440,128]{1,0:T(8,128)(2,1)S(1)}, u32[]{:S(2)}, u32[]{:S(2)}) collective-permute-start(bf16[1440,128]{1,0:T(8,128)(2,1)S(1)} %get-tuple-element.33), channel_id=1, source_target_pairs={{0,4},{1,3},{2,0},{3,7},{4,8},{5,1},{6,2},{7,11},{8,12},{9,5},{10,... | collective-permute-start | bytes 1105928 | tf_op jit(solution)/shard_map/ppermute | solution.py:279
  66.6 7.1 %collective-permute-start.10 = (bf16[640,128]{1,0:T(8,128)(2,1)S(1)}, bf16[640,128]{1,0:T(8,128)(2,1)S(1)}, u32[]{:S(2)}, u32[]{:S(2)}) collective-permute-start(bf16[640,128]{1,0:T(8,128)(2,1)S(1)} %get-tuple-element.31), channel_id=1, source_target_pairs={{0,2},{1,3},{2,6},{3,7},{4,0},{5,1},{6,10},{7,11},{8,4},{9,5},{10,... | collective-permute-start | bytes 491528 | tf_op jit(solution)/shard_map/ppermute | solution.py:279
  76.7 6.4 %collective-permute-start.18 = (bf16[64,2048]{1,0:T(8,128)(2,1)S(1)}, bf16[64,2048]{1,0:T(8,128)(2,1)S(1)}, u32[]{:S(2)}, u32[]{:S(2)}) collective-permute-start(bf16[64,2048]{1,0:T(8,128)(2,1)S(1)} %fusion.1), channel_id=1, source_target_pairs={{0,4},{1,3},{2,0},{3,7},{4,8},{5,1},{6,2},{7,11},{8,12},{9,5},{10,... | collective-permute-start | bytes 786440 | tf_op jit(solution)/shard_map/ppermute | solution.py:298
  78.4 7.5 %collective-permute-start.17 = (bf16[64,2048]{1,0:T(8,128)(2,1)S(1)}, bf16[64,2048]{1,0:T(8,128)(2,1)S(1)}, u32[]{:S(2)}, u32[]{:S(2)}) collective-permute-start(bf16[64,2048]{1,0:T(8,128)(2,1)S(1)} %fusion.2), channel_id=1, source_target_pairs={{0,4},{1,3},{2,0},{3,7},{4,8},{5,1},{6,2},{7,11},{8,12},{9,5},{10,... | collective-permute-start | bytes 786440 | tf_op jit(solution)/shard_map/ppermute | solution.py:298
  83.2 6.5 %collective-permute-start.20 = (bf16[64,2048]{1,0:T(8,128)(2,1)S(1)}, bf16[64,2048]{1,0:T(8,128)(2,1)S(1)}, u32[]{:S(2)}, u32[]{:S(2)}) collective-permute-start(bf16[64,2048]{1,0:T(8,128)(2,1)S(1)} %fusion), channel_id=1, source_target_pairs={{0,4},{1,3},{2,0},{3,7},{4,8},{5,1},{6,2},{7,11},{8,12},{9,5},{10,... | collective-permute-start | bytes 786440 | tf_op jit(solution)/shard_map/ppermute | solution.py:298
  86.0 6.4 %collective-permute-start.19 = (bf16[64,2048]{1,0:T(8,128)(2,1)S(1)}, bf16[64,2048]{1,0:T(8,128)(2,1)S(1)}, u32[]{:S(2)}, u32[]{:S(2)}) collective-permute-start(bf16[64,2048]{1,0:T(8,128)(2,1)S(1)} %fusion.3), channel_id=1, source_target_pairs={{0,4},{1,3},{2,0},{3,7},{4,8},{5,1},{6,2},{7,11},{8,12},{9,5},{10,... | collective-permute-start | bytes 786440 | tf_op jit(solution)/shard_map/ppermute | solution.py:298

commit v4 on v2

--- a/solution.py
+++ b/solution.py
@@ -107,6 +107,22 @@
         copy.wait()
 
 
+def turn_back(places, held, own, mine, rest):
+    some = mine.shape[0]
+    me = lax.axis_index("expert")
+    place = sum(jnp.where(me == e, place, 0) for e, place in enumerate(places))
+
+    @pl.when(place == 0)
+    def _():
+        mine[...] = own[:some]
+
+    @pl.when(place != 0)
+    def _():
+        mine[...] = held[:some]
+
+    rest[...] = held[some:]
+
+
 def serve_rows(width, picks, partner, *refs):
     pieces, refs, out = refs[: -1 - 2 * len(picks)], refs[-1 - 2 * len(picks) : -1], refs[-1]
     tok_rows, features = out.shape
@@ -131,7 +147,7 @@
         gated, up = pre[:, :width], pre[:, width:]
         hidden = (gated / (1.0 + jnp.exp(-gated)) * up).astype(jnp.bfloat16)
         experts.append((share, hidden, down))
-    columns = 4 * LANES
+    columns = 2 * LANES
     for start in range(0, features, columns):
         chunk, total = slice(start, min(start + columns, features)), None
         for share, hidden, down in experts:
@@ -161,10 +177,14 @@
     count = len(stops)
     partner = [0] * num_experts
     onward = [0] * num_experts
+    back = [0] * num_experts
+    places = [0] * num_experts
     for s in range(count):
         for place, turn in ((0, 1), (1, -1)):
             partner[stops[s][place]] = stops[s][1 - place]
             onward[stops[s][place]] = stops[(s + turn) % count][place]
+            back[stops[s][place]] = stops[(s - 1) % count][place]
+            places[stops[s][place]] = place
     hop = functools.partial(lax.ppermute, axis_name="expert", perm=list(enumerate(onward)))
     swap = functools.partial(lax.ppermute, axis_name="expert", perm=list(enumerate(partner)))
     whole = pl.BlockSpec(memory_space=pltpu.VMEM)
@@ -215,13 +235,28 @@
         return [lax.optimization_barrier((x, other))[0] for x in arrays]
 
     away = after(away, held)
+    some = features // LANES * 5 // 16 * tok_rows
     total = None
     for step in range(1, count):
         here = list(away)
         if step < count - 1:
             away = away if step == 1 else [jnp.concatenate(away)]
-            for at, x in enumerate(away):
-                away[at] = hop(x)
+            if step == count - 2:
+                mine, rest = pl.pallas_call(
+                    functools.partial(turn_back, places),
+                    out_shape=[
+                        jax.ShapeDtypeStruct((rows, LANES), jnp.bfloat16)
+                        for rows in (some, away[0].shape[0] - some)
+                    ],
+                    in_specs=[whole] * 2,
+                    out_specs=[whole] * 2,
+                    compiler_params=pltpu.CompilerParams(vmem_limit_bytes=2 * 1024 * 1024),
+                    name="turn_back",
+                )(away[0], packed[0])
+                away = [lax.ppermute(mine, "expert", list(enumerate(back))), hop(rest)]
+            else:
+                for at, x in enumerate(away):
+                    away[at] = hop(x)
         more = serve(here, (0, 1))
         away = after(away, more)
         parts = 2 if step >= count - 2 else 1
@@ -270,7 +305,7 @@
     )
 
     stops = chip_cycle(mesh)
-    cycle = mesh.shape["token"] == 1 and {len(s) for s in stops} == {2} and len(stops) > 2
+    cycle = mesh.shape["token"] == 1 and {len(s) for s in stops} == {2} and len(stops) > 4
 
     def per_device(tokens, expert_ids, route_weights, gate_up, down_t):
         fits = cycle and mesh.shape["expert"] <= 4 * expert_ids.shape[1] and gate_up.shape[0] == 1

time: 89.7 us -> 93.6 us (1.043)
  waiting for transfers between devices: 34.7 us -> 38.3 us
    ppermute x0 -> x2, waiting for transfers between devices: none -> 5.53 us  [ring(): away = [lax.ppermute(mine, 'expert', list(enumerate(back))), hop(rest)]]
    ppermute x7 -> x6, waiting for transfers between devices: 18.8 us -> 16.4 us  [ring(): away[at] = hop(x)]
    ppermute x0 -> x2, starting transfers between devices: none -> 2.08 us  [ring(): away = [lax.ppermute(mine, 'expert', list(enumerate(back))), hop(rest)]]
    ppermute x7 -> x6, starting transfers between devices: 12.6 us -> 11.1 us  [ring(): away[at] = hop(x)]
  transfers between devices with their start and end apart: 20 -> 21, of which waited for: 16 -> 16; matrix products, arithmetic and copies ran while one was open for 1% -> 1% of each run, Pallas kernels for 23% -> 21%
where the time goes in v4:
time: 93.6 us; the launch traced here: 93.4 us
  waiting for transfers between devices  38.3 us (41%)
  starting transfers between devices  33 us (35%)
  Pallas kernels  20.8 us (22%)
    ppermute x6, waiting for transfers between devices, ring(): away[at] = hop(x)  16.4 us
    pallas_call x8, Pallas kernels, serve(): pl.pallas_call(functools.partial(serve_rows, width, picks, partner), out_...  15.6 us
    ppermute x9, waiting for transfers between devices, ring(): total.append(hop(x))  15.3 us
    ppermute x9, starting transfers between devices, ring(): total.append(hop(x))  14.7 us
    ppermute x6, starting transfers between devices, ring(): away[at] = hop(x)  11.1 us
    ppermute x2, waiting for transfers between devices, ring(): away = [lax.ppermute(mine, 'expert', list(enumerate(back))), hop(rest)]  5.53 us
    ppermute x2, starting transfers between devices, ring(): away.append(hop(x))  4.68 us
    pallas_call x1, Pallas kernels, ring(): pl.pallas_call(load, out_shape=[jax.ShapeDtypeStruct(w.shape, w.dtype) fo...  2.37 us
  transfers between devices with their start and end apart: 21, of which 16 were waited for; matrix products, arithmetic and copies ran while one was open for 1% of the time, Pallas kernels for 21%

profile of v4, /device:TPU:0, one launch (start us, length us, event | category | flops | bytes accessed | tf_op | source)
XLA Modules:
  0.0 93.4 jit_solution(913926385094796594)
XLA Ops:
  0.0 0.5 collective-permute-start
  0.5 1.2 %pack_rows.1 = (bf16[1024,128]{1,0:T(8,128)(2,1)S(1)}, bf16[1056,128]{1,0:T(8,128)(2,1)S(1)}) custom-call(bf16[128,2048]{1,0:T(8,128)(2,1)} %tokens.1, s32[8,128]{1,0:T(8,128)} %bitcast.8, f32[8,128]{1,0:T(8,128)} %bitcast.9), custom_call_target="tpu_custom_call" | custom-call | tf_op jit(solution)/shard_map/pack_rows/pallas_call | solution.py:195
  1.7 3.1 %collective-permute-start.4 = (bf16[1056,128]{1,0:T(8,128)(2,1)S(1)}, bf16[1056,128]{1,0:T(8,128)(2,1)S(1)}, u32[]{:S(2)}, u32[]{:S(2)}) collective-permute-start(bf16[1056,128]{1,0:T(8,128)(2,1)S(1)} %get-tuple-element.24.refs_1_), channel_id=1, source_target_pairs={{0,4},{1,3},{2,0},{3,7},{4,8},{5,1},{6,2},{7,11},{8,12},{9,5},{10,... | collective-permute-start | bytes 811016 | tf_op jit(solution)/shard_map/ppermute | solution.py:210
  4.8 1.6 %collective-permute-start.2 = (bf16[1024,128]{1,0:T(8,128)(2,1)S(1)}, bf16[1024,128]{1,0:T(8,128)(2,1)S(1)}, u32[]{:S(2)}, u32[]{:S(2)}) collective-permute-start(bf16[1024,128]{1,0:T(8,128)(2,1)S(1)} %get-tuple-element.23.refs_0_.own), channel_id=1, source_target_pairs={{0,4},{1,3},{2,0},{3,7},{4,8},{5,1},{6,2},{7,11},{8,12},{9,5},{10,... | collective-permute-start | bytes 786440 | tf_op jit(solution)/shard_map/ppermute | solution.py:210
  6.4 2.4 %load.1 = (bf16[2048,768]{1,0:T(8,128)(2,1)S(1)}, bf16[2048,384]{1,0:T(8,128)(2,1)S(1)}) custom-call(bf16[2048,768]{1,0:T(8,128)(2,1)} %bitcast.5, bf16[2048,384]{1,0:T(8,128)(2,1)} %bitcast.7), custom_call_target="tpu_custom_call" | custom-call | tf_op jit(solution)/shard_map/load/pallas_call | solution.py:213
  8.8 0.4 collective-permute-done.4.refs_1_
  9.2 2.1 %collective-permute-start.5 = (bf16[1056,128]{1,0:T(8,128)(2,1)S(1)}, bf16[1056,128]{1,0:T(8,128)(2,1)S(1)}, u32[]{:S(2)}, u32[]{:S(2)}) collective-permute-start(bf16[1056,128]{1,0:T(8,128)(2,1)S(1)} %collective-permute-done.4.refs_1_), channel_id=1, source_target_pairs={{0,4},{1,3},{2,0},{3,7},{4,8},{5,1},{6,2},{7,11},{8,12},{9,5},{10,... | collective-permute-start | bytes 811016 | tf_op jit(solution)/shard_map/ppermute | solution.py:259
  11.3 0.7 collective-permute-done.2.refs_0_
  12.0 2.1 %collective-permute-start.3 = (bf16[1024,128]{1,0:T(8,128)(2,1)S(1)}, bf16[1024,128]{1,0:T(8,128)(2,1)S(1)}, u32[]{:S(2)}, u32[]{:S(2)}) collective-permute-start(bf16[1024,128]{1,0:T(8,128)(2,1)S(1)} %collective-permute-done.2.refs_0_), channel_id=1, source_target_pairs={{0,4},{1,3},{2,0},{3,7},{4,8},{5,1},{6,2},{7,11},{8,12},{9,5},{10,... | collective-permute-start | bytes 786440 | tf_op jit(solution)/shard_map/ppermute | solution.py:259
  14.1 1.9 %serve_rows.9 = f32[128,2048]{1,0:T(8,128)S(1)} custom-call(bf16[1024,128]{1,0:T(8,128)(2,1)S(1)} %collective-permute-done.2.refs_0_, bf16[1056,128]{1,0:T(8,128)(2,1)S(1)} %collective-permute-done.4.refs_1_, bf16[2048,768]{1,0:T(8,128)(2,1)S(1)} %get-tuple-element.25.refs_2_.refs_1_, bf16[2048,384]{1,0:T(8,128)(2,1)S(1)} %get-tuple-element.26.refs_3_.refs_2_, ...), custom_call_target="tpu_custom_call" | custom-call | tf_op jit(solution)/shard_map/serve_rows/pallas_call | solution.py:225
  16.1 1.6 %collective-permute-start.12 = (bf16[128,2048]{1,0:T(8,128)(2,1)S(1)}, bf16[128,2048]{1,0:T(8,128)(2,1)S(1)}, u32[]{:S(2)}, u32[]{:S(2)}) collective-permute-start(bf16[128,2048]{1,0:T(8,128)(2,1)S(1)} %convert_element_type.51), channel_id=1, source_target_pairs={{0,4},{1,3},{2,0},{3,7},{4,8},{5,1},{6,2},{7,11},{8,12},{9,5},{10,... | collective-permute-start | bytes 1572872 | tf_op jit(solution)/shard_map/ppermute | solution.py:275
  17.8 0.7 collective-permute-done.3.refs_0_
  18.5 2.2 %collective-permute-start.6 = (bf16[2080,128]{1,0:T(8,128)(2,1)S(1)}, bf16[2080,128]{1,0:T(8,128)(2,1)S(1)}, u32[]{:S(2)}, u32[]{:S(2)}) collective-permute-start(bf16[2080,128]{1,0:T(8,128)(2,1)S(1)} %pad_maximum_fusion), channel_id=1, source_target_pairs={{0,4},{1,3},{2,0},{3,7},{4,8},{5,1},{6,2},{7,11},{8,12},{9,5},{10,... | collective-permute-start | bytes 1597448 | tf_op jit(solution)/shard_map/ppermute | solution.py:259
  20.6 1.9 %serve_rows.10 = f32[128,2048]{1,0:T(8,128)S(1)} custom-call(bf16[1024,128]{1,0:T(8,128)(2,1)S(1)} %collective-permute-done.3.refs_0_, bf16[1056,128]{1,0:T(8,128)(2,1)S(1)} %collective-permute-done.5.refs_1_, bf16[2048,768]{1,0:T(8,128)(2,1)S(1)} %get-tuple-element.25.refs_2_.refs_1_, bf16[2048,384]{1,0:T(8,128)(2,1)S(1)} %get-tuple-element.26.refs_3_.refs_2_, ...), custom_call_target="tpu_custom_call" | custom-call | tf_op jit(solution)/shard_map/serve_rows/pallas_call | solution.py:225
  22.6 2.8 %collective-permute-done.12 = bf16[128,2048]{1,0:T(8,128)(2,1)S(1)} collective-permute-done((bf16[128,2048]{1,0:T(8,128)(2,1)S(1)}, bf16[128,2048]{1,0:T(8,128)(2,1)S(1)}, u32[]{:S(2)}, u32[]{:S(2)}) %collective-permute-start.12) | collective-permute-done | bytes 524320 | tf_op jit(solution)/shard_map/ppermute | solution.py:275
  25.5 1.6 %collective-permute-start.13 = (bf16[128,2048]{1,0:T(8,128)(2,1)S(1)}, bf16[128,2048]{1,0:T(8,128)(2,1)S(1)}, u32[]{:S(2)}, u32[]{:S(2)}) collective-permute-start(bf16[128,2048]{1,0:T(8,128)(2,1)S(1)} %add_convert_fusion.3), channel_id=1, source_target_pairs={{0,4},{1,3},{2,0},{3,7},{4,8},{5,1},{6,2},{7,11},{8,12},{9,5},{10,... | collective-permute-start | bytes 1572872 | tf_op jit(solution)/shard_map/ppermute | solution.py:275
  27.1 3.9 %collective-permute-done.6.refs_0_ = bf16[2080,128]{1,0:T(8,128)(2,1)S(1)} collective-permute-done((bf16[2080,128]{1,0:T(8,128)(2,1)S(1)}, bf16[2080,128]{1,0:T(8,128)(2,1)S(1)}, u32[]{:S(2)}, u32[]{:S(2)}) %collective-permute-start.6) | collective-permute-done | bytes 532512 | tf_op jit(solution)/shard_map/ppermute | solution.py:259
  31.1 1.6 %collective-permute-start.7 = (bf16[2080,128]{1,0:T(8,128)(2,1)S(1)}, bf16[2080,128]{1,0:T(8,128)(2,1)S(1)}, u32[]{:S(2)}, u32[]{:S(2)}) collective-permute-start(bf16[2080,128]{1,0:T(8,128)(2,1)S(1)} %collective-permute-done.6.refs_0_), channel_id=1, source_target_pairs={{0,4},{1,3},{2,0},{3,7},{4,8},{5,1},{6,2},{7,11},{8,12},{9,5},{10,... | collective-permute-start | bytes 1597448 | tf_op jit(solution)/shard_map/ppermute | solution.py:259
  32.6 2.0 %serve_rows.11 = f32[128,2048]{1,0:T(8,128)S(1)} custom-call(bf16[2080,128]{1,0:T(8,128)(2,1)S(1)} %collective-permute-done.6.refs_0_, bf16[2048,768]{1,0:T(8,128)(2,1)S(1)} %get-tuple-element.25.refs_2_.refs_1_, bf16[2048,384]{1,0:T(8,128)(2,1)S(1)} %get-tuple-element.26.refs_3_.refs_2_, bf16[2048,768]{1,0:T(8,128)(2,1)S(1)} %collective-permute-done.refs_4_.refs_3_, ...), custom_call_target="tpu_custom_call" | custom-call | tf_op jit(solution)/shard_map/serve_rows/pallas_call | solution.py:225
  34.6 2.0 %collective-permute-done.13 = bf16[128,2048]{1,0:T(8,128)(2,1)S(1)} collective-permute-done((bf16[128,2048]{1,0:T(8,128)(2,1)S(1)}, bf16[128,2048]{1,0:T(8,128)(2,1)S(1)}, u32[]{:S(2)}, u32[]{:S(2)}) %collective-permute-start.13) | collective-permute-done | bytes 524320 | tf_op jit(solution)/shard_map/ppermute | solution.py:275
  36.8 1.6 %collective-permute-start.14 = (bf16[128,2048]{1,0:T(8,128)(2,1)S(1)}, bf16[128,2048]{1,0:T(8,128)(2,1)S(1)}, u32[]{:S(2)}, u32[]{:S(2)}) collective-permute-start(bf16[128,2048]{1,0:T(8,128)(2,1)S(1)} %add_convert_fusion.2), channel_id=1, source_target_pairs={{0,4},{1,3},{2,0},{3,7},{4,8},{5,1},{6,2},{7,11},{8,12},{9,5},{10,... | collective-permute-start | bytes 1572872 | tf_op jit(solution)/shard_map/ppermute | solution.py:275
  38.4 3.9 %collective-permute-done.7.refs_0_ = bf16[2080,128]{1,0:T(8,128)(2,1)S(1)} collective-permute-done((bf16[2080,128]{1,0:T(8,128)(2,1)S(1)}, bf16[2080,128]{1,0:T(8,128)(2,1)S(1)}, u32[]{:S(2)}, u32[]{:S(2)}) %collective-permute-start.7) | collective-permute-done | bytes 532512 | tf_op jit(solution)/shard_map/ppermute | solution.py:259
  42.4 1.6 %collective-permute-start.8 = (bf16[2080,128]{1,0:T(8,128)(2,1)S(1)}, bf16[2080,128]{1,0:T(8,128)(2,1)S(1)}, u32[]{:S(2)}, u32[]{:S(2)}) collective-permute-start(bf16[2080,128]{1,0:T(8,128)(2,1)S(1)} %collective-permute-done.7.refs_0_), channel_id=1, source_target_pairs={{0,4},{1,3},{2,0},{3,7},{4,8},{5,1},{6,2},{7,11},{8,12},{9,5},{10,... | collective-permute-start | bytes 1597448 | tf_op jit(solution)/shard_map/ppermute | solution.py:259
  44.0 1.9 %serve_rows.12 = f32[128,2048]{1,0:T(8,128)S(1)} custom-call(bf16[2080,128]{1,0:T(8,128)(2,1)S(1)} %collective-permute-done.7.refs_0_, bf16[2048,768]{1,0:T(8,128)(2,1)S(1)} %get-tuple-element.25.refs_2_.refs_1_, bf16[2048,384]{1,0:T(8,128)(2,1)S(1)} %get-tuple-element.26.refs_3_.refs_2_, bf16[2048,768]{1,0:T(8,128)(2,1)S(1)} %collective-permute-done.refs_4_.refs_3_, ...), custom_call_target="tpu_custom_call" | custom-call | tf_op jit(solution)/shard_map/serve_rows/pallas_call | solution.py:225
  45.9 2.1 %collective-permute-done.14 = bf16[128,2048]{1,0:T(8,128)(2,1)S(1)} collective-permute-done((bf16[128,2048]{1,0:T(8,128)(2,1)S(1)}, bf16[128,2048]{1,0:T(8,128)(2,1)S(1)}, u32[]{:S(2)}, u32[]{:S(2)}) %collective-permute-start.14) | collective-permute-done | bytes 524320 | tf_op jit(solution)/shard_map/ppermute | solution.py:275
  48.1 1.6 %collective-permute-start.15 = (bf16[128,2048]{1,0:T(8,128)(2,1)S(1)}, bf16[128,2048]{1,0:T(8,128)(2,1)S(1)}, u32[]{:S(2)}, u32[]{:S(2)}) collective-permute-start(bf16[128,2048]{1,0:T(8,128)(2,1)S(1)} %add_convert_fusion.1), channel_id=1, source_target_pairs={{0,4},{1,3},{2,0},{3,7},{4,8},{5,1},{6,2},{7,11},{8,12},{9,5},{10,... | collective-permute-start | bytes 1572872 | tf_op jit(solution)/shard_map/ppermute | solution.py:275
  49.8 3.9 %collective-permute-done.8.refs_0_ = bf16[2080,128]{1,0:T(8,128)(2,1)S(1)} collective-permute-done((bf16[2080,128]{1,0:T(8,128)(2,1)S(1)}, bf16[2080,128]{1,0:T(8,128)(2,1)S(1)}, u32[]{:S(2)}, u32[]{:S(2)}) %collective-permute-start.8) | collective-permute-done | bytes 532512 | tf_op jit(solution)/shard_map/ppermute | solution.py:259
  53.7 1.6 %collective-permute-start.9 = (bf16[2080,128]{1,0:T(8,128)(2,1)S(1)}, bf16[2080,128]{1,0:T(8,128)(2,1)S(1)}, u32[]{:S(2)}, u32[]{:S(2)}) collective-permute-start(bf16[2080,128]{1,0:T(8,128)(2,1)S(1)} %collective-permute-done.8.refs_0_), channel_id=1, source_target_pairs={{0,4},{1,3},{2,0},{3,7},{4,8},{5,1},{6,2},{7,11},{8,12},{9,5},{10,... | collective-permute-start | bytes 1597448 | tf_op jit(solution)/shard_map/ppermute | solution.py:259
  55.3 2.0 %serve_rows.13 = f32[128,2048]{1,0:T(8,128)S(1)} custom-call(bf16[2080,128]{1,0:T(8,128)(2,1)S(1)} %collective-permute-done.8.refs_0_, bf16[2048,768]{1,0:T(8,128)(2,1)S(1)} %get-tuple-element.25.refs_2_.refs_1_, bf16[2048,384]{1,0:T(8,128)(2,1)S(1)} %get-tuple-element.26.refs_3_.refs_2_, bf16[2048,768]{1,0:T(8,128)(2,1)S(1)} %collective-permute-done.refs_4_.refs_3_, ...), custom_call_target="tpu_custom_call" | custom-call | tf_op jit(solution)/shard_map/serve_rows/pallas_call | solution.py:225
  57.3 2.0 %collective-permute-done.15 = bf16[128,2048]{1,0:T(8,128)(2,1)S(1)} collective-permute-done((bf16[128,2048]{1,0:T(8,128)(2,1)S(1)}, bf16[128,2048]{1,0:T(8,128)(2,1)S(1)}, u32[]{:S(2)}, u32[]{:S(2)}) %collective-permute-start.15) | collective-permute-done | bytes 524320 | tf_op jit(solution)/shard_map/ppermute | solution.py:275
  59.5 1.6 %collective-permute-start.16 = (bf16[128,2048]{1,0:T(8,128)(2,1)S(1)}, bf16[128,2048]{1,0:T(8,128)(2,1)S(1)}, u32[]{:S(2)}, u32[]{:S(2)}) collective-permute-start(bf16[128,2048]{1,0:T(8,128)(2,1)S(1)} %add_convert_fusion), channel_id=1, source_target_pairs={{0,4},{1,3},{2,0},{3,7},{4,8},{5,1},{6,2},{7,11},{8,12},{9,5},{10,... | collective-permute-start | bytes 1572872 | tf_op jit(solution)/shard_map/ppermute | solution.py:275
  61.1 3.9 %collective-permute-done.9.held.refs_0_ = bf16[2080,128]{1,0:T(8,128)(2,1)S(1)} collective-permute-done((bf16[2080,128]{1,0:T(8,128)(2,1)S(1)}, bf16[2080,128]{1,0:T(8,128)(2,1)S(1)}, u32[]{:S(2)}, u32[]{:S(2)}) %collective-permute-start.9) | collective-permute-done | bytes 532512 | tf_op jit(solution)/shard_map/ppermute | solution.py:259
  65.1 1.6 %collective-permute-start.11 = (bf16[1440,128]{1,0:T(8,128)(2,1)S(1)}, bf16[1440,128]{1,0:T(8,128)(2,1)S(1)}, u32[]{:S(2)}, u32[]{:S(2)}) collective-permute-start(bf16[1440,128]{1,0:T(8,128)(2,1)S(1)} %get-tuple-element.37), channel_id=1, source_target_pairs={{0,4},{1,3},{2,0},{3,7},{4,8},{5,1},{6,2},{7,11},{8,12},{9,5},{10,... | collective-permute-start | bytes 1105928 | tf_op jit(solution)/shard_map/ppermute | solution.py:256
  66.7 0.4 collective-permute-start.10
  67.2 1.9 %serve_rows.14 = f32[128,2048]{1,0:T(8,128)S(1)} custom-call(bf16[2080,128]{1,0:T(8,128)(2,1)S(1)} %collective-permute-done.9.held.refs_0_, bf16[2048,768]{1,0:T(8,128)(2,1)S(1)} %get-tuple-element.25.refs_2_.refs_1_, bf16[2048,384]{1,0:T(8,128)(2,1)S(1)} %get-tuple-element.26.refs_3_.refs_2_, bf16[2048,768]{1,0:T(8,128)(2,1)S(1)} %collective-permute-done.refs_4_.refs_3_, ...), custom_call_target="tpu_custom_call" | custom-call | tf_op jit(solution)/shard_map/serve_rows/pallas_call | solution.py:225
  69.1 4.7 %collective-permute-done.10.refs_0_ = bf16[640,128]{1,0:T(8,128)(2,1)S(1)} collective-permute-done((bf16[640,128]{1,0:T(8,128)(2,1)S(1)}, bf16[640,128]{1,0:T(8,128)(2,1)S(1)}, u32[]{:S(2)}, u32[]{:S(2)}) %collective-permute-start.10) | collective-permute-done | bytes 163872 | tf_op jit(solution)/shard_map/ppermute | solution.py:256
  73.8 0.8 collective-permute-done.11.refs_1_
  74.6 2.0 %serve_rows.15 = f32[128,2048]{1,0:T(8,128)S(1)} custom-call(bf16[640,128]{1,0:T(8,128)(2,1)S(1)} %collective-permute-done.10.refs_0_, bf16[1440,128]{1,0:T(8,128)(2,1)S(1)} %collective-permute-done.11.refs_1_, bf16[2048,768]{1,0:T(8,128)(2,1)S(1)} %get-tuple-element.25.refs_2_.refs_1_, bf16[2048,384]{1,0:T(8,128)(2,1)S(1)} %get-tuple-element.26.refs_3_.refs_2_, ...), custom_call_target="tpu_custom_call" | custom-call | tf_op jit(solution)/shard_map/serve_rows/pallas_call | solution.py:225
  76.7 1.6 %collective-permute-start.18 = (bf16[64,2048]{1,0:T(8,128)(2,1)S(1)}, bf16[64,2048]{1,0:T(8,128)(2,1)S(1)}, u32[]{:S(2)}, u32[]{:S(2)}) collective-permute-start(bf16[64,2048]{1,0:T(8,128)(2,1)S(1)} %fusion.1), channel_id=1, source_target_pairs={{0,4},{1,3},{2,0},{3,7},{4,8},{5,1},{6,2},{7,11},{8,12},{9,5},{10,... | collective-permute-start | bytes 786440 | tf_op jit(solution)/shard_map/ppermute | solution.py:275
  78.4 1.6 %collective-permute-start.17 = (bf16[64,2048]{1,0:T(8,128)(2,1)S(1)}, bf16[64,2048]{1,0:T(8,128)(2,1)S(1)}, u32[]{:S(2)}, u32[]{:S(2)}) collective-permute-start(bf16[64,2048]{1,0:T(8,128)(2,1)S(1)} %fusion.2), channel_id=1, source_target_pairs={{0,4},{1,3},{2,0},{3,7},{4,8},{5,1},{6,2},{7,11},{8,12},{9,5},{10,... | collective-permute-start | bytes 786440 | tf_op jit(solution)/shard_map/ppermute | solution.py:275
  80.0 3.1 %collective-permute-done.18 = bf16[64,2048]{1,0:T(8,128)(2,1)S(1)} collective-permute-done((bf16[64,2048]{1,0:T(8,128)(2,1)S(1)}, bf16[64,2048]{1,0:T(8,128)(2,1)S(1)}, u32[]{:S(2)}, u32[]{:S(2)}) %collective-permute-start.18) | collective-permute-done | bytes 262176 | tf_op jit(solution)/shard_map/ppermute | solution.py:275
  83.2 1.6 %collective-permute-start.20 = (bf16[64,2048]{1,0:T(8,128)(2,1)S(1)}, bf16[64,2048]{1,0:T(8,128)(2,1)S(1)}, u32[]{:S(2)}, u32[]{:S(2)}) collective-permute-start(bf16[64,2048]{1,0:T(8,128)(2,1)S(1)} %fusion), channel_id=1, source_target_pairs={{0,4},{1,3},{2,0},{3,7},{4,8},{5,1},{6,2},{7,11},{8,12},{9,5},{10,... | collective-permute-start | bytes 786440 | tf_op jit(solution)/shard_map/ppermute | solution.py:275
  84.8 1.1 %collective-permute-done.17 = bf16[64,2048]{1,0:T(8,128)(2,1)S(1)} collective-permute-done((bf16[64,2048]{1,0:T(8,128)(2,1)S(1)}, bf16[64,2048]{1,0:T(8,128)(2,1)S(1)}, u32[]{:S(2)}, u32[]{:S(2)}) %collective-permute-start.17) | collective-permute-done | bytes 262176 | tf_op jit(solution)/shard_map/ppermute | solution.py:275
  86.0 1.6 %collective-permute-start.19 = (bf16[64,2048]{1,0:T(8,128)(2,1)S(1)}, bf16[64,2048]{1,0:T(8,128)(2,1)S(1)}, u32[]{:S(2)}, u32[]{:S(2)}) collective-permute-start(bf16[64,2048]{1,0:T(8,128)(2,1)S(1)} %fusion.3), channel_id=1, source_target_pairs={{0,4},{1,3},{2,0},{3,7},{4,8},{5,1},{6,2},{7,11},{8,12},{9,5},{10,... | collective-permute-start | bytes 786440 | tf_op jit(solution)/shard_map/ppermute | solution.py:275
  87.6 1.9 %serve_rows.8.home = f32[128,2048]{1,0:T(8,128)S(1)} custom-call(bf16[1024,128]{1,0:T(8,128)(2,1)S(1)} %get-tuple-element.23.refs_0_.own, bf16[1056,128]{1,0:T(8,128)(2,1)S(1)} %get-tuple-element.24.refs_1_, bf16[2048,768]{1,0:T(8,128)(2,1)S(1)} %get-tuple-element.25.refs_2_.refs_1_, bf16[2048,384]{1,0:T(8,128)(2,1)S(1)} %get-tuple-element.26.refs_3_.refs_2_, ...), custom_call_target="tpu_custom_call" | custom-call | tf_op jit(solution)/shard_map/serve_rows/pallas_call | solution.py:225
  89.6 0.8 finish.2.refs_0_
  90.4 2.0 %collective-permute-done.19.got = bf16[64,2048]{1,0:T(8,128)(2,1)S(1)} collective-permute-done((bf16[64,2048]{1,0:T(8,128)(2,1)S(1)}, bf16[64,2048]{1,0:T(8,128)(2,1)S(1)}, u32[]{:S(2)}, u32[]{:S(2)}) %collective-permute-start.19) | collective-permute-done | bytes 262176 | tf_op jit(solution)/shard_map/ppermute | solution.py:275
  92.4 0.8 finish.3
  (18 shorter events, 1.0 us)
Async XLA Ops:
  0.0 14.1 %collective-permute-start = (bf16[2048,768]{1,0:T(8,128)(2,1)}, bf16[2048,768]{1,0:T(8,128)(2,1)S(1)}, u32[]{:S(2)}, u32[]{:S(2)}) collective-permute-start(bf16[2048,768]{1,0:T(8,128)(2,1)} %bitcast.4), channel_id=1, source_target_pairs={{0,1},{1,0},{2,3},{3,2},{4,5},{5,4},{6,7},{7,6},{8,9},{9,8},{10,11... | collective-permute-start | bytes 9437192 | tf_op jit(solution)/shard_map/ppermute | solution.py:212
  0.5 13.6 %collective-permute-start.1 = (bf16[2048,384]{1,0:T(8,128)(2,1)}, bf16[2048,384]{1,0:T(8,128)(2,1)S(1)}, u32[]{:S(2)}, u32[]{:S(2)}) collective-permute-start(bf16[2048,384]{1,0:T(8,128)(2,1)} %bitcast.6), channel_id=1, source_target_pairs={{0,1},{1,0},{2,3},{3,2},{4,5},{5,4},{6,7},{7,6},{8,9},{9,8},{10,11... | collective-permute-start | bytes 4718600 | tf_op jit(solution)/shard_map/ppermute | solution.py:212
  1.7 7.5 %collective-permute-start.4 = (bf16[1056,128]{1,0:T(8,128)(2,1)S(1)}, bf16[1056,128]{1,0:T(8,128)(2,1)S(1)}, u32[]{:S(2)}, u32[]{:S(2)}) collective-permute-start(bf16[1056,128]{1,0:T(8,128)(2,1)S(1)} %get-tuple-element.24.refs_1_), channel_id=1, source_target_pairs={{0,4},{1,3},{2,0},{3,7},{4,8},{5,1},{6,2},{7,11},{8,12},{9,5},{10,... | collective-permute-start | bytes 811016 | tf_op jit(solution)/shard_map/ppermute | solution.py:210
  4.8 7.2 %collective-permute-start.2 = (bf16[1024,128]{1,0:T(8,128)(2,1)S(1)}, bf16[1024,128]{1,0:T(8,128)(2,1)S(1)}, u32[]{:S(2)}, u32[]{:S(2)}) collective-permute-start(bf16[1024,128]{1,0:T(8,128)(2,1)S(1)} %get-tuple-element.23.refs_0_.own), channel_id=1, source_target_pairs={{0,4},{1,3},{2,0},{3,7},{4,8},{5,1},{6,2},{7,11},{8,12},{9,5},{10,... | collective-permute-start | bytes 786440 | tf_op jit(solution)/shard_map/ppermute | solution.py:210
  9.2 8.6 %collective-permute-start.5 = (bf16[1056,128]{1,0:T(8,128)(2,1)S(1)}, bf16[1056,128]{1,0:T(8,128)(2,1)S(1)}, u32[]{:S(2)}, u32[]{:S(2)}) collective-permute-start(bf16[1056,128]{1,0:T(8,128)(2,1)S(1)} %collective-permute-done.4.refs_1_), channel_id=1, source_target_pairs={{0,4},{1,3},{2,0},{3,7},{4,8},{5,1},{6,2},{7,11},{8,12},{9,5},{10,... | collective-permute-start | bytes 811016 | tf_op jit(solution)/shard_map/ppermute | solution.py:259
  12.0 6.5 %collective-permute-start.3 = (bf16[1024,128]{1,0:T(8,128)(2,1)S(1)}, bf16[1024,128]{1,0:T(8,128)(2,1)S(1)}, u32[]{:S(2)}, u32[]{:S(2)}) collective-permute-start(bf16[1024,128]{1,0:T(8,128)(2,1)S(1)} %collective-permute-done.2.refs_0_), channel_id=1, source_target_pairs={{0,4},{1,3},{2,0},{3,7},{4,8},{5,1},{6,2},{7,11},{8,12},{9,5},{10,... | collective-permute-start | bytes 786440 | tf_op jit(solution)/shard_map/ppermute | solution.py:259
  16.1 9.2 %collective-permute-start.12 = (bf16[128,2048]{1,0:T(8,128)(2,1)S(1)}, bf16[128,2048]{1,0:T(8,128)(2,1)S(1)}, u32[]{:S(2)}, u32[]{:S(2)}) collective-permute-start(bf16[128,2048]{1,0:T(8,128)(2,1)S(1)} %convert_element_type.51), channel_id=1, source_target_pairs={{0,4},{1,3},{2,0},{3,7},{4,8},{5,1},{6,2},{7,11},{8,12},{9,5},{10,... | collective-permute-start | bytes 1572872 | tf_op jit(solution)/shard_map/ppermute | solution.py:275
  18.5 12.6 %collective-permute-start.6 = (bf16[2080,128]{1,0:T(8,128)(2,1)S(1)}, bf16[2080,128]{1,0:T(8,128)(2,1)S(1)}, u32[]{:S(2)}, u32[]{:S(2)}) collective-permute-start(bf16[2080,128]{1,0:T(8,128)(2,1)S(1)} %pad_maximum_fusion), channel_id=1, source_target_pairs={{0,4},{1,3},{2,0},{3,7},{4,8},{5,1},{6,2},{7,11},{8,12},{9,5},{10,... | collective-permute-start | bytes 1597448 | tf_op jit(solution)/shard_map/ppermute | solution.py:259
  25.5 11.2 %collective-permute-start.13 = (bf16[128,2048]{1,0:T(8,128)(2,1)S(1)}, bf16[128,2048]{1,0:T(8,128)(2,1)S(1)}, u32[]{:S(2)}, u32[]{:S(2)}) collective-permute-start(bf16[128,2048]{1,0:T(8,128)(2,1)S(1)} %add_convert_fusion.3), channel_id=1, source_target_pairs={{0,4},{1,3},{2,0},{3,7},{4,8},{5,1},{6,2},{7,11},{8,12},{9,5},{10,... | collective-permute-start | bytes 1572872 | tf_op jit(solution)/shard_map/ppermute | solution.py:275
  31.1 11.3 %collective-permute-start.7 = (bf16[2080,128]{1,0:T(8,128)(2,1)S(1)}, bf16[2080,128]{1,0:T(8,128)(2,1)S(1)}, u32[]{:S(2)}, u32[]{:S(2)}) collective-permute-start(bf16[2080,128]{1,0:T(8,128)(2,1)S(1)} %collective-permute-done.6.refs_0_), channel_id=1, source_target_pairs={{0,4},{1,3},{2,0},{3,7},{4,8},{5,1},{6,2},{7,11},{8,12},{9,5},{10,... | collective-permute-start | bytes 1597448 | tf_op jit(solution)/shard_map/ppermute | solution.py:259
  36.8 11.2 %collective-permute-start.14 = (bf16[128,2048]{1,0:T(8,128)(2,1)S(1)}, bf16[128,2048]{1,0:T(8,128)(2,1)S(1)}, u32[]{:S(2)}, u32[]{:S(2)}) collective-permute-start(bf16[128,2048]{1,0:T(8,128)(2,1)S(1)} %add_convert_fusion.2), channel_id=1, source_target_pairs={{0,4},{1,3},{2,0},{3,7},{4,8},{5,1},{6,2},{7,11},{8,12},{9,5},{10,... | collective-permute-start | bytes 1572872 | tf_op jit(solution)/shard_map/ppermute | solution.py:275
  42.4 11.3 %collective-permute-start.8 = (bf16[2080,128]{1,0:T(8,128)(2,1)S(1)}, bf16[2080,128]{1,0:T(8,128)(2,1)S(1)}, u32[]{:S(2)}, u32[]{:S(2)}) collective-permute-start(bf16[2080,128]{1,0:T(8,128)(2,1)S(1)} %collective-permute-done.7.refs_0_), channel_id=1, source_target_pairs={{0,4},{1,3},{2,0},{3,7},{4,8},{5,1},{6,2},{7,11},{8,12},{9,5},{10,... | collective-permute-start | bytes 1597448 | tf_op jit(solution)/shard_map/ppermute | solution.py:259
  48.1 11.2 %collective-permute-start.15 = (bf16[128,2048]{1,0:T(8,128)(2,1)S(1)}, bf16[128,2048]{1,0:T(8,128)(2,1)S(1)}, u32[]{:S(2)}, u32[]{:S(2)}) collective-permute-start(bf16[128,2048]{1,0:T(8,128)(2,1)S(1)} %add_convert_fusion.1), channel_id=1, source_target_pairs={{0,4},{1,3},{2,0},{3,7},{4,8},{5,1},{6,2},{7,11},{8,12},{9,5},{10,... | collective-permute-start | bytes 1572872 | tf_op jit(solution)/shard_map/ppermute | solution.py:275
  53.7 11.3 %collective-permute-start.9 = (bf16[2080,128]{1,0:T(8,128)(2,1)S(1)}, bf16[2080,128]{1,0:T(8,128)(2,1)S(1)}, u32[]{:S(2)}, u32[]{:S(2)}) collective-permute-start(bf16[2080,128]{1,0:T(8,128)(2,1)S(1)} %collective-permute-done.8.refs_0_), channel_id=1, source_target_pairs={{0,4},{1,3},{2,0},{3,7},{4,8},{5,1},{6,2},{7,11},{8,12},{9,5},{10,... | collective-permute-start | bytes 1597448 | tf_op jit(solution)/shard_map/ppermute | solution.py:259
  59.5 17.1 %collective-permute-start.16 = (bf16[128,2048]{1,0:T(8,128)(2,1)S(1)}, bf16[128,2048]{1,0:T(8,128)(2,1)S(1)}, u32[]{:S(2)}, u32[]{:S(2)}) collective-permute-start(bf16[128,2048]{1,0:T(8,128)(2,1)S(1)} %add_convert_fusion), channel_id=1, source_target_pairs={{0,4},{1,3},{2,0},{3,7},{4,8},{5,1},{6,2},{7,11},{8,12},{9,5},{10,... | collective-permute-start | bytes 1572872 | tf_op jit(solution)/shard_map/ppermute | solution.py:275
  65.1 9.5 %collective-permute-start.11 = (bf16[1440,128]{1,0:T(8,128)(2,1)S(1)}, bf16[1440,128]{1,0:T(8,128)(2,1)S(1)}, u32[]{:S(2)}, u32[]{:S(2)}) collective-permute-start(bf16[1440,128]{1,0:T(8,128)(2,1)S(1)} %get-tuple-element.37), channel_id=1, source_target_pairs={{0,4},{1,3},{2,0},{3,7},{4,8},{5,1},{6,2},{7,11},{8,12},{9,5},{10,... | collective-permute-start | bytes 1105928 | tf_op jit(solution)/shard_map/ppermute | solution.py:256
  66.7 7.1 %collective-permute-start.10 = (bf16[640,128]{1,0:T(8,128)(2,1)S(1)}, bf16[640,128]{1,0:T(8,128)(2,1)S(1)}, u32[]{:S(2)}, u32[]{:S(2)}) collective-permute-start(bf16[640,128]{1,0:T(8,128)(2,1)S(1)} %get-tuple-element.35), channel_id=1, source_target_pairs={{0,2},{1,3},{2,6},{3,7},{4,0},{5,1},{6,10},{7,11},{8,4},{9,5},{10,... | collective-permute-start | bytes 491528 | tf_op jit(solution)/shard_map/ppermute | solution.py:256
  76.7 6.4 %collective-permute-start.18 = (bf16[64,2048]{1,0:T(8,128)(2,1)S(1)}, bf16[64,2048]{1,0:T(8,128)(2,1)S(1)}, u32[]{:S(2)}, u32[]{:S(2)}) collective-permute-start(bf16[64,2048]{1,0:T(8,128)(2,1)S(1)} %fusion.1), channel_id=1, source_target_pairs={{0,4},{1,3},{2,0},{3,7},{4,8},{5,1},{6,2},{7,11},{8,12},{9,5},{10,... | collective-permute-start | bytes 786440 | tf_op jit(solution)/shard_map/ppermute | solution.py:275
  78.4 7.5 %collective-permute-start.17 = (bf16[64,2048]{1,0:T(8,128)(2,1)S(1)}, bf16[64,2048]{1,0:T(8,128)(2,1)S(1)}, u32[]{:S(2)}, u32[]{:S(2)}) collective-permute-start(bf16[64,2048]{1,0:T(8,128)(2,1)S(1)} %fusion.2), channel_id=1, source_target_pairs={{0,4},{1,3},{2,0},{3,7},{4,8},{5,1},{6,2},{7,11},{8,12},{9,5},{10,... | collective-permute-start | bytes 786440 | tf_op jit(solution)/shard_map/ppermute | solution.py:275
  83.2 6.4 %collective-permute-start.20 = (bf16[64,2048]{1,0:T(8,128)(2,1)S(1)}, bf16[64,2048]{1,0:T(8,128)(2,1)S(1)}, u32[]{:S(2)}, u32[]{:S(2)}) collective-permute-start(bf16[64,2048]{1,0:T(8,128)(2,1)S(1)} %fusion), channel_id=1, source_target_pairs={{0,4},{1,3},{2,0},{3,7},{4,8},{5,1},{6,2},{7,11},{8,12},{9,5},{10,... | collective-permute-start | bytes 786440 | tf_op jit(solution)/shard_map/ppermute | solution.py:275
  86.0 6.4 %collective-permute-start.19 = (bf16[64,2048]{1,0:T(8,128)(2,1)S(1)}, bf16[64,2048]{1,0:T(8,128)(2,1)S(1)}, u32[]{:S(2)}, u32[]{:S(2)}) collective-permute-start(bf16[64,2048]{1,0:T(8,128)(2,1)S(1)} %fusion.3), channel_id=1, source_target_pairs={{0,4},{1,3},{2,0},{3,7},{4,8},{5,1},{6,2},{7,11},{8,12},{9,5},{10,... | collective-permute-start | bytes 786440 | tf_op jit(solution)/shard_map/ppermute | solution.py:275
